TPU v7x, 256 devices: a whole 4x4x8 slice. The times are simulated.
256 devices in a mesh: cls: 8 (over z), col: 32 (over y, x, core).
Axes of the slice: x: 4, y: 4, z: 8, core: 2. Of those that a mesh axis runs over, the one named last changes fastest.
Arguments:
- coeffs_t: float32 [49152, 1024], P(('cls', 'col')), may hold values from -6 to 6
- alpha_table: float32 [64, 4096], replicated, may hold values from -0.1875 to 0.1875
- alpha_blocks: int32 [16, 16], replicated, may hold values from 0 to 15, all different within a row
- alpha_types: int32 [16, 16], replicated, may hold values from 0 to 63
- beta_table: float32 [64, 4096], replicated, may hold values from -0.21875 to 0.21875
- beta_blocks: int32 [768, 12], P('cls'), may hold values from 0 to 191, all different within a row
- beta_types: int32 [768, 12], P('cls'), may hold values from 0 to 63
- row_counts: int32 [32], replicated, may hold values from 1 to 48, 1024 in all
Outputs:
- sigma_slots: float32 [1536, 49152], P('col', 'cls')
Inputs may be any that keep to these rules, and one draw needn't show every extreme that they name: `alpha_blocks`: each row names 16 different alpha blocks. `beta_blocks`: each row names 12 different entries: below 96 a block of the own class, from 96 on a block of the partner class. `row_counts`: the counts sum to 1024 and the largest is exactly 48.
All inputs are finite; a program needn't handle non-finite values.
Results may differ from a plain program's by a relative error of at most 0.0003.
Values sent between devices are 32-bit elements; how exact they have to be, the bound alone decides.
No kernel may reach another device: no remote copies, remote signals or barrier semaphores. Data moves between devices by JAX's collectives and lax.ppermute only.
A program may use at most 64 MiB of HBM per device.

v0:
```python
import jax
import jax.numpy as jnp
from jax import lax
from jax.sharding import PartitionSpec as P

exact_mode = lax.Precision.HIGHEST


def swapped(block, axis, apart):
    count = lax.axis_size(axis)
    route = []
    for low in range(count):
        high = low | 1 << apart
        if high != low and high < count:
            route += [(low, high), (high, low)]
    return lax.ppermute(block, axis, route)


def alpha_local(coeffs_t, alpha_table, alpha_blocks, alpha_types):
    alpha_count = alpha_blocks.shape[0]
    block_size = coeffs_t.shape[1] // alpha_count
    column_count = coeffs_t.shape[0]
    blocked = coeffs_t.reshape(column_count, alpha_count, block_size)

    def alpha_add_term(running, column):
        block_ids, type_ids = column
        source = jnp.take(blocked, block_ids, axis=1)
        matrices = jnp.take(alpha_table, type_ids, axis=0).reshape(
            alpha_count, block_size, block_size
        )
        return (running + jnp.einsum("rib,iab->ria", source, matrices, precision=exact_mode), None)

    running, unused = lax.scan(
        alpha_add_term, jnp.zeros(blocked.shape, jnp.float32), (alpha_blocks.T, alpha_types.T)
    )
    return running.reshape(coeffs_t.shape)


def beta_local(own_rows, partner_rows, beta_table, beta_blocks, beta_types):
    row_total = own_rows.shape[0]
    class_width = own_rows.shape[1]
    block_size = beta_blocks.shape[0] * 0 + int(round(beta_table.shape[1] ** 0.5))
    per_class = class_width // block_size
    stacked = jnp.concatenate([own_rows, partner_rows], 1).reshape(
        row_total, 2 * per_class, block_size
    )

    def beta_add_term(running, column):
        block_ids, type_ids = column
        source = jnp.take(stacked, block_ids, axis=1)
        matrices = jnp.take(beta_table, type_ids, axis=0).reshape(per_class, block_size, block_size)
        return (running + jnp.einsum("rma,mab->rmb", source, matrices, precision=exact_mode), None)

    initial = jnp.zeros((row_total, per_class, block_size), jnp.float32)
    running, unused = lax.scan(beta_add_term, initial, (beta_blocks.T, beta_types.T))
    return running.reshape(row_total, class_width)


def gather_slots(local_t, starts, row_counts, capacity):
    padded = jnp.concatenate([local_t, jnp.zeros((local_t.shape[0], capacity), local_t.dtype)], 1)
    offsets = jnp.arange(capacity, dtype=jnp.int32)
    row_index = starts[:, None] + offsets[None, :]
    in_range = offsets[None, :] < row_counts[:, None]
    picked = jnp.take(padded, row_index, axis=1)
    picked = jnp.where(in_range[None, :, :], picked, jnp.float32(0.0))
    return jnp.transpose(picked, (1, 2, 0))


def on_device(
    coeffs_t,
    alpha_table,
    alpha_blocks,
    alpha_types,
    beta_table,
    beta_blocks,
    beta_types,
    row_counts,
):
    groups = lax.axis_size("col")
    capacity = 3 * coeffs_t.shape[1] // (2 * groups)
    starts = jnp.cumsum(row_counts) - row_counts
    alpha_part = alpha_local(coeffs_t, alpha_table, alpha_blocks, alpha_types)
    coeff_slots = gather_slots(coeffs_t, starts, row_counts, capacity)
    alpha_slots = gather_slots(alpha_part, starts, row_counts, capacity)
    own_rows, alpha_rows = (
        lax.all_to_all(coeff_slots, "col", split_axis=0, concat_axis=2, tiled=True),
        lax.all_to_all(alpha_slots, "col", split_axis=0, concat_axis=2, tiled=True),
    )
    own_rows = own_rows.reshape(capacity, -1)
    partner_rows = swapped(own_rows, "cls", 0)
    alpha_rows = alpha_rows.reshape(capacity, -1)
    return alpha_rows + beta_local(own_rows, partner_rows, beta_table, beta_blocks, beta_types)


def solution(mesh):
    return jax.shard_map(
        on_device,
        mesh=mesh,
        in_specs=(P(("cls", "col"), None), P(), P(), P(), P(), P("cls", None), P("cls", None), P()),
        out_specs=P("col", "cls"),
        check_vma=False,
    )
```

profile of v0, /device:TPU:1, one launch (start us, length us, event | category | flops | bytes accessed | tf_op | source)
XLA Modules:
  0.0 446.5 jit_solution(8192160652040043797)
XLA Ops:
  5.5 99.2 %while.22 = (s32[]{:T(128)}, f32[192,16,64]{0,2,1:T(8,128)}, s32[16,16]{1,0:T(8,128)S(1)}, f32[64,4096]{1,0:T(8,128)}, s32[16,16]{1,0:T(8,128)S(1)}, /*index=5*/f32[192,16,64]{0,2,1:T(8,128)S(1)}, s32[]{:T(128)}, s32[]{:T(128)}) while((s32[]{:T(128)}, f32[192,16,64]{0,2,1:T(8,128)}, s32[16,16]{1,0:T(8,128)S(1)}, ...), condition=%wide.region_1.2_spmd.clone, body=%wide.region_0.0_spmd.clone.sunk | while | flops 151652640 | bytes 5251887 | solution.py:33
  13.5 3.4 fusion.34
  19.7 3.4 fusion.34
  26.0 3.4 fusion.34
  32.3 3.4 fusion.34
  38.5 3.4 fusion.34
  44.8 3.4 fusion.34
  51.1 3.4 fusion.34
  57.4 3.4 fusion.34
  63.6 3.4 fusion.34
  69.9 3.4 fusion.34
  76.2 3.4 fusion.34
  82.5 3.4 fusion.34
  88.7 3.4 fusion.34
  95.0 3.4 fusion.34
  101.3 3.4 fusion.34
  106.0 4.6 %gather_fusion.5 = f32[1536,192]{1,0:T(8,128)} fusion(f32[192,1072]{0,1:T(8,128)S(1)} %concatenate.15, s32[2048]{0:T(1024)S(1)} %pad_clamp_fusion.4), kind=kCustom, calls=%fused_computation.5.clone | custom fusion | bytes 2365440 | tf_op jit(solution)/shard_map/jit(_take)/gather | solution.py:64
  110.6 4.6 %gather_fusion.4 = f32[1536,192]{1,0:T(8,128)} fusion(f32[192,1072]{0,1:T(8,128)S(1)} %concatenate.14, s32[2048]{0:T(1024)S(1)} %pad_clamp_fusion.4), kind=kCustom, calls=%fused_computation.2.clone | custom fusion | bytes 2365440 | tf_op jit(solution)/shard_map/jit(_take)/gather | solution.py:64
  117.8 31.0 %all_to_all.30 = f32[32,48,192]{2,1,0:T(8,128)S(1)} all-to-all(f32[32,48,192]{2,1,0:T(8,128)S(1)} %get-tuple-element.164), channel_id=1, replica_groups=mesh['cls'=8,'col'=32] {'col'}, dimensions={0} | all-to-all | bytes 2359296 | tf_op jit(solution)/shard_map/all_to_all | solution.py:86
  153.0 4.3 all-to-all-start
  159.3 20.4 %all-to-all-done = f32[32,48,192]{2,1,0:T(8,128)S(1)} async-done(((f32[32,48,192]{2,1,0:T(8,128)}), f32[32,48,192]{2,1,0:T(8,128)S(1)}, u32[]{:S(2)}, u32[]{:S(2)}) %all-to-all-start) | async-done | bytes 1179680 | tf_op jit(solution)/shard_map/all_to_all | solution.py:87
  186.4 4.9 %copy.52 = f32[48,192,64]{2,0,1:T(8,128)} copy(f32[48,192,64]{2,1,0:T(8,128)S(1)} %pad_maximum_fusion) | data formatting | bytes 4718592
  191.2 249.7 %while.23 = (s32[]{:T(128)}, f32[48,96,64]{2,0,1:T(8,128)}, s32[12,96]{1,0:T(8,128)}, f32[64,4096]{1,0:T(8,128)S(1)}, s32[12,96]{1,0:T(8,128)}, /*index=5*/f32[48,192,64]{2,0,1:T(8,128)}, s32[]{:T(128)}, s32[]{:T(128)}) while((s32[]{:T(128)}, f32[48,96,64]{2,0,1:T(8,128)}, s32[12,96]{1,0:T(8,128)}, f32[64,4096]{1,0:T(8,128)S(1)}, ...), condition=%wide.region_4.6_spmd.clone, body=%wide.region_3.5_spmd.clone.sunk | while | flops 227774144 | bytes 20066544 | solution.py:55
  198.2 4.7 %copy.57 = f32[96,64,64]{2,1,0:T(8,128)} copy(f32[96,64,64]{0,2,1:T(8,128)} %broadcast_select_fusion.2) | data formatting | bytes 3145728 | tf_op jit(solution)/shard_map/while/body/eval_jaxpr/jit(_take)/select_n | solution.py:51
  202.9 3.0 gather_fusion.3
  205.9 5.8 %bitcast_add_fusion.2 = f32[48,96,64]{2,0,1:T(8,128)} fusion(f32[48,96,64]{2,0,1:T(8,128)} %get-tuple-element.291, f32[96,64,64]{2,1,0:T(8,128)} %copy.57, f32[96,48,64]{2,1,0:T(8,128)S(1)} %gather_fusion.3, pred[96]{0:T(512)(128)(4,1)S(1)} %get-tuple-element.257, pred[]{:T(512)S(6)} %compare.9), kind=kOutput, calls=%fused_computation.28.clone.1 | convolution fusion | flops 227377152 | bytes 5111905 | tf_op jit(solution)/shard_map/while/body/eval_jaxpr/rma,mab->rmb/dot_general | solution.py:52
  218.7 4.7 %copy.57 = f32[96,64,64]{2,1,0:T(8,128)} copy(f32[96,64,64]{0,2,1:T(8,128)} %broadcast_select_fusion.2) | data formatting | bytes 3145728 | tf_op jit(solution)/shard_map/while/body/eval_jaxpr/jit(_take)/select_n | solution.py:51
  226.4 6.1 %bitcast_add_fusion.2 = f32[48,96,64]{2,0,1:T(8,128)} fusion(f32[48,96,64]{2,0,1:T(8,128)} %get-tuple-element.291, f32[96,64,64]{2,1,0:T(8,128)} %copy.57, f32[96,48,64]{2,1,0:T(8,128)S(1)} %gather_fusion.3, pred[96]{0:T(512)(128)(4,1)S(1)} %get-tuple-element.257, pred[]{:T(512)S(6)} %compare.9), kind=kOutput, calls=%fused_computation.28.clone.1 | convolution fusion | flops 227377152 | bytes 5111905 | tf_op jit(solution)/shard_map/while/body/eval_jaxpr/rma,mab->rmb/dot_general | solution.py:52
  239.5 4.7 %copy.57 = f32[96,64,64]{2,1,0:T(8,128)} copy(f32[96,64,64]{0,2,1:T(8,128)} %broadcast_select_fusion.2) | data formatting | bytes 3145728 | tf_op jit(solution)/shard_map/while/body/eval_jaxpr/jit(_take)/select_n | solution.py:51
  247.3 6.1 %bitcast_add_fusion.2 = f32[48,96,64]{2,0,1:T(8,128)} fusion(f32[48,96,64]{2,0,1:T(8,128)} %get-tuple-element.291, f32[96,64,64]{2,1,0:T(8,128)} %copy.57, f32[96,48,64]{2,1,0:T(8,128)S(1)} %gather_fusion.3, pred[96]{0:T(512)(128)(4,1)S(1)} %get-tuple-element.257, pred[]{:T(512)S(6)} %compare.9), kind=kOutput, calls=%fused_computation.28.clone.1 | convolution fusion | flops 227377152 | bytes 5111905 | tf_op jit(solution)/shard_map/while/body/eval_jaxpr/rma,mab->rmb/dot_general | solution.py:52
  260.3 4.7 %copy.57 = f32[96,64,64]{2,1,0:T(8,128)} copy(f32[96,64,64]{0,2,1:T(8,128)} %broadcast_select_fusion.2) | data formatting | bytes 3145728 | tf_op jit(solution)/shard_map/while/body/eval_jaxpr/jit(_take)/select_n | solution.py:51
  268.1 6.1 %bitcast_add_fusion.2 = f32[48,96,64]{2,0,1:T(8,128)} fusion(f32[48,96,64]{2,0,1:T(8,128)} %get-tuple-element.291, f32[96,64,64]{2,1,0:T(8,128)} %copy.57, f32[96,48,64]{2,1,0:T(8,128)S(1)} %gather_fusion.3, pred[96]{0:T(512)(128)(4,1)S(1)} %get-tuple-element.257, pred[]{:T(512)S(6)} %compare.9), kind=kOutput, calls=%fused_computation.28.clone.1 | convolution fusion | flops 227377152 | bytes 5111905 | tf_op jit(solution)/shard_map/while/body/eval_jaxpr/rma,mab->rmb/dot_general | solution.py:52
  281.2 4.7 %copy.57 = f32[96,64,64]{2,1,0:T(8,128)} copy(f32[96,64,64]{0,2,1:T(8,128)} %broadcast_select_fusion.2) | data formatting | bytes 3145728 | tf_op jit(solution)/shard_map/while/body/eval_jaxpr/jit(_take)/select_n | solution.py:51
  288.9 6.1 %bitcast_add_fusion.2 = f32[48,96,64]{2,0,1:T(8,128)} fusion(f32[48,96,64]{2,0,1:T(8,128)} %get-tuple-element.291, f32[96,64,64]{2,1,0:T(8,128)} %copy.57, f32[96,48,64]{2,1,0:T(8,128)S(1)} %gather_fusion.3, pred[96]{0:T(512)(128)(4,1)S(1)} %get-tuple-element.257, pred[]{:T(512)S(6)} %compare.9), kind=kOutput, calls=%fused_computation.28.clone.1 | convolution fusion | flops 227377152 | bytes 5111905 | tf_op jit(solution)/shard_map/while/body/eval_jaxpr/rma,mab->rmb/dot_general | solution.py:52
  302.0 4.7 %copy.57 = f32[96,64,64]{2,1,0:T(8,128)} copy(f32[96,64,64]{0,2,1:T(8,128)} %broadcast_select_fusion.2) | data formatting | bytes 3145728 | tf_op jit(solution)/shard_map/while/body/eval_jaxpr/jit(_take)/select_n | solution.py:51
  309.8 6.1 %bitcast_add_fusion.2 = f32[48,96,64]{2,0,1:T(8,128)} fusion(f32[48,96,64]{2,0,1:T(8,128)} %get-tuple-element.291, f32[96,64,64]{2,1,0:T(8,128)} %copy.57, f32[96,48,64]{2,1,0:T(8,128)S(1)} %gather_fusion.3, pred[96]{0:T(512)(128)(4,1)S(1)} %get-tuple-element.257, pred[]{:T(512)S(6)} %compare.9), kind=kOutput, calls=%fused_computation.28.clone.1 | convolution fusion | flops 227377152 | bytes 5111905 | tf_op jit(solution)/shard_map/while/body/eval_jaxpr/rma,mab->rmb/dot_general | solution.py:52
  322.8 4.7 %copy.57 = f32[96,64,64]{2,1,0:T(8,128)} copy(f32[96,64,64]{0,2,1:T(8,128)} %broadcast_select_fusion.2) | data formatting | bytes 3145728 | tf_op jit(solution)/shard_map/while/body/eval_jaxpr/jit(_take)/select_n | solution.py:51
  330.6 6.1 %bitcast_add_fusion.2 = f32[48,96,64]{2,0,1:T(8,128)} fusion(f32[48,96,64]{2,0,1:T(8,128)} %get-tuple-element.291, f32[96,64,64]{2,1,0:T(8,128)} %copy.57, f32[96,48,64]{2,1,0:T(8,128)S(1)} %gather_fusion.3, pred[96]{0:T(512)(128)(4,1)S(1)} %get-tuple-element.257, pred[]{:T(512)S(6)} %compare.9), kind=kOutput, calls=%fused_computation.28.clone.1 | convolution fusion | flops 227377152 | bytes 5111905 | tf_op jit(solution)/shard_map/while/body/eval_jaxpr/rma,mab->rmb/dot_general | solution.py:52
  343.7 4.7 %copy.57 = f32[96,64,64]{2,1,0:T(8,128)} copy(f32[96,64,64]{0,2,1:T(8,128)} %broadcast_select_fusion.2) | data formatting | bytes 3145728 | tf_op jit(solution)/shard_map/while/body/eval_jaxpr/jit(_take)/select_n | solution.py:51
  351.4 6.1 %bitcast_add_fusion.2 = f32[48,96,64]{2,0,1:T(8,128)} fusion(f32[48,96,64]{2,0,1:T(8,128)} %get-tuple-element.291, f32[96,64,64]{2,1,0:T(8,128)} %copy.57, f32[96,48,64]{2,1,0:T(8,128)S(1)} %gather_fusion.3, pred[96]{0:T(512)(128)(4,1)S(1)} %get-tuple-element.257, pred[]{:T(512)S(6)} %compare.9), kind=kOutput, calls=%fused_computation.28.clone.1 | convolution fusion | flops 227377152 | bytes 5111905 | tf_op jit(solution)/shard_map/while/body/eval_jaxpr/rma,mab->rmb/dot_general | solution.py:52
  364.5 4.7 %copy.57 = f32[96,64,64]{2,1,0:T(8,128)} copy(f32[96,64,64]{0,2,1:T(8,128)} %broadcast_select_fusion.2) | data formatting | bytes 3145728 | tf_op jit(solution)/shard_map/while/body/eval_jaxpr/jit(_take)/select_n | solution.py:51
  372.3 6.1 %bitcast_add_fusion.2 = f32[48,96,64]{2,0,1:T(8,128)} fusion(f32[48,96,64]{2,0,1:T(8,128)} %get-tuple-element.291, f32[96,64,64]{2,1,0:T(8,128)} %copy.57, f32[96,48,64]{2,1,0:T(8,128)S(1)} %gather_fusion.3, pred[96]{0:T(512)(128)(4,1)S(1)} %get-tuple-element.257, pred[]{:T(512)S(6)} %compare.9), kind=kOutput, calls=%fused_computation.28.clone.1 | convolution fusion | flops 227377152 | bytes 5111905 | tf_op jit(solution)/shard_map/while/body/eval_jaxpr/rma,mab->rmb/dot_general | solution.py:52
  385.4 4.7 %copy.57 = f32[96,64,64]{2,1,0:T(8,128)} copy(f32[96,64,64]{0,2,1:T(8,128)} %broadcast_select_fusion.2) | data formatting | bytes 3145728 | tf_op jit(solution)/shard_map/while/body/eval_jaxpr/jit(_take)/select_n | solution.py:51
  393.1 6.1 %bitcast_add_fusion.2 = f32[48,96,64]{2,0,1:T(8,128)} fusion(f32[48,96,64]{2,0,1:T(8,128)} %get-tuple-element.291, f32[96,64,64]{2,1,0:T(8,128)} %copy.57, f32[96,48,64]{2,1,0:T(8,128)S(1)} %gather_fusion.3, pred[96]{0:T(512)(128)(4,1)S(1)} %get-tuple-element.257, pred[]{:T(512)S(6)} %compare.9), kind=kOutput, calls=%fused_computation.28.clone.1 | convolution fusion | flops 227377152 | bytes 5111905 | tf_op jit(solution)/shard_map/while/body/eval_jaxpr/rma,mab->rmb/dot_general | solution.py:52
  406.2 4.7 %copy.57 = f32[96,64,64]{2,1,0:T(8,128)} copy(f32[96,64,64]{0,2,1:T(8,128)} %broadcast_select_fusion.2) | data formatting | bytes 3145728 | tf_op jit(solution)/shard_map/while/body/eval_jaxpr/jit(_take)/select_n | solution.py:51
  414.0 6.1 %bitcast_add_fusion.2 = f32[48,96,64]{2,0,1:T(8,128)} fusion(f32[48,96,64]{2,0,1:T(8,128)} %get-tuple-element.291, f32[96,64,64]{2,1,0:T(8,128)} %copy.57, f32[96,48,64]{2,1,0:T(8,128)S(1)} %gather_fusion.3, pred[96]{0:T(512)(128)(4,1)S(1)} %get-tuple-element.257, pred[]{:T(512)S(6)} %compare.9), kind=kOutput, calls=%fused_computation.28.clone.1 | convolution fusion | flops 227377152 | bytes 5111905 | tf_op jit(solution)/shard_map/while/body/eval_jaxpr/rma,mab->rmb/dot_general | solution.py:52
  427.1 4.7 %copy.57 = f32[96,64,64]{2,1,0:T(8,128)} copy(f32[96,64,64]{0,2,1:T(8,128)} %broadcast_select_fusion.2) | data formatting | bytes 3145728 | tf_op jit(solution)/shard_map/while/body/eval_jaxpr/jit(_take)/select_n | solution.py:51
  434.8 6.1 %bitcast_add_fusion.2 = f32[48,96,64]{2,0,1:T(8,128)} fusion(f32[48,96,64]{2,0,1:T(8,128)} %get-tuple-element.291, f32[96,64,64]{2,1,0:T(8,128)} %copy.57, f32[96,48,64]{2,1,0:T(8,128)S(1)} %gather_fusion.3, pred[96]{0:T(512)(128)(4,1)S(1)} %get-tuple-element.257, pred[]{:T(512)S(6)} %compare.9), kind=kOutput, calls=%fused_computation.28.clone.1 | convolution fusion | flops 227377152 | bytes 5111905 | tf_op jit(solution)/shard_map/while/body/eval_jaxpr/rma,mab->rmb/dot_general | solution.py:52
  (242 shorter events, 192.0 us)
Async XLA Ops:
  104.7 1.2 copy-start.1
  110.6 4.6 %copy-start.2 = (f32[1536,192]{1,0:T(8,128)S(1)}, f32[1536,192]{1,0:T(8,128)}, u32[]{:S(2)}) copy-start(f32[1536,192]{1,0:T(8,128)} %gather_fusion.5) | copy-start | bytes 3538948
  151.4 30.8 %collective-permute-start = (f32[48,6144]{1,0:T(8,128)}, f32[48,6144]{1,0:T(8,128)}, u32[]{:S(2)}, u32[]{:S(2)}) collective-permute-start(f32[48,6144]{1,0:T(8,128)} %reshape.224), channel_id=1, source_target_pairs={{0,32},{32,0},{64,96},{96,64},{128,160},{160,128},{192,224},{224,1... | collective-permute-start | bytes 3538952 | tf_op jit(solution)/shard_map/ppermute | solution.py:16
  153.0 26.6 %all-to-all-start = ((f32[32,48,192]{2,1,0:T(8,128)}), f32[32,48,192]{2,1,0:T(8,128)S(1)}, u32[]{:S(2)}, u32[]{:S(2)}) async-start(f32[32,48,192]{2,1,0:T(8,128)} %get-tuple-element.165), calls=%async_computation | async-start | bytes 3145728 | tf_op jit(solution)/shard_map/all_to_all | solution.py:87
  186.4 4.9 %copy-start = (f32[64,4096]{1,0:T(8,128)S(1)}, f32[64,4096]{1,0:T(8,128)}, u32[]{:S(2)}) copy-start(f32[64,4096]{1,0:T(8,128)} %param.18) | copy-start | bytes 3145732
where the time goes:
time: 450 us; the launch traced here: 447 us
  local copies, waits for them, and re-layouts  218 us (48%)
  matrix products  126 us (28%)
  other arithmetic  44 us (10%)
  blocking collectives  31 us (7%)
  waiting for transfers between devices  20.4 us (5%)
  starting transfers between devices  5.95 us (1%)
    dot_general x12, matrix products, beta_add_term(): jnp.einsum('rma,mab->rmb', source, matrices, precision=exact_mode)  73.1 us
    select_n x12, local copies, waits for them, and re-layouts, beta_add_term(): jnp.take(beta_table, type_ids, axis=0)  56.7 us
    dot_general x16, matrix products, alpha_add_term(): jnp.einsum('rib,iab->ria', source, matrices, precision=exact_mode)  52.8 us
    gather x24, local copies, waits for them, and re-layouts, beta_add_term(): jnp.take(beta_table, type_ids, axis=0)  48.5 us
    gather x12, local copies, waits for them, and re-layouts, beta_add_term(): source = jnp.take(stacked, block_ids, axis=1)  36.4 us
    gather x32, local copies, waits for them, and re-layouts, alpha_add_term(): jnp.take(alpha_table, type_ids, axis=0)  35 us
    all_to_all x1, blocking collectives, on_device(): lax.all_to_all(coeff_slots, 'col', split_axis=0, concat_axis=2, tiled=True)  31 us
    select_n x24, other arithmetic, beta_add_term(): jnp.take(beta_table, type_ids, axis=0)  26.1 us
  transfers between devices with their start and end apart: 2, of which 1 were waited for; matrix products, arithmetic and copies ran while one was open for 1% of the time, Pallas kernels for 0%

commit v1 on v0

v1 whole, which is shorter than its diff:
```python
import jax
import jax.numpy as jnp
from jax import lax
from jax.experimental import pallas as pl
from jax.experimental.pallas import tpu as pltpu
from jax.sharding import PartitionSpec as P

f32 = jnp.float32
bf16 = jnp.bfloat16

NA = 1024
BLK = 64
COLS = 32
CAP = 48
LOCAL = 192
HALF = CAP // 2
PACK = CAP + HALF
ROWS = NA + CAP + 8


def split(x):
    hi = x.astype(bf16)
    return hi, (x - hi.astype(f32)).astype(bf16)


def left_half(shape):
    return lax.broadcasted_iota(jnp.int32, shape, len(shape) - 1) < BLK


def load_transposed(x_ref, buf_ref):
    for c in range(NA // 128):
        cols = slice(128 * c, 128 * c + 128)
        last = x_ref[128:192, cols]
        buf_ref[cols, 0:128] = x_ref[0:128, cols].T
        buf_ref[cols, 128:256] = jnp.concatenate([last, last], 0).T


def write_slots(counts_ref, buf_ref, out_ref):
    buf_ref[NA:ROWS, :] = jnp.zeros((ROWS - NA, 256), f32)
    row = lax.broadcasted_iota(jnp.int32, (CAP, 128), 0)
    row_low = lax.broadcasted_iota(jnp.int32, (HALF, 128), 0)
    row_low = jnp.where(left_half((HALF, 128)), row_low, row_low + HALF)
    left = left_half((8, 128))
    sub = lax.broadcasted_iota(jnp.int32, (8, 256), 0)

    def one(j, start):
        count = counts_ref[j]
        base = pl.multiple_of((start // 8) * 8, 8)
        shift = 8 - (start - base)
        turned = [pltpu.roll(buf_ref[pl.ds(base + 8 * n, 8), :], shift & 7, 0) for n in range(CAP // 8 + 1)]
        rows = [jnp.where(sub < shift, turned[n], turned[n + 1]) for n in range(CAP // 8)]
        main = jnp.concatenate([r[:, 0:128] for r in rows], 0)
        out_ref[j, 0:CAP, :] = jnp.where(row < count, main, 0.0)
        third = [r[:, 128:256] for r in rows]
        folded = jnp.concatenate(
            [jnp.where(left, third[n], third[n + HALF // 8]) for n in range(HALF // 8)], 0
        )
        out_ref[j, CAP:PACK, :] = jnp.where(row_low < count, folded, 0.0)
        return start + count

    lax.fori_loop(0, COLS, one, jnp.int32(0))


def coeff_kernel(counts_ref, x_ref, out_ref, buf_ref):
    load_transposed(x_ref, buf_ref)
    write_slots(counts_ref, buf_ref, out_ref)


def alpha_kernel(counts_ref, blocks_ref, types_ref, x_ref, table_ref, out_ref, buf_ref, a_ref, hi_ref, lo_ref):
    load_transposed(x_ref, buf_ref)
    blocks = NA // BLK
    for b in range(blocks):
        hi, lo = split(buf_ref[BLK * b:BLK * b + BLK, :])
        for half in range(2):
            at = slice(128 * b + BLK * half, 128 * b + BLK * half + BLK)
            hi_ref[at, :] = hi
            lo_ref[at, :] = lo

    def place(i, carry):
        for k in range(blocks):
            col = pl.multiple_of(blocks_ref[i, k] * 128, 128)
            row = pl.multiple_of(i * BLK, BLK)
            a_ref[pl.ds(row, BLK), pl.ds(col, 128)] = table_ref[types_ref[i, k]]
        return carry

    lax.fori_loop(0, blocks, place, 0)
    for r in range(4):
        rows = slice(256 * r, 256 * r + 256)
        a = a_ref[rows, :]
        buf_ref[rows, :] = jnp.dot(a, hi_ref[...], preferred_element_type=f32) + jnp.dot(
            a, lo_ref[...], preferred_element_type=f32
        )
    write_slots(counts_ref, buf_ref, out_ref)


def beta_kernel(blocks_ref, types_ref, own_ref, partner_ref, alpha_ref, table_ref, out_ref, hi_ref, lo_ref):
    left = left_half((CAP, 128))
    left_low = left_half((HALF, 128))

    def swap(x):
        return pltpu.roll(x, BLK, 1)

    def unpack(ref, base):
        def one(j, carry):
            main = ref[j, 0:CAP, :]
            low = ref[j, CAP:PACK, :]
            main_r = swap(main)
            low_r = swap(low)
            parts = (
                jnp.where(left, main, main_r),
                jnp.where(left, main_r, main),
                jnp.concatenate([jnp.where(left_low, low, low_r), jnp.where(left_low, low_r, low)], 0),
            )
            for n in range(3):
                hi, lo = split(parts[n])
                hi_ref[base + 3 * j + n] = hi
                lo_ref[base + 3 * j + n] = lo
            return carry

        lax.fori_loop(0, COLS, one, 0)

    unpack(own_ref, 0)
    unpack(partner_ref, 96)

    def block(m):
        total = jnp.zeros((2 * CAP, 128), f32)
        for g in range(3):
            hi_parts, lo_parts, w_parts = [], [], []
            for q in range(2):
                s0 = blocks_ref[4 * g + 2 * q, m]
                s1 = blocks_ref[4 * g + 2 * q + 1, m]
                hi_parts.append(jnp.where(left, hi_ref[s0], hi_ref[s1]))
                lo_parts.append(jnp.where(left, lo_ref[s0], lo_ref[s1]))
                w_parts.append(table_ref[types_ref[4 * g + 2 * q, m]])
                w_parts.append(table_ref[types_ref[4 * g + 2 * q + 1, m]])
            lhs = jnp.concatenate([jnp.concatenate(hi_parts, 1), jnp.concatenate(lo_parts, 1)], 0)
            total = total + jnp.dot(lhs, jnp.concatenate(w_parts, 0), preferred_element_type=f32)
        both = total[0:CAP] + total[CAP:]
        return both + swap(both)

    def triple(u, carry):
        a_main, a_low = alpha_ref[2 * u, 0:CAP, :], alpha_ref[2 * u, CAP:PACK, :]
        b_main, b_low = alpha_ref[2 * u + 1, 0:CAP, :], alpha_ref[2 * u + 1, CAP:PACK, :]
        b_main_r = swap(b_main)
        alphas = (
            a_main,
            jnp.where(left, jnp.concatenate([a_low, swap(a_low)], 0), b_main_r),
            jnp.where(left, b_main_r, jnp.concatenate([swap(b_low), b_low], 0)),
        )
        for q in range(3):
            pair = jnp.where(left, block(6 * u + 2 * q), block(6 * u + 2 * q + 1))
            col = pl.multiple_of(u * 384 + 128 * q, 128)
            out_ref[:, pl.ds(col, 128)] = alphas[q] + pair
        return carry

    lax.fori_loop(0, COLS // 2, triple, 0)


def smem():
    return pl.BlockSpec(memory_space=pltpu.SMEM)


def vmem():
    return pl.BlockSpec(memory_space=pltpu.VMEM)


def split_table(table):
    tiles = table.reshape(table.shape[0], BLK, BLK)
    hi = lax.reduce_precision(tiles, 8, 7)
    return jnp.concatenate([hi, tiles - hi], 2).astype(bf16)


def on_device(coeffs_t, alpha_table, alpha_blocks, alpha_types, beta_table, beta_blocks, beta_types, row_counts):
    slots = jax.ShapeDtypeStruct((COLS, PACK, 128), f32)
    coeff_slots = pl.pallas_call(
        coeff_kernel,
        in_specs=[smem(), vmem()],
        out_specs=vmem(),
        out_shape=slots,
        scratch_shapes=[pltpu.VMEM((ROWS, 256), f32)],
        name="coeff_slots",
    )(row_counts, coeffs_t)
    alpha_slots = pl.pallas_call(
        alpha_kernel,
        in_specs=[smem(), smem(), smem(), vmem(), vmem()],
        out_specs=vmem(),
        out_shape=slots,
        scratch_shapes=[
            pltpu.VMEM((ROWS, 256), f32),
            pltpu.VMEM((NA, 2 * NA), bf16),
            pltpu.VMEM((2 * NA, 256), bf16),
            pltpu.VMEM((2 * NA, 256), bf16),
        ],
        name="alpha_slots",
    )(row_counts, alpha_blocks, alpha_types, coeffs_t, split_table(alpha_table))
    own = lax.all_to_all(coeff_slots, "col", split_axis=0, concat_axis=0, tiled=True)
    partner = lax.ppermute(own, "cls", [(i, i ^ 1) for i in range(8)])
    alpha = lax.all_to_all(alpha_slots, "col", split_axis=0, concat_axis=0, tiled=True)
    return pl.pallas_call(
        beta_kernel,
        in_specs=[smem(), smem(), vmem(), vmem(), vmem(), vmem()],
        out_specs=vmem(),
        out_shape=jax.ShapeDtypeStruct((CAP, 96 * BLK), f32),
        scratch_shapes=[pltpu.VMEM((192, CAP, 128), bf16), pltpu.VMEM((192, CAP, 128), bf16)],
        name="beta_sum",
    )(beta_blocks.T, beta_types.T, own, partner, alpha, split_table(beta_table))


def solution(mesh):
    return jax.shard_map(
        on_device,
        mesh=mesh,
        in_specs=(P(("cls", "col"), None), P(), P(), P(), P(), P("cls", None), P("cls", None), P()),
        out_specs=P("col", "cls"),
        check_vma=False,
    )
```

time: 450 us -> 83.2 us (0.18)
  local copies, waits for them, and re-layouts: 218 us -> 4.01 us
  matrix products: 126 us -> 0 us
  other arithmetic: 44 us -> 7.12 us
  blocking collectives: 31 us -> 0 us
  Pallas kernels: 0 us -> 27.3 us
  starting transfers between devices: 5.95 us -> 15.1 us
  waiting for transfers between devices: 20.4 us -> 29.2 us
    gather x86 -> x0, local copies, waits for them, and re-layouts: 139 us -> none  [the longest x24 48.5 us: beta_add_term(): jnp.take(beta_table, type_ids, axis=0)]
    dot_general x28 -> x0, matrix products: 126 us -> none  [the longest x12 73.1 us: beta_add_term(): jnp.einsum('rma,mab->rmb', source, matrices, precision=exact_mode)]
    select_n x12 -> x0, local copies, waits for them, and re-layouts: 56.7 us -> none  [beta_add_term(): jnp.take(beta_table, type_ids, axis=0)]
    all_to_all x1 -> x0, blocking collectives: 31 us -> none  [on_device(): lax.all_to_all(coeff_slots, 'col', split_axis=0, concat_axis=2, tiled=True)]
    pallas_call x0 -> x3, Pallas kernels: none -> 27.3 us  [the longest x1 17.1 us: on_device(): pl.pallas_call(beta_kernel, in_specs=[smem(), smem(), vmem(), vmem(), vme...]
    select_n x41 -> x0, other arithmetic: 26.3 us -> none  [the longest x24 26.1 us: beta_add_term(): jnp.take(beta_table, type_ids, axis=0)]
    all_to_all x1 -> x2, starting transfers between devices: 4.31 us -> 13.5 us  [the longest x1 8.58 us: on_device(): lax.all_to_all(coeff_slots, 'col', split_axis=0, concat_axis=0, tiled=True)]
    unnamed x10 -> x2, local copies, waits for them, and re-layouts: 9.03 us -> 0.01 us
  transfers between devices with their start and end apart: 2 -> 3, of which waited for: 1 -> 2; matrix products, arithmetic and copies ran while one was open for 1% -> 13% of each run, Pallas kernels for 0% -> 9%
where the time goes in v1:
time: 83.2 us; the launch traced here: 82.8 us
  waiting for transfers between devices  29.2 us (35%)
  Pallas kernels  27.3 us (33%)
  starting transfers between devices  15.1 us (18%)
  other arithmetic  7.12 us (9%)
  local copies, waits for them, and re-layouts  4.01 us (5%)
    pallas_call x1, Pallas kernels, on_device(): pl.pallas_call(beta_kernel, in_specs=[smem(), smem(), vmem(), vmem(), vme...  17.1 us
    all_to_all x1, waiting for transfers between devices, on_device(): lax.all_to_all(coeff_slots, 'col', split_axis=0, concat_axis=0, tiled=True)  14.6 us
    all_to_all x1, waiting for transfers between devices, on_device(): lax.all_to_all(alpha_slots, 'col', split_axis=0, concat_axis=0, tiled=True)  14.5 us
    all_to_all x1, starting transfers between devices, on_device(): lax.all_to_all(coeff_slots, 'col', split_axis=0, concat_axis=0, tiled=True)  8.58 us
    pallas_call x1, Pallas kernels, on_device(): pl.pallas_call(alpha_kernel, in_specs=[smem(), smem(), smem(), vmem(), vm...  7.12 us
    all_to_all x1, starting transfers between devices, on_device(): lax.all_to_all(alpha_slots, 'col', split_axis=0, concat_axis=0, tiled=True)  4.91 us
    concatenate x2, other arithmetic, split_table(): return jnp.concatenate([hi, tiles - hi], 2).astype(bf16)  4.66 us
    reshape x2, local copies, waits for them, and re-layouts, split_table(): tiles = table.reshape(table.shape[0], BLK, BLK)  4.01 us
  transfers between devices with their start and end apart: 3, of which 2 were waited for; matrix products, arithmetic and copies ran while one was open for 13% of the time, Pallas kernels for 9%

profile of v1, /device:TPU:1, one launch (start us, length us, event | category | flops | bytes accessed | tf_op | source)
XLA Modules:
  0.0 82.8 jit_solution(9864145626945726741)
XLA Ops:
  0.0 3.1 %coeff_slots.1 = f32[32,72,128]{2,1,0:T(8,128)} custom-call(s32[32]{0:T(128)} %counts_ref.3, f32[192,1024]{1,0:T(8,128)} %x_ref.3), custom_call_target="tpu_custom_call" | custom-call | tf_op jit(solution)/shard_map/coeff_slots/pallas_call | solution.py:175
  3.1 8.6 %all-to-all-start = ((f32[32,72,128]{2,1,0:T(8,128)}), f32[32,72,128]{2,1,0:T(8,128)S(1)}, u32[]{:S(2)}, u32[]{:S(2)}) async-start(f32[32,72,128]{2,1,0:T(8,128)} %coeff_slots.1), calls=%async_computation | async-start | bytes 2359296 | tf_op jit(solution)/shard_map/all_to_all | solution.py:196
  11.7 2.0 %reshape.6 = f32[64,64,64]{2,1,0:T(8,128)S(1)} reshape(f32[64,4096]{1,0:T(8,128)} %param.9) | data formatting | bytes 2097152 | tf_op jit(solution)/shard_map/reshape | solution.py:168
  13.7 1.9 %reduce-precision_convert_fusion.1 = (bf16[64,64,64]{2,1,0:T(8,128)(2,1)}, bf16[64,64,64]{2,1,0:T(8,128)(2,1)}) fusion(f32[64,64,64]{2,1,0:T(8,128)S(1)} %reshape.6), kind=kLoop, calls=%fused_computation.3 | loop fusion | flops 1048576 | bytes 2097152 | tf_op jit(solution)/shard_map/convert.2
  15.6 14.6 %all-to-all-done.own_ref = f32[32,72,128]{2,1,0:T(8,128)S(1)} async-done(((f32[32,72,128]{2,1,0:T(8,128)}), f32[32,72,128]{2,1,0:T(8,128)S(1)}, u32[]{:S(2)}, u32[]{:S(2)}) %all-to-all-start) | async-done | bytes 1179680 | tf_op jit(solution)/shard_map/all_to_all | solution.py:196
  30.2 0.0 copy-start
  30.2 1.6 %collective-permute-start = (f32[32,72,128]{2,1,0:T(8,128)S(1)}, f32[32,72,128]{2,1,0:T(8,128)}, u32[]{:S(2)}, u32[]{:S(2)}) collective-permute-start(f32[32,72,128]{2,1,0:T(8,128)S(1)} %all-to-all-done.own_ref), channel_id=1, source_target_pairs={{0,32},{32,0},{64,96},{96,64},{128,160},{160,128},{192,224},{224,1... | collective-permute-start | bytes 3538952 | tf_op jit(solution)/shard_map/ppermute | solution.py:197
  31.8 3.1 %pad_maximum_fusion.table_ref = bf16[64,64,128]{2,1,0:T(8,128)(2,1)} fusion(bf16[64,64,64]{2,1,0:T(8,128)(2,1)} %get-tuple-element.8, bf16[64,64,64]{2,1,0:T(8,128)(2,1)} %get-tuple-element.7), kind=kLoop, calls=%fused_computation.6 | loop fusion | flops 2097152 | bytes 2097152 | tf_op jit(solution)/shard_map/concatenate | solution.py:170
  35.0 7.1 %alpha_slots.1 = f32[32,72,128]{2,1,0:T(8,128)} custom-call(s32[32]{0:T(128)} %counts_ref.3, s32[16,16]{1,0:T(8,128)} %blocks_ref.1, s32[16,16]{1,0:T(8,128)} %types_ref.1, f32[192,1024]{1,0:T(8,128)} %x_ref.3, bf16[64,64,128]{2,1,0:T(8,128)(2,1)} %pad_maximum_fusion.table_ref), custom_call_target="tpu_custom_call" | custom-call | tf_op jit(solution)/shard_map/alpha_slots/pallas_call | solution.py:183
  42.1 0.0 copy-done
  42.1 4.9 %all-to-all-start.1 = ((f32[32,72,128]{2,1,0:T(8,128)}), f32[32,72,128]{2,1,0:T(8,128)}, u32[]{:S(2)}, u32[]{:S(2)}) async-start(f32[32,72,128]{2,1,0:T(8,128)} %alpha_slots.1), calls=%async_computation.1 | async-start | bytes 2359296 | tf_op jit(solution)/shard_map/all_to_all | solution.py:198
  47.0 2.0 %reshape.7 = f32[64,64,64]{2,1,0:T(8,128)S(1)} reshape(f32[64,4096]{1,0:T(8,128)} %param.12) | data formatting | bytes 2097152 | tf_op jit(solution)/shard_map/reshape | solution.py:168
  49.0 0.6 reduce-precision_convert_fusion
  49.6 1.6 %pad_maximum_fusion.1.table_ref = bf16[64,64,128]{2,1,0:T(8,128)(2,1)} fusion(bf16[64,64,64]{2,1,0:T(8,128)(2,1)S(1)} %get-tuple-element.6, bf16[64,64,64]{2,1,0:T(8,128)(2,1)S(1)} %get-tuple-element.5), kind=kLoop, calls=%fused_computation.7 | loop fusion | flops 2097152 | bytes 2097152 | tf_op jit(solution)/shard_map/concatenate | solution.py:170
  51.1 14.5 %all-to-all-done.1.alpha_ref = f32[32,72,128]{2,1,0:T(8,128)} async-done(((f32[32,72,128]{2,1,0:T(8,128)}), f32[32,72,128]{2,1,0:T(8,128)}, u32[]{:S(2)}, u32[]{:S(2)}) %all-to-all-start.1) | async-done | bytes 1179680 | tf_op jit(solution)/shard_map/all_to_all | solution.py:198
  65.7 0.0 collective-permute-done.partner_ref
  65.7 17.1 %beta_sum.1 = f32[48,6144]{1,0:T(8,128)} custom-call(s32[12,96]{1,0:T(8,128)} %bitcast.2, s32[12,96]{1,0:T(8,128)} %bitcast.3, f32[32,72,128]{2,1,0:T(8,128)} %copy-done, f32[32,72,128]{2,1,0:T(8,128)} %collective-permute-done.partner_ref, f32[32,72,128]{2,1,0:T(8,128)} %all-to-all-done.1.alpha_ref, bf16[64,64,128]{2,1,0:T(8,128)(2,1)} %pad_maximum_fusion.1.table_ref), custom_call_target="tpu_custom_call" | custom-call | tf_op jit(solution)/shard_map/beta_sum/pallas_call | solution.py:199
Async XLA Ops:
  3.1 27.1 %all-to-all-start = ((f32[32,72,128]{2,1,0:T(8,128)}), f32[32,72,128]{2,1,0:T(8,128)S(1)}, u32[]{:S(2)}, u32[]{:S(2)}) async-start(f32[32,72,128]{2,1,0:T(8,128)} %coeff_slots.1), calls=%async_computation | async-start | bytes 2359296 | tf_op jit(solution)/shard_map/all_to_all | solution.py:196
  30.2 11.9 %copy-start = (f32[32,72,128]{2,1,0:T(8,128)}, f32[32,72,128]{2,1,0:T(8,128)S(1)}, u32[]{:S(2)}) copy-start(f32[32,72,128]{2,1,0:T(8,128)S(1)} %all-to-all-done.own_ref) | copy-start | bytes 3538948
  30.2 35.5 %collective-permute-start = (f32[32,72,128]{2,1,0:T(8,128)S(1)}, f32[32,72,128]{2,1,0:T(8,128)}, u32[]{:S(2)}, u32[]{:S(2)}) collective-permute-start(f32[32,72,128]{2,1,0:T(8,128)S(1)} %all-to-all-done.own_ref), channel_id=1, source_target_pairs={{0,32},{32,0},{64,96},{96,64},{128,160},{160,128},{192,224},{224,1... | collective-permute-start | bytes 3538952 | tf_op jit(solution)/shard_map/ppermute | solution.py:197
  42.1 23.6 %all-to-all-start.1 = ((f32[32,72,128]{2,1,0:T(8,128)}), f32[32,72,128]{2,1,0:T(8,128)}, u32[]{:S(2)}, u32[]{:S(2)}) async-start(f32[32,72,128]{2,1,0:T(8,128)} %alpha_slots.1), calls=%async_computation.1 | async-start | bytes 2359296 | tf_op jit(solution)/shard_map/all_to_all | solution.py:198

commit v2 on v1

--- a/solution.py
+++ b/solution.py
@@ -93,49 +93,63 @@
     write_slots(counts_ref, buf_ref, out_ref)
 
 
-def beta_kernel(blocks_ref, types_ref, own_ref, partner_ref, alpha_ref, table_ref, out_ref, hi_ref, lo_ref):
+def swap(x):
+    return pltpu.roll(x, BLK, 1)
+
+
+def unpack(ref, x_ref, base):
     left = left_half((CAP, 128))
     left_low = left_half((HALF, 128))
 
-    def swap(x):
-        return pltpu.roll(x, BLK, 1)
-
-    def unpack(ref, base):
-        def one(j, carry):
-            main = ref[j, 0:CAP, :]
-            low = ref[j, CAP:PACK, :]
-            main_r = swap(main)
-            low_r = swap(low)
-            parts = (
-                jnp.where(left, main, main_r),
-                jnp.where(left, main_r, main),
-                jnp.concatenate([jnp.where(left_low, low, low_r), jnp.where(left_low, low_r, low)], 0),
-            )
-            for n in range(3):
-                hi, lo = split(parts[n])
-                hi_ref[base + 3 * j + n] = hi
-                lo_ref[base + 3 * j + n] = lo
-            return carry
-
-        lax.fori_loop(0, COLS, one, 0)
-
-    unpack(own_ref, 0)
-    unpack(partner_ref, 96)
+    def one(j, carry):
+        main = ref[j, 0:CAP, :]
+        low = ref[j, CAP:PACK, :]
+        main_r = swap(main)
+        low_r = swap(low)
+        main_lo = main - main.astype(bf16).astype(f32)
+        low_lo = low - low.astype(bf16).astype(f32)
+        main_lo_r = swap(main_lo)
+        low_lo_r = swap(low_lo)
+        x_ref[base + 3 * j] = jnp.where(left, main, main_lo_r).astype(bf16)
+        x_ref[base + 3 * j + 1] = jnp.where(left, main_r, main_lo).astype(bf16)
+        x_ref[base + 3 * j + 2] = jnp.concatenate(
+            [jnp.where(left_low, low, low_lo_r), jnp.where(left_low, low_r, low_lo)], 0
+        ).astype(bf16)
+        return carry
+
+    lax.fori_loop(0, COLS, one, 0)
+
+
+def own_kernel(own_ref, x_ref):
+    unpack(own_ref, x_ref, 0)
+
+
+def beta_kernel(
+    blocks_ref, types_ref, own_hbm, partner_hbm, alpha_hbm, table_hbm, out_hbm,
+    x_ref, partner_ref, alpha_ref, table_ref, out_ref, sems, out_sems,
+):
+    own_copy = pltpu.make_async_copy(own_hbm, x_ref.at[0:96], sems.at[0])
+    partner_copy = pltpu.make_async_copy(partner_hbm, partner_ref, sems.at[1])
+    alpha_copy = pltpu.make_async_copy(alpha_hbm, alpha_ref, sems.at[2])
+    table_copy = pltpu.make_async_copy(table_hbm, table_ref, sems.at[3])
+    partner_copy.start()
+    own_copy.start()
+    table_copy.start()
+    alpha_copy.start()
+    left = left_half((CAP, 128))
+    partner_copy.wait()
+    unpack(partner_ref, x_ref, 96)
+    own_copy.wait()
+    table_copy.wait()
+    alpha_copy.wait()
 
     def block(m):
-        total = jnp.zeros((2 * CAP, 128), f32)
-        for g in range(3):
-            hi_parts, lo_parts, w_parts = [], [], []
-            for q in range(2):
-                s0 = blocks_ref[4 * g + 2 * q, m]
-                s1 = blocks_ref[4 * g + 2 * q + 1, m]
-                hi_parts.append(jnp.where(left, hi_ref[s0], hi_ref[s1]))
-                lo_parts.append(jnp.where(left, lo_ref[s0], lo_ref[s1]))
-                w_parts.append(table_ref[types_ref[4 * g + 2 * q, m]])
-                w_parts.append(table_ref[types_ref[4 * g + 2 * q + 1, m]])
-            lhs = jnp.concatenate([jnp.concatenate(hi_parts, 1), jnp.concatenate(lo_parts, 1)], 0)
-            total = total + jnp.dot(lhs, jnp.concatenate(w_parts, 0), preferred_element_type=f32)
-        both = total[0:CAP] + total[CAP:]
+        lhs, rhs = [], []
+        for k in range(12):
+            lhs.append(x_ref[blocks_ref[k, m]])
+            w = table_ref[types_ref[k, m]]
+            rhs += [w, w]
+        both = jnp.dot(jnp.concatenate(lhs, 1), jnp.concatenate(rhs, 0), preferred_element_type=f32)
         return both + swap(both)
 
     def triple(u, carry):
@@ -153,7 +167,15 @@
             out_ref[:, pl.ds(col, 128)] = alphas[q] + pair
         return carry
 
-    lax.fori_loop(0, COLS // 2, triple, 0)
+    copies = []
+    for part in range(4):
+        lax.fori_loop(4 * part, 4 * part + 4, triple, 0)
+        cols = slice(1536 * part, 1536 * part + 1536)
+        copy = pltpu.make_async_copy(out_ref.at[:, cols], out_hbm.at[:, cols], out_sems.at[part])
+        copy.start()
+        copies.append(copy)
+    for copy in copies:
+        copy.wait()
 
 
 def smem():
@@ -162,6 +184,10 @@
 
 def vmem():
     return pl.BlockSpec(memory_space=pltpu.VMEM)
+
+
+def hbm():
+    return pl.BlockSpec(memory_space=pl.ANY)
 
 
 def split_table(table):
@@ -194,16 +220,32 @@
         name="alpha_slots",
     )(row_counts, alpha_blocks, alpha_types, coeffs_t, split_table(alpha_table))
     own = lax.all_to_all(coeff_slots, "col", split_axis=0, concat_axis=0, tiled=True)
+    own, alpha_slots = lax.optimization_barrier((own, alpha_slots))
     partner = lax.ppermute(own, "cls", [(i, i ^ 1) for i in range(8)])
     alpha = lax.all_to_all(alpha_slots, "col", split_axis=0, concat_axis=0, tiled=True)
+    own_x = pl.pallas_call(
+        own_kernel,
+        in_specs=[vmem()],
+        out_specs=vmem(),
+        out_shape=jax.ShapeDtypeStruct((96, CAP, 128), bf16),
+        name="own_split",
+    )(own)
     return pl.pallas_call(
         beta_kernel,
-        in_specs=[smem(), smem(), vmem(), vmem(), vmem(), vmem()],
-        out_specs=vmem(),
+        in_specs=[smem(), smem(), hbm(), hbm(), hbm(), hbm()],
+        out_specs=hbm(),
         out_shape=jax.ShapeDtypeStruct((CAP, 96 * BLK), f32),
-        scratch_shapes=[pltpu.VMEM((192, CAP, 128), bf16), pltpu.VMEM((192, CAP, 128), bf16)],
+        scratch_shapes=[
+            pltpu.VMEM((192, CAP, 128), bf16),
+            pltpu.VMEM((COLS, PACK, 128), f32),
+            pltpu.VMEM((COLS, PACK, 128), f32),
+            pltpu.VMEM((64, BLK, 128), bf16),
+            pltpu.VMEM((CAP, 96 * BLK), f32),
+            pltpu.SemaphoreType.DMA((4,)),
+            pltpu.SemaphoreType.DMA((4,)),
+        ],
         name="beta_sum",
-    )(beta_blocks.T, beta_types.T, own, partner, alpha, split_table(beta_table))
+    )(beta_blocks.T, beta_types.T, own_x, partner, alpha, split_table(beta_table))
 
 
 def solution(mesh):

time: 83.2 us -> 72.4 us (0.87)
  waiting for transfers between devices: 29.2 us -> 19.1 us
  other arithmetic: 7.12 us -> 4.35 us
  Pallas kernels: 27.3 us -> 29.3 us
    all_to_all x1, waiting for transfers between devices: 14.6 us -> 7.22 us  [on_device(): lax.all_to_all(coeff_slots, 'col', split_axis=0, concat_axis=0, tiled=True)]
    all_to_all x1, waiting for transfers between devices: 14.5 us -> 9.58 us  [on_device(): lax.all_to_all(alpha_slots, 'col', split_axis=0, concat_axis=0, tiled=True)]
    ppermute x1, waiting for transfers between devices: 0.01 us -> 2.32 us  [on_device(): partner = lax.ppermute(own, 'cls', [(i, i ^ 1) for i in range(8)])]
    pallas_call x1 -> x2, Pallas kernels: 17.1 us -> 19.1 us  [the longest x1 14.2 us: on_device(): pl.pallas_call(beta_kernel, in_specs=[smem(), smem(), hbm(), hbm(), hbm()...]
    concatenate x2, other arithmetic: 4.66 us -> 3.2 us  [split_table(): return jnp.concatenate([hi, tiles - hi], 2).astype(bf16)]
    another operation x2, other arithmetic: 2.46 us -> 1.15 us
  transfers between devices with their start and end apart: 3 -> 3, of which waited for: 2 -> 3; matrix products, arithmetic and copies ran while one was open for 13% -> 12% of each run, Pallas kernels for 9% -> 17%
where the time goes in v2:
time: 72.4 us; the launch traced here: 72 us
  Pallas kernels  29.3 us (40%)
  waiting for transfers between devices  19.1 us (26%)
  starting transfers between devices  15.1 us (21%)
  other arithmetic  4.35 us (6%)
  local copies, waits for them, and re-layouts  4.01 us (6%)
    pallas_call x1, Pallas kernels, on_device(): pl.pallas_call(beta_kernel, in_specs=[smem(), smem(), hbm(), hbm(), hbm()...  14.2 us
    all_to_all x1, waiting for transfers between devices, on_device(): lax.all_to_all(alpha_slots, 'col', split_axis=0, concat_axis=0, tiled=True)  9.58 us
    all_to_all x1, starting transfers between devices, on_device(): lax.all_to_all(coeff_slots, 'col', split_axis=0, concat_axis=0, tiled=True)  8.58 us
    all_to_all x1, waiting for transfers between devices, on_device(): lax.all_to_all(coeff_slots, 'col', split_axis=0, concat_axis=0, tiled=True)  7.22 us
    pallas_call x1, Pallas kernels, on_device(): pl.pallas_call(alpha_kernel, in_specs=[smem(), smem(), smem(), vmem(), vm...  7.13 us
    all_to_all x1, starting transfers between devices, on_device(): lax.all_to_all(alpha_slots, 'col', split_axis=0, concat_axis=0, tiled=True)  4.92 us
    pallas_call x1, Pallas kernels, on_device(): pl.pallas_call(own_kernel, in_specs=[vmem()], out_specs=vmem(), out_shape...  4.9 us
    reshape x2, local copies, waits for them, and re-layouts, split_table(): tiles = table.reshape(table.shape[0], BLK, BLK)  4.01 us
  transfers between devices with their start and end apart: 3, of which 3 were waited for; matrix products, arithmetic and copies ran while one was open for 12% of the time, Pallas kernels for 17%

profile of v2, /device:TPU:1, one launch (start us, length us, event | category | flops | bytes accessed | tf_op | source)
XLA Modules:
  0.0 72.0 jit_solution(12187057736923711375)
XLA Ops:
  0.0 3.1 %coeff_slots.1 = f32[32,72,128]{2,1,0:T(8,128)} custom-call(s32[32]{0:T(128)} %counts_ref.3, f32[192,1024]{1,0:T(8,128)} %x_ref.3), custom_call_target="tpu_custom_call" | custom-call | tf_op jit(solution)/shard_map/coeff_slots/pallas_call | solution.py:201
  3.1 8.6 %all-to-all-start = ((f32[32,72,128]{2,1,0:T(8,128)}), f32[32,72,128]{2,1,0:T(8,128)S(1)}, u32[]{:S(2)}, u32[]{:S(2)}) async-start(f32[32,72,128]{2,1,0:T(8,128)} %coeff_slots.1), calls=%async_computation | async-start | bytes 2359296 | tf_op jit(solution)/shard_map/all_to_all | solution.py:222
  11.7 2.0 %reshape.6 = f32[64,64,64]{2,1,0:T(8,128)S(1)} reshape(f32[64,4096]{1,0:T(8,128)} %param.9) | data formatting | bytes 2097152 | tf_op jit(solution)/shard_map/reshape | solution.py:194
  13.7 0.6 reduce-precision_convert_fusion.1
  14.3 1.6 %pad_maximum_fusion.table_ref = bf16[64,64,128]{2,1,0:T(8,128)(2,1)} fusion(bf16[64,64,64]{2,1,0:T(8,128)(2,1)S(1)} %get-tuple-element.12, bf16[64,64,64]{2,1,0:T(8,128)(2,1)S(1)} %get-tuple-element.11), kind=kLoop, calls=%fused_computation.6 | loop fusion | flops 2097152 | bytes 2097152 | tf_op jit(solution)/shard_map/concatenate | solution.py:196
  15.9 7.1 %alpha_slots.1 = f32[32,72,128]{2,1,0:T(8,128)} custom-call(s32[32]{0:T(128)} %counts_ref.3, s32[16,16]{1,0:T(8,128)} %blocks_ref.1, s32[16,16]{1,0:T(8,128)} %types_ref.1, f32[192,1024]{1,0:T(8,128)} %x_ref.3, bf16[64,64,128]{2,1,0:T(8,128)(2,1)} %pad_maximum_fusion.table_ref), custom_call_target="tpu_custom_call" | custom-call | tf_op jit(solution)/shard_map/alpha_slots/pallas_call | solution.py:209
  23.0 7.2 %all-to-all-done.own_ref = f32[32,72,128]{2,1,0:T(8,128)S(1)} async-done(((f32[32,72,128]{2,1,0:T(8,128)}), f32[32,72,128]{2,1,0:T(8,128)S(1)}, u32[]{:S(2)}, u32[]{:S(2)}) %all-to-all-start) | async-done | bytes 1179680 | tf_op jit(solution)/shard_map/all_to_all | solution.py:222
  30.2 0.0 copy-start
  30.2 1.6 %collective-permute-start = (f32[32,72,128]{2,1,0:T(8,128)S(1)}, f32[32,72,128]{2,1,0:T(8,128)}, u32[]{:S(2)}, u32[]{:S(2)}) collective-permute-start(f32[32,72,128]{2,1,0:T(8,128)S(1)} %all-to-all-done.own_ref), channel_id=1, source_target_pairs={{0,32},{32,0},{64,96},{96,64},{128,160},{160,128},{192,224},{224,1... | collective-permute-start | bytes 3538952 | tf_op jit(solution)/shard_map/ppermute | solution.py:224
  31.8 4.9 %all-to-all-start.1 = ((f32[32,72,128]{2,1,0:T(8,128)}), f32[32,72,128]{2,1,0:T(8,128)}, u32[]{:S(2)}, u32[]{:S(2)}) async-start(f32[32,72,128]{2,1,0:T(8,128)} %alpha_slots.1), calls=%async_computation.1 | async-start | bytes 2359296 | tf_op jit(solution)/shard_map/all_to_all | solution.py:225
  36.8 2.0 %reshape.7 = f32[64,64,64]{2,1,0:T(8,128)S(1)} reshape(f32[64,4096]{1,0:T(8,128)} %param.12) | data formatting | bytes 2097152 | tf_op jit(solution)/shard_map/reshape | solution.py:194
  38.8 0.0 copy-done
  38.8 0.6 reduce-precision_convert_fusion
  39.4 1.6 %pad_maximum_fusion.1.table_hbm = bf16[64,64,128]{2,1,0:T(8,128)(2,1)} fusion(bf16[64,64,64]{2,1,0:T(8,128)(2,1)S(1)} %get-tuple-element.10, bf16[64,64,64]{2,1,0:T(8,128)(2,1)S(1)} %get-tuple-element.9), kind=kLoop, calls=%fused_computation.7 | loop fusion | flops 2097152 | bytes 2097152 | tf_op jit(solution)/shard_map/concatenate | solution.py:196
  41.0 4.9 %own_split.1.own_hbm = bf16[96,48,128]{2,1,0:T(8,128)(2,1)} custom-call(f32[32,72,128]{2,1,0:T(8,128)} %copy-done), custom_call_target="tpu_custom_call" | custom-call | tf_op jit(solution)/shard_map/own_split/pallas_call | solution.py:226
  45.9 9.6 %all-to-all-done.1.alpha_hbm = f32[32,72,128]{2,1,0:T(8,128)} async-done(((f32[32,72,128]{2,1,0:T(8,128)}), f32[32,72,128]{2,1,0:T(8,128)}, u32[]{:S(2)}, u32[]{:S(2)}) %all-to-all-start.1) | async-done | bytes 1179680 | tf_op jit(solution)/shard_map/all_to_all | solution.py:225
  55.5 2.3 %collective-permute-done.partner_hbm = f32[32,72,128]{2,1,0:T(8,128)} collective-permute-done((f32[32,72,128]{2,1,0:T(8,128)S(1)}, f32[32,72,128]{2,1,0:T(8,128)}, u32[]{:S(2)}, u32[]{:S(2)}) %collective-permute-start) | collective-permute-done | bytes 1179680 | tf_op jit(solution)/shard_map/ppermute | solution.py:224
  57.8 14.2 %beta_sum.1 = f32[48,6144]{1,0:T(8,128)} custom-call(s32[12,96]{1,0:T(8,128)} %bitcast.2, s32[12,96]{1,0:T(8,128)} %bitcast.3, bf16[96,48,128]{2,1,0:T(8,128)(2,1)} %own_split.1.own_hbm, f32[32,72,128]{2,1,0:T(8,128)} %collective-permute-done.partner_hbm, f32[32,72,128]{2,1,0:T(8,128)} %all-to-all-done.1.alpha_hbm, ...), custom_call_target="tpu_custom_call" | custom-call | tf_op jit(solution)/shard_map/beta_sum/pallas_call | solution.py:233
Async XLA Ops:
  3.1 27.1 %all-to-all-start = ((f32[32,72,128]{2,1,0:T(8,128)}), f32[32,72,128]{2,1,0:T(8,128)S(1)}, u32[]{:S(2)}, u32[]{:S(2)}) async-start(f32[32,72,128]{2,1,0:T(8,128)} %coeff_slots.1), calls=%async_computation | async-start | bytes 2359296 | tf_op jit(solution)/shard_map/all_to_all | solution.py:222
  30.2 8.6 %copy-start = (f32[32,72,128]{2,1,0:T(8,128)}, f32[32,72,128]{2,1,0:T(8,128)S(1)}, u32[]{:S(2)}) copy-start(f32[32,72,128]{2,1,0:T(8,128)S(1)} %all-to-all-done.own_ref) | copy-start | bytes 3538948
  30.2 27.6 %collective-permute-start = (f32[32,72,128]{2,1,0:T(8,128)S(1)}, f32[32,72,128]{2,1,0:T(8,128)}, u32[]{:S(2)}, u32[]{:S(2)}) collective-permute-start(f32[32,72,128]{2,1,0:T(8,128)S(1)} %all-to-all-done.own_ref), channel_id=1, source_target_pairs={{0,32},{32,0},{64,96},{96,64},{128,160},{160,128},{192,224},{224,1... | collective-permute-start | bytes 3538952 | tf_op jit(solution)/shard_map/ppermute | solution.py:224
  31.8 23.6 %all-to-all-start.1 = ((f32[32,72,128]{2,1,0:T(8,128)}), f32[32,72,128]{2,1,0:T(8,128)}, u32[]{:S(2)}, u32[]{:S(2)}) async-start(f32[32,72,128]{2,1,0:T(8,128)} %alpha_slots.1), calls=%async_computation.1 | async-start | bytes 2359296 | tf_op jit(solution)/shard_map/all_to_all | solution.py:225

commit v3 on v2

--- a/solution.py
+++ b/solution.py
@@ -97,7 +97,7 @@
     return pltpu.roll(x, BLK, 1)
 
 
-def unpack(ref, x_ref, base):
+def unpack(ref, z_ref, base):
     left = left_half((CAP, 128))
     left_low = left_half((HALF, 128))
 
@@ -106,15 +106,14 @@
         low = ref[j, CAP:PACK, :]
         main_r = swap(main)
         low_r = swap(low)
-        main_lo = main - main.astype(bf16).astype(f32)
-        low_lo = low - low.astype(bf16).astype(f32)
-        main_lo_r = swap(main_lo)
-        low_lo_r = swap(low_lo)
-        x_ref[base + 3 * j] = jnp.where(left, main, main_lo_r).astype(bf16)
-        x_ref[base + 3 * j + 1] = jnp.where(left, main_r, main_lo).astype(bf16)
-        x_ref[base + 3 * j + 2] = jnp.concatenate(
-            [jnp.where(left_low, low, low_lo_r), jnp.where(left_low, low_r, low_lo)], 0
-        ).astype(bf16)
+        parts = (
+            jnp.where(left, main, main_r),
+            jnp.where(left, main_r, main),
+            jnp.concatenate([jnp.where(left_low, low, low_r), jnp.where(left_low, low_r, low)], 0),
+        )
+        for n in range(3):
+            hi, lo = split(parts[n])
+            z_ref[base + 3 * j + n] = jnp.concatenate([hi, lo], 1)
         return carry
 
     lax.fori_loop(0, COLS, one, 0)
@@ -143,16 +142,27 @@
     table_copy.wait()
     alpha_copy.wait()
 
+    pick = left_half((CAP, 256)) | (lax.broadcasted_iota(jnp.int32, (CAP, 256), 1) // BLK == 2)
+
     def block(m):
-        lhs, rhs = [], []
-        for k in range(12):
-            lhs.append(x_ref[blocks_ref[k, m]])
-            w = table_ref[types_ref[k, m]]
-            rhs += [w, w]
-        both = jnp.dot(jnp.concatenate(lhs, 1), jnp.concatenate(rhs, 0), preferred_element_type=f32)
+        hi, lo, w = [], [], []
+        for k in range(0, 12, 2):
+            pair = jnp.where(pick, x_ref[blocks_ref[k, m]], x_ref[blocks_ref[k + 1, m]])
+            hi.append(pair[:, 0:128])
+            lo.append(pair[:, 128:256])
+            w.append(table_ref[types_ref[k, m]])
+            w.append(table_ref[types_ref[k + 1, m]])
+        lhs = jnp.concatenate([jnp.concatenate(hi, 1), jnp.concatenate(lo, 1)], 0)
+        both = jnp.dot(lhs, jnp.concatenate(w, 0), preferred_element_type=f32)
+        both = both[0:CAP] + both[CAP:]
         return both + swap(both)
 
-    def triple(u, carry):
+    def triples(n, carry):
+        for half in range(2):
+            triple(2 * n + half)
+        return carry
+
+    def triple(u):
         a_main, a_low = alpha_ref[2 * u, 0:CAP, :], alpha_ref[2 * u, CAP:PACK, :]
         b_main, b_low = alpha_ref[2 * u + 1, 0:CAP, :], alpha_ref[2 * u + 1, CAP:PACK, :]
         b_main_r = swap(b_main)
@@ -165,11 +175,10 @@
             pair = jnp.where(left, block(6 * u + 2 * q), block(6 * u + 2 * q + 1))
             col = pl.multiple_of(u * 384 + 128 * q, 128)
             out_ref[:, pl.ds(col, 128)] = alphas[q] + pair
-        return carry
 
     copies = []
     for part in range(4):
-        lax.fori_loop(4 * part, 4 * part + 4, triple, 0)
+        lax.fori_loop(2 * part, 2 * part + 2, triples, 0)
         cols = slice(1536 * part, 1536 * part + 1536)
         copy = pltpu.make_async_copy(out_ref.at[:, cols], out_hbm.at[:, cols], out_sems.at[part])
         copy.start()
@@ -227,7 +236,7 @@
         own_kernel,
         in_specs=[vmem()],
         out_specs=vmem(),
-        out_shape=jax.ShapeDtypeStruct((96, CAP, 128), bf16),
+        out_shape=jax.ShapeDtypeStruct((96, CAP, 256), bf16),
         name="own_split",
     )(own)
     return pl.pallas_call(
@@ -236,7 +245,7 @@
         out_specs=hbm(),
         out_shape=jax.ShapeDtypeStruct((CAP, 96 * BLK), f32),
         scratch_shapes=[
-            pltpu.VMEM((192, CAP, 128), bf16),
+            pltpu.VMEM((192, CAP, 256), bf16),
             pltpu.VMEM((COLS, PACK, 128), f32),
             pltpu.VMEM((COLS, PACK, 128), f32),
             pltpu.VMEM((64, BLK, 128), bf16),

time: 72.4 us -> 70 us (0.967)
  Pallas kernels: 29.3 us -> 27.3 us
    pallas_call x1, Pallas kernels: 14.2 us -> 11.7 us  [on_device(): pl.pallas_call(beta_kernel, in_specs=[smem(), smem(), hbm(), hbm(), hbm()...]
  transfers between devices with their start and end apart: 3 -> 3, of which waited for: 3 -> 3; matrix products, arithmetic and copies ran while one was open for 12% -> 12% of each run, Pallas kernels for 17% -> 18%
where the time goes in v3:
time: 70 us; the launch traced here: 69.5 us
  Pallas kernels  27.3 us (39%)
  waiting for transfers between devices  18.7 us (27%)
  starting transfers between devices  15.1 us (22%)
  other arithmetic  4.28 us (6%)
  local copies, waits for them, and re-layouts  4.01 us (6%)
    pallas_call x1, Pallas kernels, on_device(): pl.pallas_call(beta_kernel, in_specs=[smem(), smem(), hbm(), hbm(), hbm()...  11.7 us
    all_to_all x1, waiting for transfers between devices, on_device(): lax.all_to_all(alpha_slots, 'col', split_axis=0, concat_axis=0, tiled=True)  9.19 us
    all_to_all x1, starting transfers between devices, on_device(): lax.all_to_all(coeff_slots, 'col', split_axis=0, concat_axis=0, tiled=True)  8.58 us
    all_to_all x1, waiting for transfers between devices, on_device(): lax.all_to_all(coeff_slots, 'col', split_axis=0, concat_axis=0, tiled=True)  7.24 us
    pallas_call x1, Pallas kernels, on_device(): pl.pallas_call(alpha_kernel, in_specs=[smem(), smem(), smem(), vmem(), vm...  7.14 us
    pallas_call x1, Pallas kernels, on_device(): pl.pallas_call(own_kernel, in_specs=[vmem()], out_specs=vmem(), out_shape...  5.34 us
    all_to_all x1, starting transfers between devices, on_device(): lax.all_to_all(alpha_slots, 'col', split_axis=0, concat_axis=0, tiled=True)  4.93 us
    reshape x2, local copies, waits for them, and re-layouts, split_table(): tiles = table.reshape(table.shape[0], BLK, BLK)  4.01 us
  transfers between devices with their start and end apart: 3, of which 3 were waited for; matrix products, arithmetic and copies ran while one was open for 12% of the time, Pallas kernels for 18%

profile of v3, /device:TPU:1, one launch (start us, length us, event | category | flops | bytes accessed | tf_op | source)
XLA Modules:
  0.0 69.5 jit_solution(13255758447883829446)
XLA Ops:
  0.0 3.1 %coeff_slots.1 = f32[32,72,128]{2,1,0:T(8,128)} custom-call(s32[32]{0:T(128)} %counts_ref.3, f32[192,1024]{1,0:T(8,128)} %x_ref.3), custom_call_target="tpu_custom_call" | custom-call | tf_op jit(solution)/shard_map/coeff_slots/pallas_call | solution.py:210
  3.1 8.6 %all-to-all-start = ((f32[32,72,128]{2,1,0:T(8,128)}), f32[32,72,128]{2,1,0:T(8,128)S(1)}, u32[]{:S(2)}, u32[]{:S(2)}) async-start(f32[32,72,128]{2,1,0:T(8,128)} %coeff_slots.1), calls=%async_computation | async-start | bytes 2359296 | tf_op jit(solution)/shard_map/all_to_all | solution.py:231
  11.7 2.0 %reshape.6 = f32[64,64,64]{2,1,0:T(8,128)S(1)} reshape(f32[64,4096]{1,0:T(8,128)} %param.9) | data formatting | bytes 2097152 | tf_op jit(solution)/shard_map/reshape | solution.py:203
  13.7 0.6 reduce-precision_convert_fusion.1
  14.3 1.6 %pad_maximum_fusion.table_ref = bf16[64,64,128]{2,1,0:T(8,128)(2,1)} fusion(bf16[64,64,64]{2,1,0:T(8,128)(2,1)S(1)} %get-tuple-element.12, bf16[64,64,64]{2,1,0:T(8,128)(2,1)S(1)} %get-tuple-element.11), kind=kLoop, calls=%fused_computation.6 | loop fusion | flops 2097152 | bytes 2097152 | tf_op jit(solution)/shard_map/concatenate | solution.py:205
  15.8 7.1 %alpha_slots.1 = f32[32,72,128]{2,1,0:T(8,128)} custom-call(s32[32]{0:T(128)} %counts_ref.3, s32[16,16]{1,0:T(8,128)} %blocks_ref.1, s32[16,16]{1,0:T(8,128)} %types_ref.1, f32[192,1024]{1,0:T(8,128)} %x_ref.3, bf16[64,64,128]{2,1,0:T(8,128)(2,1)} %pad_maximum_fusion.table_ref), custom_call_target="tpu_custom_call" | custom-call | tf_op jit(solution)/shard_map/alpha_slots/pallas_call | solution.py:218
  23.0 7.2 %all-to-all-done.own_ref = f32[32,72,128]{2,1,0:T(8,128)S(1)} async-done(((f32[32,72,128]{2,1,0:T(8,128)}), f32[32,72,128]{2,1,0:T(8,128)S(1)}, u32[]{:S(2)}, u32[]{:S(2)}) %all-to-all-start) | async-done | bytes 1179680 | tf_op jit(solution)/shard_map/all_to_all | solution.py:231
  30.2 0.0 copy-start
  30.2 1.6 %collective-permute-start = (f32[32,72,128]{2,1,0:T(8,128)S(1)}, f32[32,72,128]{2,1,0:T(8,128)}, u32[]{:S(2)}, u32[]{:S(2)}) collective-permute-start(f32[32,72,128]{2,1,0:T(8,128)S(1)} %all-to-all-done.own_ref), channel_id=1, source_target_pairs={{0,32},{32,0},{64,96},{96,64},{128,160},{160,128},{192,224},{224,1... | collective-permute-start | bytes 3538952 | tf_op jit(solution)/shard_map/ppermute | solution.py:233
  31.8 4.9 %all-to-all-start.1 = ((f32[32,72,128]{2,1,0:T(8,128)}), f32[32,72,128]{2,1,0:T(8,128)}, u32[]{:S(2)}, u32[]{:S(2)}) async-start(f32[32,72,128]{2,1,0:T(8,128)} %alpha_slots.1), calls=%async_computation.1 | async-start | bytes 2359296 | tf_op jit(solution)/shard_map/all_to_all | solution.py:234
  36.8 2.0 %reshape.7 = f32[64,64,64]{2,1,0:T(8,128)S(1)} reshape(f32[64,4096]{1,0:T(8,128)} %param.12) | data formatting | bytes 2097152 | tf_op jit(solution)/shard_map/reshape | solution.py:203
  38.8 0.0 copy-done
  38.8 0.6 reduce-precision_convert_fusion
  39.4 1.6 %pad_maximum_fusion.1.table_hbm = bf16[64,64,128]{2,1,0:T(8,128)(2,1)} fusion(bf16[64,64,64]{2,1,0:T(8,128)(2,1)S(1)} %get-tuple-element.10, bf16[64,64,64]{2,1,0:T(8,128)(2,1)S(1)} %get-tuple-element.9), kind=kLoop, calls=%fused_computation.7 | loop fusion | flops 2097152 | bytes 2097152 | tf_op jit(solution)/shard_map/concatenate | solution.py:205
  41.0 5.3 %own_split.1.own_hbm = bf16[96,48,256]{2,1,0:T(8,128)(2,1)} custom-call(f32[32,72,128]{2,1,0:T(8,128)} %copy-done), custom_call_target="tpu_custom_call" | custom-call | tf_op jit(solution)/shard_map/own_split/pallas_call | solution.py:235
  46.3 9.2 %all-to-all-done.1.alpha_hbm = f32[32,72,128]{2,1,0:T(8,128)} async-done(((f32[32,72,128]{2,1,0:T(8,128)}), f32[32,72,128]{2,1,0:T(8,128)}, u32[]{:S(2)}, u32[]{:S(2)}) %all-to-all-start.1) | async-done | bytes 1179680 | tf_op jit(solution)/shard_map/all_to_all | solution.py:234
  55.5 2.3 %collective-permute-done.partner_hbm = f32[32,72,128]{2,1,0:T(8,128)} collective-permute-done((f32[32,72,128]{2,1,0:T(8,128)S(1)}, f32[32,72,128]{2,1,0:T(8,128)}, u32[]{:S(2)}, u32[]{:S(2)}) %collective-permute-start) | collective-permute-done | bytes 1179680 | tf_op jit(solution)/shard_map/ppermute | solution.py:233
  57.8 11.7 %beta_sum.1 = f32[48,6144]{1,0:T(8,128)} custom-call(s32[12,96]{1,0:T(8,128)} %bitcast.2, s32[12,96]{1,0:T(8,128)} %bitcast.3, bf16[96,48,256]{2,1,0:T(8,128)(2,1)} %own_split.1.own_hbm, f32[32,72,128]{2,1,0:T(8,128)} %collective-permute-done.partner_hbm, f32[32,72,128]{2,1,0:T(8,128)} %all-to-all-done.1.alpha_hbm, ...), custom_call_target="tpu_custom_call" | custom-call | tf_op jit(solution)/shard_map/beta_sum/pallas_call | solution.py:242
Async XLA Ops:
  3.1 27.1 %all-to-all-start = ((f32[32,72,128]{2,1,0:T(8,128)}), f32[32,72,128]{2,1,0:T(8,128)S(1)}, u32[]{:S(2)}, u32[]{:S(2)}) async-start(f32[32,72,128]{2,1,0:T(8,128)} %coeff_slots.1), calls=%async_computation | async-start | bytes 2359296 | tf_op jit(solution)/shard_map/all_to_all | solution.py:231
  30.2 8.6 %copy-start = (f32[32,72,128]{2,1,0:T(8,128)}, f32[32,72,128]{2,1,0:T(8,128)S(1)}, u32[]{:S(2)}) copy-start(f32[32,72,128]{2,1,0:T(8,128)S(1)} %all-to-all-done.own_ref) | copy-start | bytes 3538948
  30.2 27.6 %collective-permute-start = (f32[32,72,128]{2,1,0:T(8,128)S(1)}, f32[32,72,128]{2,1,0:T(8,128)}, u32[]{:S(2)}, u32[]{:S(2)}) collective-permute-start(f32[32,72,128]{2,1,0:T(8,128)S(1)} %all-to-all-done.own_ref), channel_id=1, source_target_pairs={{0,32},{32,0},{64,96},{96,64},{128,160},{160,128},{192,224},{224,1... | collective-permute-start | bytes 3538952 | tf_op jit(solution)/shard_map/ppermute | solution.py:233
  31.8 23.6 %all-to-all-start.1 = ((f32[32,72,128]{2,1,0:T(8,128)}), f32[32,72,128]{2,1,0:T(8,128)}, u32[]{:S(2)}, u32[]{:S(2)}) async-start(f32[32,72,128]{2,1,0:T(8,128)} %alpha_slots.1), calls=%async_computation.1 | async-start | bytes 2359296 | tf_op jit(solution)/shard_map/all_to_all | solution.py:234

commit v4 on v2

--- a/solution.py
+++ b/solution.py
@@ -12,9 +12,14 @@
 BLK = 64
 COLS = 32
 CAP = 48
-LOCAL = 192
 HALF = CAP // 2
 PACK = CAP + HALF
+BLOCKS = 96
+DEPTH = 12
+FIRST = 22
+BOUNDS = (0, BLOCKS, BLOCKS + 3 * FIRST, 2 * BLOCKS)
+UNROLL = 32
+LIST = 640
 ROWS = NA + CAP + 8
 
 
@@ -97,60 +102,131 @@
     return pltpu.roll(x, BLK, 1)
 
 
-def unpack(ref, x_ref, base):
+def unpack(ref, senders, x_ref):
     left = left_half((CAP, 128))
     left_low = left_half((HALF, 128))
 
     def one(j, carry):
         main = ref[j, 0:CAP, :]
         low = ref[j, CAP:PACK, :]
-        main_r = swap(main)
-        low_r = swap(low)
         main_lo = main - main.astype(bf16).astype(f32)
         low_lo = low - low.astype(bf16).astype(f32)
-        main_lo_r = swap(main_lo)
-        low_lo_r = swap(low_lo)
-        x_ref[base + 3 * j] = jnp.where(left, main, main_lo_r).astype(bf16)
-        x_ref[base + 3 * j + 1] = jnp.where(left, main_r, main_lo).astype(bf16)
-        x_ref[base + 3 * j + 2] = jnp.concatenate(
+        main_r, low_r, main_lo_r, low_lo_r = swap(main), swap(low), swap(main_lo), swap(low_lo)
+        x_ref[3 * j] = jnp.where(left, main, main_lo_r).astype(bf16)
+        x_ref[3 * j + 1] = jnp.where(left, main_r, main_lo).astype(bf16)
+        x_ref[3 * j + 2] = jnp.concatenate(
             [jnp.where(left_low, low, low_lo_r), jnp.where(left_low, low_r, low_lo)], 0
         ).astype(bf16)
         return carry
 
-    lax.fori_loop(0, COLS, one, 0)
-
-
-def own_kernel(own_ref, x_ref):
-    unpack(own_ref, x_ref, 0)
-
-
-def beta_kernel(
-    blocks_ref, types_ref, own_hbm, partner_hbm, alpha_hbm, table_hbm, out_hbm,
-    x_ref, partner_ref, alpha_ref, table_ref, out_ref, sems, out_sems,
+    lax.fori_loop(0, senders, one, 0)
+    x_ref[3 * senders] = jnp.zeros((CAP, 128), bf16)
+
+
+def plan_kernel(blocks_ref, types_ref, words_ref, lists_ref, totals_ref, entry_ref, counts_ref, smem_ref, sem):
+    entry_ref[...] = jnp.full((16, 128), 1 << 20, jnp.int32)
+    entry_ref[0:DEPTH, 0:BLOCKS] = blocks_ref[...]
+    entries = entry_ref[...]
+    entry_ref[...] = jnp.zeros((16, 128), jnp.int32)
+    entry_ref[0:DEPTH, 0:BLOCKS] = types_ref[...]
+    types = entry_ref[...]
+    row = lax.broadcasted_iota(jnp.int32, (16, 128), 0)
+    counts_ref[...] = jnp.zeros((8, 128), jnp.int32)
+    for q in range(3):
+        low, high = BOUNDS[q], BOUNDS[q + 1]
+        held = jnp.where((entries >= low) & (entries < high), 1, 0)
+        word = (types << 8) | (entries - low)
+        rank = jnp.zeros((1, 128), jnp.int32)
+        ordered = jnp.full((16, 128), high - low, jnp.int32)
+        for k in range(DEPTH):
+            here = (row == rank) & (held[k:k + 1] > 0)
+            ordered = jnp.where(here, word[k:k + 1], ordered)
+            rank = rank + held[k:k + 1]
+        words_ref[q] = ordered
+        counts_ref[q:q + 1, :] = (rank + 1) >> 1
+    copy = pltpu.make_async_copy(counts_ref, smem_ref, sem)
+    copy.start()
+    copy.wait()
+    for q in range(3):
+
+        def add(m, at):
+            for i in range(DEPTH // 2):
+                lists_ref[q, at + i] = m * 8 + i
+            return at + smem_ref[q, m]
+
+        end = lax.fori_loop(0, BLOCKS, add, jnp.int32(0))
+        for i in range(UNROLL):
+            lists_ref[q, end + i] = BLOCKS * 8
+        totals_ref[q] = (end + UNROLL - 1) // UNROLL
+
+
+def accumulate(q, words_ref, lists_ref, totals_ref, x_ref, table_ref, acc_ref):
+    def batch(n, carry):
+        for i in range(UNROLL):
+            item = lists_ref[q, n * UNROLL + i]
+            m = item >> 3
+            pair = (item & 7) * 2
+            w0 = words_ref[q, pair, m]
+            w1 = words_ref[q, pair + 1, m]
+            t0 = table_ref[w0 >> 8]
+            t1 = table_ref[w1 >> 8]
+            lhs = jnp.concatenate([x_ref[w0 & 255], x_ref[w1 & 255]], 1)
+            rhs = jnp.concatenate([t0, t0, t1, t1], 0)
+            acc_ref[m] = acc_ref[m] + jnp.dot(lhs, rhs, preferred_element_type=f32)
+        return carry
+
+    lax.fori_loop(0, totals_ref[q], batch, 0)
+
+
+def zero(acc_ref):
+    def one(m, carry):
+        acc_ref[m] = jnp.zeros((CAP, 128), f32)
+        return carry
+
+    lax.fori_loop(0, BLOCKS + 1, one, 0)
+
+
+def folded(acc_ref, pair, left):
+    a = acc_ref[2 * pair]
+    b = acc_ref[2 * pair + 1]
+    return jnp.where(left, a + swap(a), b + swap(b))
+
+
+def own_kernel(words_ref, lists_ref, totals_ref, own_ref, table_ref, acc_ref, x_ref):
+    zero(acc_ref)
+    unpack(own_ref, COLS, x_ref)
+    accumulate(0, words_ref, lists_ref, totals_ref, x_ref, table_ref, acc_ref)
+
+
+def first_kernel(words_ref, lists_ref, totals_ref, partner_ref, table_ref, prior_hbm, out_ref, x_ref, acc_ref, sem):
+    copy = pltpu.make_async_copy(prior_hbm, acc_ref, sem)
+    copy.start()
+    unpack(partner_ref, FIRST, x_ref)
+    copy.wait()
+    accumulate(1, words_ref, lists_ref, totals_ref, x_ref, table_ref, acc_ref)
+    left = left_half((CAP, 128))
+
+    def one(p, carry):
+        out_ref[:, pl.ds(pl.multiple_of(p * 128, 128), 128)] = folded(acc_ref, p, left)
+        return carry
+
+    lax.fori_loop(0, BLOCKS // 2, one, 0)
+
+
+def last_kernel(
+    words_ref, lists_ref, totals_ref, partner_ref, table_ref, prior_hbm, alpha_hbm, out_hbm,
+    x_ref, acc_ref, prior_ref, alpha_ref, out_ref, sems, out_sems,
 ):
-    own_copy = pltpu.make_async_copy(own_hbm, x_ref.at[0:96], sems.at[0])
-    partner_copy = pltpu.make_async_copy(partner_hbm, partner_ref, sems.at[1])
-    alpha_copy = pltpu.make_async_copy(alpha_hbm, alpha_ref, sems.at[2])
-    table_copy = pltpu.make_async_copy(table_hbm, table_ref, sems.at[3])
-    partner_copy.start()
-    own_copy.start()
-    table_copy.start()
+    prior_copy = pltpu.make_async_copy(prior_hbm, prior_ref, sems.at[0])
+    alpha_copy = pltpu.make_async_copy(alpha_hbm, alpha_ref, sems.at[1])
+    prior_copy.start()
     alpha_copy.start()
+    zero(acc_ref)
+    unpack(partner_ref, COLS - FIRST, x_ref)
+    accumulate(2, words_ref, lists_ref, totals_ref, x_ref, table_ref, acc_ref)
+    prior_copy.wait()
+    alpha_copy.wait()
     left = left_half((CAP, 128))
-    partner_copy.wait()
-    unpack(partner_ref, x_ref, 96)
-    own_copy.wait()
-    table_copy.wait()
-    alpha_copy.wait()
-
-    def block(m):
-        lhs, rhs = [], []
-        for k in range(12):
-            lhs.append(x_ref[blocks_ref[k, m]])
-            w = table_ref[types_ref[k, m]]
-            rhs += [w, w]
-        both = jnp.dot(jnp.concatenate(lhs, 1), jnp.concatenate(rhs, 0), preferred_element_type=f32)
-        return both + swap(both)
 
     def triple(u, carry):
         a_main, a_low = alpha_ref[2 * u, 0:CAP, :], alpha_ref[2 * u, CAP:PACK, :]
@@ -161,10 +237,9 @@
             jnp.where(left, jnp.concatenate([a_low, swap(a_low)], 0), b_main_r),
             jnp.where(left, b_main_r, jnp.concatenate([swap(b_low), b_low], 0)),
         )
-        for q in range(3):
-            pair = jnp.where(left, block(6 * u + 2 * q), block(6 * u + 2 * q + 1))
-            col = pl.multiple_of(u * 384 + 128 * q, 128)
-            out_ref[:, pl.ds(col, 128)] = alphas[q] + pair
+        for n in range(3):
+            col = pl.ds(pl.multiple_of(u * 384 + 128 * n, 128), 128)
+            out_ref[:, col] = alphas[n] + (prior_ref[:, col] + folded(acc_ref, 3 * u + n, left))
         return carry
 
     copies = []
@@ -219,33 +294,70 @@
         ],
         name="alpha_slots",
     )(row_counts, alpha_blocks, alpha_types, coeffs_t, split_table(alpha_table))
+    words, lists, totals = pl.pallas_call(
+        plan_kernel,
+        in_specs=[vmem(), vmem()],
+        out_specs=[vmem(), smem(), smem()],
+        out_shape=[
+            jax.ShapeDtypeStruct((3, 16, 128), jnp.int32),
+            jax.ShapeDtypeStruct((3, LIST), jnp.int32),
+            jax.ShapeDtypeStruct((3,), jnp.int32),
+        ],
+        scratch_shapes=[
+            pltpu.VMEM((16, 128), jnp.int32),
+            pltpu.VMEM((8, 128), jnp.int32),
+            pltpu.SMEM((8, 128), jnp.int32),
+            pltpu.SemaphoreType.DMA,
+        ],
+        name="beta_plan",
+    )(beta_blocks.T, beta_types.T)
+    tiles = split_table(beta_table)
     own = lax.all_to_all(coeff_slots, "col", split_axis=0, concat_axis=0, tiled=True)
-    own, alpha_slots = lax.optimization_barrier((own, alpha_slots))
-    partner = lax.ppermute(own, "cls", [(i, i ^ 1) for i in range(8)])
+    own, alpha_slots, tiles, words, lists, totals = lax.optimization_barrier(
+        (own, alpha_slots, tiles, words, lists, totals)
+    )
+    route = [(i, i ^ 1) for i in range(8)]
+    partner_first = lax.ppermute(own[:FIRST], "cls", route)
     alpha = lax.all_to_all(alpha_slots, "col", split_axis=0, concat_axis=0, tiled=True)
-    own_x = pl.pallas_call(
+    acc_shape = (BLOCKS + 1, CAP, 128)
+    acc = pl.pallas_call(
         own_kernel,
-        in_specs=[vmem()],
+        in_specs=[smem(), smem(), smem(), vmem(), vmem()],
         out_specs=vmem(),
-        out_shape=jax.ShapeDtypeStruct((96, CAP, 128), bf16),
-        name="own_split",
-    )(own)
+        out_shape=jax.ShapeDtypeStruct(acc_shape, f32),
+        scratch_shapes=[pltpu.VMEM((3 * COLS + 1, CAP, 128), bf16)],
+        name="beta_own",
+    )(words, lists, totals, own, tiles)
+    rest, acc = lax.optimization_barrier((own[FIRST:], acc))
+    partner_last = lax.ppermute(rest, "cls", route)
+    prior = pl.pallas_call(
+        first_kernel,
+        in_specs=[smem(), smem(), smem(), vmem(), vmem(), hbm()],
+        out_specs=vmem(),
+        out_shape=jax.ShapeDtypeStruct((CAP, BLOCKS * BLK), f32),
+        scratch_shapes=[
+            pltpu.VMEM((3 * FIRST + 1, CAP, 128), bf16),
+            pltpu.VMEM(acc_shape, f32),
+            pltpu.SemaphoreType.DMA,
+        ],
+        name="beta_first",
+    )(words, lists, totals, partner_first, tiles, acc)
     return pl.pallas_call(
-        beta_kernel,
-        in_specs=[smem(), smem(), hbm(), hbm(), hbm(), hbm()],
+        last_kernel,
+        in_specs=[smem(), smem(), smem(), vmem(), vmem(), hbm(), hbm()],
         out_specs=hbm(),
-        out_shape=jax.ShapeDtypeStruct((CAP, 96 * BLK), f32),
+        out_shape=jax.ShapeDtypeStruct((CAP, BLOCKS * BLK), f32),
         scratch_shapes=[
-            pltpu.VMEM((192, CAP, 128), bf16),
+            pltpu.VMEM((3 * (COLS - FIRST) + 1, CAP, 128), bf16),
+            pltpu.VMEM(acc_shape, f32),
+            pltpu.VMEM((CAP, BLOCKS * BLK), f32),
             pltpu.VMEM((COLS, PACK, 128), f32),
-            pltpu.VMEM((COLS, PACK, 128), f32),
-            pltpu.VMEM((64, BLK, 128), bf16),
-            pltpu.VMEM((CAP, 96 * BLK), f32),
+            pltpu.VMEM((CAP, BLOCKS * BLK), f32),
+            pltpu.SemaphoreType.DMA((2,)),
             pltpu.SemaphoreType.DMA((4,)),
-            pltpu.SemaphoreType.DMA((4,)),
-        ],
-        name="beta_sum",
-    )(beta_blocks.T, beta_types.T, own_x, partner, alpha, split_table(beta_table))
+        ],
+        name="beta_last",
+    )(words, lists, totals, partner_last, tiles, prior, alpha)
 
 
 def solution(mesh):

time: 72.4 us -> 86.8 us (1.20)
  Pallas kernels: 29.3 us -> 49.3 us
  waiting for transfers between devices: 19.1 us -> 6.56 us
  starting transfers between devices: 15.1 us -> 17.7 us
  local copies, waits for them, and re-layouts: 4.01 us -> 6.01 us
  other arithmetic: 4.35 us -> 5.92 us
    pallas_call x2 -> x4, Pallas kernels: 19.1 us -> 38.9 us  [the longest x1 11.8 us: on_device(): pl.pallas_call(first_kernel, in_specs=[smem(), smem(), smem(), vmem(), vm...]
    all_to_all x1, waiting for transfers between devices: 9.58 us -> 0.01 us  [on_device(): lax.all_to_all(alpha_slots, 'col', split_axis=0, concat_axis=0, tiled=True)]
    all_to_all x1, waiting for transfers between devices: 7.22 us -> 0.01 us  [on_device(): lax.all_to_all(coeff_slots, 'col', split_axis=0, concat_axis=0, tiled=True)]
    ppermute x1 -> x2, waiting for transfers between devices: 2.32 us -> 6.56 us  [the longest x1 6.55 us: on_device(): partner_first = lax.ppermute(own[:FIRST], 'cls', route)]
    all_to_all x1, starting transfers between devices: 4.92 us -> 7.38 us  [on_device(): lax.all_to_all(alpha_slots, 'col', split_axis=0, concat_axis=0, tiled=True)]
    unnamed x2 -> x8, local copies, waits for them, and re-layouts: 0.01 us -> 1.77 us
    another operation x2, other arithmetic: 1.15 us -> 2.74 us
  transfers between devices with their start and end apart: 3 -> 4, of which waited for: 3 -> 1; matrix products, arithmetic and copies ran while one was open for 12% -> 12% of each run, Pallas kernels for 17% -> 45%
where the time goes in v4:
time: 86.8 us; the launch traced here: 85.6 us
  Pallas kernels  49.3 us (57%)
  starting transfers between devices  17.7 us (20%)
  waiting for transfers between devices  6.56 us (8%)
  local copies, waits for them, and re-layouts  6.01 us (7%)
  other arithmetic  5.92 us (7%)
    pallas_call x1, Pallas kernels, on_device(): pl.pallas_call(first_kernel, in_specs=[smem(), smem(), smem(), vmem(), vm...  11.8 us
    pallas_call x1, Pallas kernels, on_device(): pl.pallas_call(own_kernel, in_specs=[smem(), smem(), smem(), vmem(), vmem...  11.6 us
    all_to_all x1, starting transfers between devices, on_device(): lax.all_to_all(coeff_slots, 'col', split_axis=0, concat_axis=0, tiled=True)  8.58 us
    pallas_call x1, Pallas kernels, on_device(): pl.pallas_call(plan_kernel, in_specs=[vmem(), vmem()], out_specs=[vmem(),...  8 us
    pallas_call x1, Pallas kernels, on_device(): pl.pallas_call(last_kernel, in_specs=[smem(), smem(), smem(), vmem(), vme...  7.51 us
    all_to_all x1, starting transfers between devices, on_device(): lax.all_to_all(alpha_slots, 'col', split_axis=0, concat_axis=0, tiled=True)  7.38 us
    pallas_call x1, Pallas kernels, on_device(): pl.pallas_call(alpha_kernel, in_specs=[smem(), smem(), smem(), vmem(), vm...  7.14 us
    ppermute x1, waiting for transfers between devices, on_device(): partner_first = lax.ppermute(own[:FIRST], 'cls', route)  6.55 us
  transfers between devices with their start and end apart: 4, of which 1 were waited for; matrix products, arithmetic and copies ran while one was open for 12% of the time, Pallas kernels for 45%

profile of v4, /device:TPU:1, one launch (start us, length us, event | category | flops | bytes accessed | tf_op | source)
XLA Modules:
  0.0 85.6 jit_solution(12562544561469619171)
XLA Ops:
  0.0 0.0 copy-start.2
  0.0 3.2 %coeff_slots.1 = f32[32,72,128]{2,1,0:T(8,128)} custom-call(s32[32]{0:T(128)} %counts_ref.3, f32[192,1024]{1,0:T(8,128)} %x_ref.3), custom_call_target="tpu_custom_call" | custom-call | tf_op jit(solution)/shard_map/coeff_slots/pallas_call | solution.py:276
  3.2 8.6 %all-to-all-start = ((f32[32,72,128]{2,1,0:T(8,128)}), f32[32,72,128]{2,1,0:T(8,128)S(1)}, u32[]{:S(2)}, u32[]{:S(2)}) async-start(f32[32,72,128]{2,1,0:T(8,128)} %coeff_slots.1), calls=%async_computation | async-start | bytes 2359296 | tf_op jit(solution)/shard_map/all_to_all | solution.py:315
  11.8 0.0 copy-done.2
  11.8 2.2 %reshape.6 = f32[64,64,64]{2,1,0:T(8,128)} reshape(f32[64,4096]{1,0:T(8,128)S(1)} %copy-done.2) | data formatting | bytes 2097152 | tf_op jit(solution)/shard_map/reshape | solution.py:269
  13.9 2.0 %reshape.7 = f32[64,64,64]{2,1,0:T(8,128)S(1)} reshape(f32[64,4096]{1,0:T(8,128)} %param.12) | data formatting | bytes 2097152 | tf_op jit(solution)/shard_map/reshape | solution.py:269
  16.0 8.0 %beta_plan.1 = (s32[3,16,128]{2,1,0:T(8,128)}, s32[3,640]{1,0:T(4,128)}, s32[3]{0:T(128)}) custom-call(s32[12,96]{1,0:T(8,128)} %bitcast.2, s32[12,96]{1,0:T(8,128)} %bitcast.3), custom_call_target="tpu_custom_call" | custom-call | tf_op jit(solution)/shard_map/beta_plan/pallas_call | solution.py:297
  24.0 2.2 %reduce-precision_convert_fusion.1 = (bf16[64,64,64]{2,1,0:T(8,128)(2,1)S(1)}, bf16[64,64,64]{2,1,0:T(8,128)(2,1)S(1)}) fusion(f32[64,64,64]{2,1,0:T(8,128)} %reshape.6), kind=kLoop, calls=%fused_computation.3 | loop fusion | flops 1048576 | bytes 2097152 | tf_op jit(solution)/shard_map/convert.2
  26.1 1.6 %pad_maximum_fusion.table_ref = bf16[64,64,128]{2,1,0:T(8,128)(2,1)} fusion(bf16[64,64,64]{2,1,0:T(8,128)(2,1)S(1)} %get-tuple-element.30, bf16[64,64,64]{2,1,0:T(8,128)(2,1)S(1)} %get-tuple-element.29), kind=kLoop, calls=%fused_computation.6 | loop fusion | flops 2097152 | bytes 2097152 | tf_op jit(solution)/shard_map/concatenate | solution.py:271
  27.7 7.1 %alpha_slots.1 = f32[32,72,128]{2,1,0:T(8,128)} custom-call(s32[32]{0:T(128)} %counts_ref.3, s32[16,16]{1,0:T(8,128)} %blocks_ref.1, s32[16,16]{1,0:T(8,128)} %types_ref.1, f32[192,1024]{1,0:T(8,128)} %x_ref.3, bf16[64,64,128]{2,1,0:T(8,128)(2,1)} %pad_maximum_fusion.table_ref), custom_call_target="tpu_custom_call" | custom-call | tf_op jit(solution)/shard_map/alpha_slots/pallas_call | solution.py:284
  34.8 0.6 reduce-precision_convert_fusion
  35.4 1.6 %pad_maximum_fusion.1.table_ref = bf16[64,64,128]{2,1,0:T(8,128)(2,1)} fusion(bf16[64,64,64]{2,1,0:T(8,128)(2,1)S(1)} %get-tuple-element.28, bf16[64,64,64]{2,1,0:T(8,128)(2,1)S(1)} %get-tuple-element.27), kind=kLoop, calls=%fused_computation.7 | loop fusion | flops 2097152 | bytes 2097152 | tf_op jit(solution)/shard_map/concatenate | solution.py:271
  37.0 0.0 all-to-all-done.own_ref
  37.0 0.0 copy-start
  37.0 7.4 %all-to-all-start.1 = ((f32[32,72,128]{2,1,0:T(8,128)}), f32[32,72,128]{2,1,0:T(8,128)S(1)}, u32[]{:S(2)}, u32[]{:S(2)}) async-start(f32[32,72,128]{2,1,0:T(8,128)} %alpha_slots.1), calls=%async_computation.1 | async-start | bytes 2359296 | tf_op jit(solution)/shard_map/all_to_all | solution.py:321
  44.4 0.1 slice.7
  44.5 1.7 %collective-permute-start.1 = (f32[22,72,128]{2,1,0:T(8,128)S(1)}, f32[22,72,128]{2,1,0:T(8,128)}, u32[]{:S(2)}, u32[]{:S(2)}) collective-permute-start(f32[22,72,128]{2,1,0:T(8,128)S(1)} %slice.7), channel_id=1, source_target_pairs={{0,32},{32,0},{64,96},{96,64},{128,160},{160,128},{192,224},{224,1... | collective-permute-start | bytes 2433032 | tf_op jit(solution)/shard_map/ppermute | solution.py:320
  46.2 0.0 copy-done
  46.3 11.6 %beta_own.1.prior_hbm = f32[97,48,128]{2,1,0:T(8,128)} custom-call(s32[3,16,128]{2,1,0:T(8,128)} %get-tuple-element.19.words_ref, s32[3,640]{1,0:T(4,128)} %get-tuple-element.20.lists_ref, s32[3]{0:T(128)} %get-tuple-element.21.totals_ref, f32[32,72,128]{2,1,0:T(8,128)} %copy-done, bf16[64,64,128]{2,1,0:T(8,128)(2,1)} %pad_maximum_fusion.1.table_ref), custom_call_target="tpu_custom_call" | custom-call | tf_op jit(solution)/shard_map/beta_own/pallas_call | solution.py:323
  57.9 0.0 collective-permute-start
  57.9 6.6 %collective-permute-done.1.partner_ref = f32[22,72,128]{2,1,0:T(8,128)} collective-permute-done((f32[22,72,128]{2,1,0:T(8,128)S(1)}, f32[22,72,128]{2,1,0:T(8,128)}, u32[]{:S(2)}, u32[]{:S(2)}) %collective-permute-start.1) | collective-permute-done | bytes 811040 | tf_op jit(solution)/shard_map/ppermute | solution.py:320
  64.4 11.8 %beta_first.1.prior_hbm = f32[48,6144]{1,0:T(8,128)} custom-call(s32[3,16,128]{2,1,0:T(8,128)} %get-tuple-element.19.words_ref, s32[3,640]{1,0:T(4,128)} %get-tuple-element.20.lists_ref, s32[3]{0:T(128)} %get-tuple-element.21.totals_ref, f32[22,72,128]{2,1,0:T(8,128)} %collective-permute-done.1.partner_ref, ...), custom_call_target="tpu_custom_call" | custom-call | tf_op jit(solution)/shard_map/beta_first/pallas_call | solution.py:333
  76.3 0.0 collective-permute-done.partner_ref
  76.3 0.0 copy-start.3
  76.3 0.0 all-to-all-done.1.alpha_hbm
  76.3 0.7 copy-done.3
  77.0 0.0 copy-start.1
  77.0 1.0 %copy-done.1 = f32[32,72,128]{2,1,0:T(8,128)} copy-done((f32[32,72,128]{2,1,0:T(8,128)}, f32[32,72,128]{2,1,0:T(8,128)S(1)}, u32[]{:S(2)}) %copy-start.1) | copy-done | bytes 1179672
  78.0 7.5 %beta_last.1 = f32[48,6144]{1,0:T(8,128)} custom-call(s32[3,16,128]{2,1,0:T(8,128)} %get-tuple-element.19.words_ref, s32[3,640]{1,0:T(4,128)} %get-tuple-element.20.lists_ref, s32[3]{0:T(128)} %get-tuple-element.21.totals_ref, f32[10,72,128]{2,1,0:T(8,128)} %copy-done.3, bf16[64,64,128]{2,1,0:T(8,128)(2,1)} %pad_maximum_fusion.1.table_ref, ...), custom_call_target="tpu_custom_call" | custom-call | tf_op jit(solution)/shard_map/beta_last/pallas_call | solution.py:345
  (1 shorter events, 0.0 us)
Async XLA Ops:
  0.0 11.8 %copy-start.2 = (f32[64,4096]{1,0:T(8,128)S(1)}, f32[64,4096]{1,0:T(8,128)}, u32[]{:S(2)}) copy-start(f32[64,4096]{1,0:T(8,128)} %param.9) | copy-start | bytes 3145732
  3.2 33.9 %all-to-all-start = ((f32[32,72,128]{2,1,0:T(8,128)}), f32[32,72,128]{2,1,0:T(8,128)S(1)}, u32[]{:S(2)}, u32[]{:S(2)}) async-start(f32[32,72,128]{2,1,0:T(8,128)} %coeff_slots.1), calls=%async_computation | async-start | bytes 2359296 | tf_op jit(solution)/shard_map/all_to_all | solution.py:315
  37.0 9.2 %copy-start = (f32[32,72,128]{2,1,0:T(8,128)}, f32[32,72,128]{2,1,0:T(8,128)S(1)}, u32[]{:S(2)}) copy-start(f32[32,72,128]{2,1,0:T(8,128)S(1)} %all-to-all-done.own_ref) | copy-start | bytes 3538948
  37.0 39.2 %all-to-all-start.1 = ((f32[32,72,128]{2,1,0:T(8,128)}), f32[32,72,128]{2,1,0:T(8,128)S(1)}, u32[]{:S(2)}, u32[]{:S(2)}) async-start(f32[32,72,128]{2,1,0:T(8,128)} %alpha_slots.1), calls=%async_computation.1 | async-start | bytes 2359296 | tf_op jit(solution)/shard_map/all_to_all | solution.py:321
  44.5 19.9 %collective-permute-start.1 = (f32[22,72,128]{2,1,0:T(8,128)S(1)}, f32[22,72,128]{2,1,0:T(8,128)}, u32[]{:S(2)}, u32[]{:S(2)}) collective-permute-start(f32[22,72,128]{2,1,0:T(8,128)S(1)} %slice.7), channel_id=1, source_target_pairs={{0,32},{32,0},{64,96},{96,64},{128,160},{160,128},{192,224},{224,1... | collective-permute-start | bytes 2433032 | tf_op jit(solution)/shard_map/ppermute | solution.py:320
  57.9 18.4 %collective-permute-start = (f32[10,72,128]{2,1,0:T(8,128)S(1)}, f32[10,72,128]{2,1,0:T(8,128)S(1)}, u32[]{:S(2)}, u32[]{:S(2)}) collective-permute-start(f32[10,72,128]{2,1,0:T(8,128)S(1)} %slice.6), channel_id=1, source_target_pairs={{0,32},{32,0},{64,96},{96,64},{128,160},{160,128},{192,224},{224,1... | collective-permute-start | bytes 1105928 | tf_op jit(solution)/shard_map/ppermute | solution.py:332
  76.3 0.7 copy-start.3
  77.0 1.0 %copy-start.1 = (f32[32,72,128]{2,1,0:T(8,128)}, f32[32,72,128]{2,1,0:T(8,128)S(1)}, u32[]{:S(2)}) copy-start(f32[32,72,128]{2,1,0:T(8,128)S(1)} %all-to-all-done.1.alpha_hbm) | copy-start | bytes 3538948

commit v5 on v4

--- a/solution.py
+++ b/solution.py
@@ -16,10 +16,11 @@
 PACK = CAP + HALF
 BLOCKS = 96
 DEPTH = 12
-FIRST = 22
+FIRST = 24
 BOUNDS = (0, BLOCKS, BLOCKS + 3 * FIRST, 2 * BLOCKS)
 UNROLL = 32
-LIST = 640
+GROUP = 4
+LIST = 384
 ROWS = NA + CAP + 8
 
 
@@ -102,25 +103,27 @@
     return pltpu.roll(x, BLK, 1)
 
 
-def unpack(ref, senders, x_ref):
+def unpack(ref, senders, z_ref):
     left = left_half((CAP, 128))
     left_low = left_half((HALF, 128))
 
     def one(j, carry):
         main = ref[j, 0:CAP, :]
         low = ref[j, CAP:PACK, :]
-        main_lo = main - main.astype(bf16).astype(f32)
-        low_lo = low - low.astype(bf16).astype(f32)
-        main_r, low_r, main_lo_r, low_lo_r = swap(main), swap(low), swap(main_lo), swap(low_lo)
-        x_ref[3 * j] = jnp.where(left, main, main_lo_r).astype(bf16)
-        x_ref[3 * j + 1] = jnp.where(left, main_r, main_lo).astype(bf16)
-        x_ref[3 * j + 2] = jnp.concatenate(
-            [jnp.where(left_low, low, low_lo_r), jnp.where(left_low, low_r, low_lo)], 0
-        ).astype(bf16)
+        main_r = swap(main)
+        low_r = swap(low)
+        parts = (
+            jnp.where(left, main, main_r),
+            jnp.where(left, main_r, main),
+            jnp.concatenate([jnp.where(left_low, low, low_r), jnp.where(left_low, low_r, low)], 0),
+        )
+        for n in range(3):
+            hi, lo = split(parts[n])
+            z_ref[3 * j + n] = jnp.concatenate([hi, lo], 1)
         return carry
 
     lax.fori_loop(0, senders, one, 0)
-    x_ref[3 * senders] = jnp.zeros((CAP, 128), bf16)
+    z_ref[3 * senders] = jnp.zeros((CAP, 256), bf16)
 
 
 def plan_kernel(blocks_ref, types_ref, words_ref, lists_ref, totals_ref, entry_ref, counts_ref, smem_ref, sem):
@@ -142,37 +145,46 @@
             here = (row == rank) & (held[k:k + 1] > 0)
             ordered = jnp.where(here, word[k:k + 1], ordered)
             rank = rank + held[k:k + 1]
-        words_ref[q] = ordered
-        counts_ref[q:q + 1, :] = (rank + 1) >> 1
+        words_ref[16 * q:16 * q + 16, :] = ordered
+        counts_ref[q:q + 1, :] = (rank + GROUP - 1) // GROUP
     copy = pltpu.make_async_copy(counts_ref, smem_ref, sem)
     copy.start()
     copy.wait()
+
+    def add(m, ends):
+        ends = list(ends)
+        for q in range(3):
+            for i in range(DEPTH // GROUP):
+                lists_ref[ends[q] + i] = m * 4 + i
+            ends[q] = ends[q] + smem_ref[q, m]
+        return tuple(ends)
+
+    ends = lax.fori_loop(0, BLOCKS, add, tuple(jnp.int32(LIST * q) for q in range(3)), unroll=4)
     for q in range(3):
-
-        def add(m, at):
-            for i in range(DEPTH // 2):
-                lists_ref[q, at + i] = m * 8 + i
-            return at + smem_ref[q, m]
-
-        end = lax.fori_loop(0, BLOCKS, add, jnp.int32(0))
         for i in range(UNROLL):
-            lists_ref[q, end + i] = BLOCKS * 8
-        totals_ref[q] = (end + UNROLL - 1) // UNROLL
-
-
-def accumulate(q, words_ref, lists_ref, totals_ref, x_ref, table_ref, acc_ref):
+            lists_ref[ends[q] + i] = BLOCKS * 4
+        totals_ref[q] = (ends[q] - LIST * q + UNROLL - 1) // UNROLL
+
+
+def accumulate(q, words_ref, lists_ref, totals_ref, z_ref, table_ref, acc_ref):
+    pick = left_half((CAP, 256)) | (lax.broadcasted_iota(jnp.int32, (CAP, 256), 1) // BLK == 2)
+
     def batch(n, carry):
-        for i in range(UNROLL):
-            item = lists_ref[q, n * UNROLL + i]
-            m = item >> 3
-            pair = (item & 7) * 2
-            w0 = words_ref[q, pair, m]
-            w1 = words_ref[q, pair + 1, m]
-            t0 = table_ref[w0 >> 8]
-            t1 = table_ref[w1 >> 8]
-            lhs = jnp.concatenate([x_ref[w0 & 255], x_ref[w1 & 255]], 1)
-            rhs = jnp.concatenate([t0, t0, t1, t1], 0)
-            acc_ref[m] = acc_ref[m] + jnp.dot(lhs, rhs, preferred_element_type=f32)
+        for g in range(UNROLL):
+            item = lists_ref[LIST * q + n * UNROLL + g]
+            m = item >> 2
+            at = 2048 * q + (item & 3) * 512 + m
+            hi, lo, w = [], [], []
+            for i in range(0, GROUP, 2):
+                w0 = words_ref[at + 128 * i]
+                w1 = words_ref[at + 128 * i + 128]
+                pair = jnp.where(pick, z_ref[w0 & 255], z_ref[w1 & 255])
+                hi.append(pair[:, 0:128])
+                lo.append(pair[:, 128:256])
+                w += [table_ref[w0 >> 8], table_ref[w1 >> 8]]
+            lhs = jnp.concatenate([jnp.concatenate(hi, 1), jnp.concatenate(lo, 1)], 0)
+            both = jnp.dot(lhs, jnp.concatenate(w, 0), preferred_element_type=f32)
+            acc_ref[m] = acc_ref[m] + (both[0:CAP] + both[CAP:])
         return carry
 
     lax.fori_loop(0, totals_ref[q], batch, 0)
@@ -262,7 +274,7 @@
 
 
 def hbm():
-    return pl.BlockSpec(memory_space=pl.ANY)
+    return pl.BlockSpec(memory_space=pltpu.HBM)
 
 
 def split_table(table):
@@ -299,8 +311,8 @@
         in_specs=[vmem(), vmem()],
         out_specs=[vmem(), smem(), smem()],
         out_shape=[
-            jax.ShapeDtypeStruct((3, 16, 128), jnp.int32),
-            jax.ShapeDtypeStruct((3, LIST), jnp.int32),
+            jax.ShapeDtypeStruct((48, 128), jnp.int32),
+            jax.ShapeDtypeStruct((3 * LIST,), jnp.int32),
             jax.ShapeDtypeStruct((3,), jnp.int32),
         ],
         scratch_shapes=[
@@ -311,6 +323,7 @@
         ],
         name="beta_plan",
     )(beta_blocks.T, beta_types.T)
+    words = words.reshape(-1)
     tiles = split_table(beta_table)
     own = lax.all_to_all(coeff_slots, "col", split_axis=0, concat_axis=0, tiled=True)
     own, alpha_slots, tiles, words, lists, totals = lax.optimization_barrier(
@@ -325,7 +338,7 @@
         in_specs=[smem(), smem(), smem(), vmem(), vmem()],
         out_specs=vmem(),
         out_shape=jax.ShapeDtypeStruct(acc_shape, f32),
-        scratch_shapes=[pltpu.VMEM((3 * COLS + 1, CAP, 128), bf16)],
+        scratch_shapes=[pltpu.VMEM((3 * COLS + 1, CAP, 256), bf16)],
         name="beta_own",
     )(words, lists, totals, own, tiles)
     rest, acc = lax.optimization_barrier((own[FIRST:], acc))
@@ -336,7 +349,7 @@
         out_specs=vmem(),
         out_shape=jax.ShapeDtypeStruct((CAP, BLOCKS * BLK), f32),
         scratch_shapes=[
-            pltpu.VMEM((3 * FIRST + 1, CAP, 128), bf16),
+            pltpu.VMEM((3 * FIRST + 1, CAP, 256), bf16),
             pltpu.VMEM(acc_shape, f32),
             pltpu.SemaphoreType.DMA,
         ],
@@ -348,7 +361,7 @@
         out_specs=hbm(),
         out_shape=jax.ShapeDtypeStruct((CAP, BLOCKS * BLK), f32),
         scratch_shapes=[
-            pltpu.VMEM((3 * (COLS - FIRST) + 1, CAP, 128), bf16),
+            pltpu.VMEM((3 * (COLS - FIRST) + 1, CAP, 256), bf16),
             pltpu.VMEM(acc_shape, f32),
             pltpu.VMEM((CAP, BLOCKS * BLK), f32),
             pltpu.VMEM((COLS, PACK, 128), f32),

time: 86.8 us -> 82.5 us (0.950)
  Pallas kernels: 49.3 us -> 42.6 us
  waiting for transfers between devices: 6.56 us -> 9.39 us
    pallas_call x1, Pallas kernels: 8 us -> 3.05 us  [on_device(): pl.pallas_call(plan_kernel, in_specs=[vmem(), vmem()], out_specs=[vmem(),...]
    ppermute x1, waiting for transfers between devices: 6.55 us -> 9.39 us  [on_device(): partner_first = lax.ppermute(own[:FIRST], 'cls', route)]
    pallas_call x1, Pallas kernels: 11.6 us -> 10.4 us  [on_device(): pl.pallas_call(own_kernel, in_specs=[smem(), smem(), smem(), vmem(), vmem...]
  transfers between devices with their start and end apart: 4 -> 4, of which waited for: 1 -> 1; matrix products, arithmetic and copies ran while one was open for 12% -> 12% of each run, Pallas kernels for 45% -> 39%
where the time goes in v5:
time: 82.5 us; the launch traced here: 81.7 us
  Pallas kernels  42.6 us (52%)
  starting transfers between devices  17.7 us (21%)
  waiting for transfers between devices  9.39 us (11%)
  local copies, waits for them, and re-layouts  5.98 us (7%)
  other arithmetic  5.92 us (7%)
    pallas_call x1, Pallas kernels, on_device(): pl.pallas_call(first_kernel, in_specs=[smem(), smem(), smem(), vmem(), vm...  11.7 us
    pallas_call x1, Pallas kernels, on_device(): pl.pallas_call(own_kernel, in_specs=[smem(), smem(), smem(), vmem(), vmem...  10.4 us
    ppermute x1, waiting for transfers between devices, on_device(): partner_first = lax.ppermute(own[:FIRST], 'cls', route)  9.39 us
    all_to_all x1, starting transfers between devices, on_device(): lax.all_to_all(coeff_slots, 'col', split_axis=0, concat_axis=0, tiled=True)  8.58 us
    all_to_all x1, starting transfers between devices, on_device(): lax.all_to_all(alpha_slots, 'col', split_axis=0, concat_axis=0, tiled=True)  7.38 us
    pallas_call x1, Pallas kernels, on_device(): pl.pallas_call(last_kernel, in_specs=[smem(), smem(), smem(), vmem(), vme...  7.2 us
    pallas_call x1, Pallas kernels, on_device(): pl.pallas_call(alpha_kernel, in_specs=[smem(), smem(), smem(), vmem(), vm...  7.14 us
    reshape x2, local copies, waits for them, and re-layouts, split_table(): tiles = table.reshape(table.shape[0], BLK, BLK)  4.17 us
  transfers between devices with their start and end apart: 4, of which 1 were waited for; matrix products, arithmetic and copies ran while one was open for 12% of the time, Pallas kernels for 39%

profile of v5, /device:TPU:1, one launch (start us, length us, event | category | flops | bytes accessed | tf_op | source)
XLA Modules:
  0.0 81.7 jit_solution(9479907282337853976)
XLA Ops:
  0.0 0.0 copy-start.2
  0.0 3.2 %coeff_slots.1 = f32[32,72,128]{2,1,0:T(8,128)} custom-call(s32[32]{0:T(128)} %counts_ref.3, f32[192,1024]{1,0:T(8,128)} %x_ref.3), custom_call_target="tpu_custom_call" | custom-call | tf_op jit(solution)/shard_map/coeff_slots/pallas_call | solution.py:288
  3.2 8.6 %all-to-all-start = ((f32[32,72,128]{2,1,0:T(8,128)}), f32[32,72,128]{2,1,0:T(8,128)S(1)}, u32[]{:S(2)}, u32[]{:S(2)}) async-start(f32[32,72,128]{2,1,0:T(8,128)} %coeff_slots.1), calls=%async_computation | async-start | bytes 2359296 | tf_op jit(solution)/shard_map/all_to_all | solution.py:328
  11.8 0.0 copy-done.2
  11.8 2.2 %reshape.9 = f32[64,64,64]{2,1,0:T(8,128)} reshape(f32[64,4096]{1,0:T(8,128)S(1)} %copy-done.2) | data formatting | bytes 2097152 | tf_op jit(solution)/shard_map/reshape | solution.py:281
  13.9 2.0 %reshape.10 = f32[64,64,64]{2,1,0:T(8,128)S(1)} reshape(f32[64,4096]{1,0:T(8,128)} %param.12) | data formatting | bytes 2097152 | tf_op jit(solution)/shard_map/reshape | solution.py:281
  16.0 3.0 %beta_plan.1 = (s32[48,128]{1,0:T(8,128)}, s32[1152]{0:T(1024)}, s32[3]{0:T(128)}) custom-call(s32[12,96]{1,0:T(8,128)} %bitcast.6, s32[12,96]{1,0:T(8,128)} %bitcast.7), custom_call_target="tpu_custom_call" | custom-call | tf_op jit(solution)/shard_map/beta_plan/pallas_call | solution.py:309
  19.0 2.2 %reduce-precision_convert_fusion.1 = (bf16[64,64,64]{2,1,0:T(8,128)(2,1)S(1)}, bf16[64,64,64]{2,1,0:T(8,128)(2,1)S(1)}) fusion(f32[64,64,64]{2,1,0:T(8,128)} %reshape.9), kind=kLoop, calls=%fused_computation.3 | loop fusion | flops 1048576 | bytes 2097152 | tf_op jit(solution)/shard_map/convert.2
  21.2 1.6 %pad_maximum_fusion.table_ref = bf16[64,64,128]{2,1,0:T(8,128)(2,1)} fusion(bf16[64,64,64]{2,1,0:T(8,128)(2,1)S(1)} %get-tuple-element.30, bf16[64,64,64]{2,1,0:T(8,128)(2,1)S(1)} %get-tuple-element.29), kind=kLoop, calls=%fused_computation.6 | loop fusion | flops 2097152 | bytes 2097152 | tf_op jit(solution)/shard_map/concatenate | solution.py:283
  22.8 7.1 %alpha_slots.1 = f32[32,72,128]{2,1,0:T(8,128)} custom-call(s32[32]{0:T(128)} %counts_ref.3, s32[16,16]{1,0:T(8,128)} %blocks_ref.1, s32[16,16]{1,0:T(8,128)} %types_ref.1, f32[192,1024]{1,0:T(8,128)} %x_ref.3, bf16[64,64,128]{2,1,0:T(8,128)(2,1)} %pad_maximum_fusion.table_ref), custom_call_target="tpu_custom_call" | custom-call | tf_op jit(solution)/shard_map/alpha_slots/pallas_call | solution.py:296
  29.9 0.6 reduce-precision_convert_fusion
  30.5 1.6 %pad_maximum_fusion.1.table_ref = bf16[64,64,128]{2,1,0:T(8,128)(2,1)} fusion(bf16[64,64,64]{2,1,0:T(8,128)(2,1)S(1)} %get-tuple-element.28, bf16[64,64,64]{2,1,0:T(8,128)(2,1)S(1)} %get-tuple-element.27), kind=kLoop, calls=%fused_computation.7 | loop fusion | flops 2097152 | bytes 2097152 | tf_op jit(solution)/shard_map/concatenate | solution.py:283
  32.1 0.0 all-to-all-done.own_ref
  32.1 0.0 copy-start
  32.1 7.4 %all-to-all-start.1 = ((f32[32,72,128]{2,1,0:T(8,128)}), f32[32,72,128]{2,1,0:T(8,128)S(1)}, u32[]{:S(2)}, u32[]{:S(2)}) async-start(f32[32,72,128]{2,1,0:T(8,128)} %alpha_slots.1), calls=%async_computation.1 | async-start | bytes 2359296 | tf_op jit(solution)/shard_map/all_to_all | solution.py:334
  39.5 0.1 slice.7
  39.5 1.7 %collective-permute-start.1 = (f32[24,72,128]{2,1,0:T(8,128)S(1)}, f32[24,72,128]{2,1,0:T(8,128)}, u32[]{:S(2)}, u32[]{:S(2)}) collective-permute-start(f32[24,72,128]{2,1,0:T(8,128)S(1)} %slice.7), channel_id=1, source_target_pairs={{0,32},{32,0},{64,96},{96,64},{128,160},{160,128},{192,224},{224,1... | collective-permute-start | bytes 2654216 | tf_op jit(solution)/shard_map/ppermute | solution.py:333
  41.3 0.0 copy-done
  41.3 10.4 %beta_own.1.prior_hbm = f32[97,48,128]{2,1,0:T(8,128)} custom-call(s32[6144]{0:T(1024)} %bitcast.3, s32[1152]{0:T(1024)} %get-tuple-element.20.lists_ref, s32[3]{0:T(128)} %get-tuple-element.21.totals_ref, f32[32,72,128]{2,1,0:T(8,128)} %copy-done, bf16[64,64,128]{2,1,0:T(8,128)(2,1)} %pad_maximum_fusion.1.table_ref), custom_call_target="tpu_custom_call" | custom-call | tf_op jit(solution)/shard_map/beta_own/pallas_call | solution.py:336
  51.7 0.0 collective-permute-start
  51.7 9.4 %collective-permute-done.1.partner_ref = f32[24,72,128]{2,1,0:T(8,128)} collective-permute-done((f32[24,72,128]{2,1,0:T(8,128)S(1)}, f32[24,72,128]{2,1,0:T(8,128)}, u32[]{:S(2)}, u32[]{:S(2)}) %collective-permute-start.1) | collective-permute-done | bytes 884768 | tf_op jit(solution)/shard_map/ppermute | solution.py:333
  61.1 11.7 %beta_first.1.prior_hbm = f32[48,6144]{1,0:T(8,128)} custom-call(s32[6144]{0:T(1024)} %bitcast.4, s32[1152]{0:T(1024)} %get-tuple-element.20.lists_ref, s32[3]{0:T(128)} %get-tuple-element.21.totals_ref, f32[24,72,128]{2,1,0:T(8,128)} %collective-permute-done.1.partner_ref, bf16[64,64,128]{2,1,0:T(8,128)(2,1)} %pad_maximum_fusion.1.table_ref, ...), custom_call_target="tpu_custom_call" | custom-call | tf_op jit(solution)/shard_map/beta_first/pallas_call | solution.py:346
  72.8 0.0 collective-permute-done.partner_ref
  72.8 0.0 copy-start.3
  72.8 0.0 all-to-all-done.1.alpha_hbm
  72.8 0.7 copy-done.3
  73.5 0.0 copy-start.1
  73.5 1.0 %copy-done.1 = f32[32,72,128]{2,1,0:T(8,128)} copy-done((f32[32,72,128]{2,1,0:T(8,128)}, f32[32,72,128]{2,1,0:T(8,128)S(1)}, u32[]{:S(2)}) %copy-start.1) | copy-done | bytes 1179672
  74.5 7.2 %beta_last.1 = f32[48,6144]{1,0:T(8,128)} custom-call(s32[6144]{0:T(1024)} %bitcast.5, s32[1152]{0:T(1024)} %get-tuple-element.20.lists_ref, s32[3]{0:T(128)} %get-tuple-element.21.totals_ref, f32[8,72,128]{2,1,0:T(8,128)} %copy-done.3, bf16[64,64,128]{2,1,0:T(8,128)(2,1)} %pad_maximum_fusion.1.table_ref, f32[48,6144]{1,0:T(8,128)} %beta_first.1.prior_hbm, ...), custom_call_target="tpu_custom_call" | custom-call | tf_op jit(solution)/shard_map/beta_last/pallas_call | solution.py:358
  (1 shorter events, 0.0 us)
Async XLA Ops:
  0.0 11.8 %copy-start.2 = (f32[64,4096]{1,0:T(8,128)S(1)}, f32[64,4096]{1,0:T(8,128)}, u32[]{:S(2)}) copy-start(f32[64,4096]{1,0:T(8,128)} %param.9) | copy-start | bytes 3145732
  3.2 28.9 %all-to-all-start = ((f32[32,72,128]{2,1,0:T(8,128)}), f32[32,72,128]{2,1,0:T(8,128)S(1)}, u32[]{:S(2)}, u32[]{:S(2)}) async-start(f32[32,72,128]{2,1,0:T(8,128)} %coeff_slots.1), calls=%async_computation | async-start | bytes 2359296 | tf_op jit(solution)/shard_map/all_to_all | solution.py:328
  32.1 9.2 %copy-start = (f32[32,72,128]{2,1,0:T(8,128)}, f32[32,72,128]{2,1,0:T(8,128)S(1)}, u32[]{:S(2)}) copy-start(f32[32,72,128]{2,1,0:T(8,128)S(1)} %all-to-all-done.own_ref) | copy-start | bytes 3538948
  32.1 40.7 %all-to-all-start.1 = ((f32[32,72,128]{2,1,0:T(8,128)}), f32[32,72,128]{2,1,0:T(8,128)S(1)}, u32[]{:S(2)}, u32[]{:S(2)}) async-start(f32[32,72,128]{2,1,0:T(8,128)} %alpha_slots.1), calls=%async_computation.1 | async-start | bytes 2359296 | tf_op jit(solution)/shard_map/all_to_all | solution.py:334
  39.5 21.5 %collective-permute-start.1 = (f32[24,72,128]{2,1,0:T(8,128)S(1)}, f32[24,72,128]{2,1,0:T(8,128)}, u32[]{:S(2)}, u32[]{:S(2)}) collective-permute-start(f32[24,72,128]{2,1,0:T(8,128)S(1)} %slice.7), channel_id=1, source_target_pairs={{0,32},{32,0},{64,96},{96,64},{128,160},{160,128},{192,224},{224,1... | collective-permute-start | bytes 2654216 | tf_op jit(solution)/shard_map/ppermute | solution.py:333
  51.7 21.1 %collective-permute-start = (f32[8,72,128]{2,1,0:T(8,128)S(1)}, f32[8,72,128]{2,1,0:T(8,128)S(1)}, u32[]{:S(2)}, u32[]{:S(2)}) collective-permute-start(f32[8,72,128]{2,1,0:T(8,128)S(1)} %slice.6), channel_id=1, source_target_pairs={{0,32},{32,0},{64,96},{96,64},{128,160},{160,128},{192,224},{224,1... | collective-permute-start | bytes 884744 | tf_op jit(solution)/shard_map/ppermute | solution.py:345
  72.8 0.7 copy-start.3
  73.5 1.0 %copy-start.1 = (f32[32,72,128]{2,1,0:T(8,128)}, f32[32,72,128]{2,1,0:T(8,128)S(1)}, u32[]{:S(2)}) copy-start(f32[32,72,128]{2,1,0:T(8,128)S(1)} %all-to-all-done.1.alpha_hbm) | copy-start | bytes 3538948

commit v6 on v3

v6 whole, which is shorter than its diff:
```python
import jax
import jax.numpy as jnp
from jax import lax
from jax.experimental import pallas as pl
from jax.experimental.pallas import tpu as pltpu
from jax.sharding import PartitionSpec as P

f32 = jnp.float32
bf16 = jnp.bfloat16

NA = 1024
BLK = 64
COLS = 32
CAP = 48
HALF = CAP // 2
PACK = CAP + HALF
BLOCKS = 96
DEPTH = 12
PARTS = ((0, 32, 0), (32, 16, 48))
SPLIT = 48
TRIP = 12
ROWS = NA + CAP + 8


def split(x):
    hi = x.astype(bf16)
    return hi, (x - hi.astype(f32)).astype(bf16)


def left_half(shape):
    return lax.broadcasted_iota(jnp.int32, shape, len(shape) - 1) < BLK


def load_transposed(x_ref, buf_ref):
    for c in range(NA // 128):
        cols = slice(128 * c, 128 * c + 128)
        last = x_ref[128:192, cols]
        buf_ref[cols, 0:128] = x_ref[0:128, cols].T
        buf_ref[cols, 128:256] = jnp.concatenate([last, last], 0).T


def write_slots(counts_ref, buf_ref, out_ref):
    buf_ref[NA:ROWS, :] = jnp.zeros((ROWS - NA, 256), f32)
    left = left_half((8, 128))
    sub = lax.broadcasted_iota(jnp.int32, (8, 256), 0)

    def one(j, start):
        count = counts_ref[j]
        base = pl.multiple_of((start // 8) * 8, 8)
        shift = 8 - (start - base)
        turned = [pltpu.roll(buf_ref[pl.ds(base + 8 * n, 8), :], shift & 7, 0) for n in range(CAP // 8 + 1)]
        main, third = [], []
        for n in range(CAP // 8):
            rows = jnp.where(sub < shift, turned[n], turned[n + 1])
            rows = jnp.where(sub < count - 8 * n, rows, 0.0)
            main.append(rows[:, 0:128])
            third.append(rows[:, 128:256])
        for part in range(2):
            first, size, at = PARTS[part]
            n0, n1 = first // 8, size // 8
            half = n1 // 2
            low = [jnp.where(left, third[n0 + n], third[n0 + half + n]) for n in range(half)]
            out_ref[j, at:at + size, :] = jnp.concatenate(main[n0:n0 + n1], 0)
            out_ref[j, at + size:at + size + size // 2, :] = jnp.concatenate(low, 0) if half > 1 else low[0]
        return start + count

    lax.fori_loop(0, COLS, one, jnp.int32(0))


def coeff_kernel(counts_ref, x_ref, out_ref, buf_ref):
    load_transposed(x_ref, buf_ref)
    write_slots(counts_ref, buf_ref, out_ref)


def alpha_kernel(counts_ref, blocks_ref, types_ref, x_ref, table_ref, out_ref, buf_ref, a_ref, hi_ref, lo_ref):
    load_transposed(x_ref, buf_ref)
    blocks = NA // BLK
    for b in range(blocks):
        hi, lo = split(buf_ref[BLK * b:BLK * b + BLK, :])
        for half in range(2):
            at = slice(128 * b + BLK * half, 128 * b + BLK * half + BLK)
            hi_ref[at, :] = hi
            lo_ref[at, :] = lo

    def place(i, carry):
        for k in range(blocks):
            col = pl.multiple_of(blocks_ref[i, k] * 128, 128)
            row = pl.multiple_of(i * BLK, BLK)
            a_ref[pl.ds(row, BLK), pl.ds(col, 128)] = table_ref[types_ref[i, k]]
        return carry

    lax.fori_loop(0, blocks, place, 0)
    for r in range(4):
        rows = slice(256 * r, 256 * r + 256)
        a = a_ref[rows, :]
        buf_ref[rows, :] = jnp.dot(a, hi_ref[...], preferred_element_type=f32) + jnp.dot(
            a, lo_ref[...], preferred_element_type=f32
        )
    write_slots(counts_ref, buf_ref, out_ref)


def swap(x):
    return pltpu.roll(x, BLK, 1)


def fields(ref, j, size, at):
    main = ref[j, at:at + size, :]
    low = ref[j, at + size:at + size + size // 2, :]
    return main, swap(main), low, swap(low)


def unpack(ref, size, at, z_ref, base):
    left = left_half((size, 128))
    left_low = left_half((size // 2, 128))

    def one(j, carry):
        main, main_r, low, low_r = fields(ref, j, size, at)
        parts = (
            jnp.where(left, main, main_r),
            jnp.where(left, main_r, main),
            jnp.concatenate([jnp.where(left_low, low, low_r), jnp.where(left_low, low_r, low)], 0),
        )
        for n in range(3):
            hi, lo = split(parts[n])
            z_ref[base + 3 * j + n] = jnp.concatenate([hi, lo], 1)
        return carry

    lax.fori_loop(0, COLS, one, 0, unroll=2)


def own_kernel(own_ref, za_ref, zb_ref):
    for (first, size, at), z_ref in zip(PARTS, (za_ref, zb_ref)):
        unpack(own_ref, size, at, z_ref, 0)


def product(blocks_ref, types_ref, z_ref, table_ref, size, store):
    pick = left_half((size, 256)) | (lax.broadcasted_iota(jnp.int32, (size, 256), 1) // BLK == 2)
    left = left_half((size, 128))

    def block(m):
        hi, lo, w = [], [], []
        for k in range(0, DEPTH, 2):
            pair = jnp.where(pick, z_ref[blocks_ref[k, m]], z_ref[blocks_ref[k + 1, m]])
            hi.append(pair[:, 0:128])
            lo.append(pair[:, 128:256])
            w.append(table_ref[types_ref[k, m]])
            w.append(table_ref[types_ref[k + 1, m]])
        lhs = jnp.concatenate([jnp.concatenate(hi, 1), jnp.concatenate(lo, 1)], 0)
        both = jnp.dot(lhs, jnp.concatenate(w, 0), preferred_element_type=f32)
        both = both[0:size] + both[size:]
        return both + swap(both)

    def trip(n, carry):
        for i in range(TRIP):
            p = n * TRIP + i
            col = pl.ds(pl.multiple_of(p * 128, 128), 128)
            store(col, jnp.where(left, block(2 * p), block(2 * p + 1)))
        return carry

    lax.fori_loop(0, BLOCKS // (2 * TRIP), trip, 0)


def first_kernel(blocks_ref, types_ref, own_hbm, partner_hbm, table_ref, out_ref, z_ref, partner_ref, sems):
    size = PARTS[0][1]
    own_copy = pltpu.make_async_copy(own_hbm, z_ref.at[0:BLOCKS], sems.at[0])
    partner_copy = pltpu.make_async_copy(partner_hbm, partner_ref, sems.at[1])
    partner_copy.start()
    own_copy.start()
    partner_copy.wait()
    unpack(partner_ref, size, 0, z_ref, BLOCKS)
    own_copy.wait()

    def store(col, value):
        out_ref[:, col] = value

    product(blocks_ref, types_ref, z_ref, table_ref, size, store)


def last_kernel(
    blocks_ref, types_ref, own_hbm, partner_ref, table_ref, first_hbm, alpha_hbm, out_hbm,
    z_ref, alpha_ref, out_ref, sems, out_sems,
):
    (_, size_a, at_a), (start, size, at_b) = PARTS
    own_copy = pltpu.make_async_copy(own_hbm, z_ref.at[0:BLOCKS], sems.at[0])
    first_copy = pltpu.make_async_copy(first_hbm, out_ref.at[0:start, :], sems.at[1])
    alpha_copy = pltpu.make_async_copy(alpha_hbm, alpha_ref, sems.at[2])
    own_copy.start()
    first_copy.start()
    alpha_copy.start()
    unpack(partner_ref, size, 0, z_ref, BLOCKS)
    own_copy.wait()

    def store(col, value):
        out_ref[start:CAP, col] = value

    product(blocks_ref, types_ref, z_ref, table_ref, size, store)
    first_copy.wait()
    alpha_copy.wait()

    def triple(u, carry):
        for rows, length, at in ((0, size_a, at_a), (start, size, at_b)):
            left = left_half((length, 128))
            a_main, _, a_low, a_low_r = fields(alpha_ref, 2 * u, length, at)
            _, b_main_r, b_low, b_low_r = fields(alpha_ref, 2 * u + 1, length, at)
            alphas = (
                a_main,
                jnp.where(left, jnp.concatenate([a_low, a_low_r], 0), b_main_r),
                jnp.where(left, b_main_r, jnp.concatenate([b_low_r, b_low], 0)),
            )
            for n in range(3):
                col = pl.ds(pl.multiple_of(u * 384 + 128 * n, 128), 128)
                out_ref[rows:rows + length, col] = alphas[n] + out_ref[rows:rows + length, col]
        return carry

    copies = []
    for part in range(4):
        lax.fori_loop(4 * part, 4 * part + 4, triple, 0, unroll=2)
        cols = slice(1536 * part, 1536 * part + 1536)
        copy = pltpu.make_async_copy(out_ref.at[:, cols], out_hbm.at[:, cols], out_sems.at[part])
        copy.start()
        copies.append(copy)
    for copy in copies:
        copy.wait()


def in_vmem(x):
    return pltpu.with_memory_space_constraint(x, pltpu.VMEM)


def smem():
    return pl.BlockSpec(memory_space=pltpu.SMEM)


def vmem():
    return pl.BlockSpec(memory_space=pltpu.VMEM)


def hbm():
    return pl.BlockSpec(memory_space=pl.ANY)


def split_table(table):
    tiles = table.reshape(table.shape[0], BLK, BLK)
    hi = lax.reduce_precision(tiles, 8, 7)
    return jnp.concatenate([hi, tiles - hi], 2).astype(bf16)


def on_device(coeffs_t, alpha_table, alpha_blocks, alpha_types, beta_table, beta_blocks, beta_types, row_counts):
    slots = jax.ShapeDtypeStruct((COLS, PACK, 128), f32)
    coeff_slots = pl.pallas_call(
        coeff_kernel,
        in_specs=[smem(), vmem()],
        out_specs=vmem(),
        out_shape=slots,
        scratch_shapes=[pltpu.VMEM((ROWS, 256), f32)],
        name="coeff_slots",
    )(row_counts, coeffs_t)
    alpha_slots = pl.pallas_call(
        alpha_kernel,
        in_specs=[smem(), smem(), smem(), vmem(), vmem()],
        out_specs=vmem(),
        out_shape=slots,
        scratch_shapes=[
            pltpu.VMEM((ROWS, 256), f32),
            pltpu.VMEM((NA, 2 * NA), bf16),
            pltpu.VMEM((2 * NA, 256), bf16),
            pltpu.VMEM((2 * NA, 256), bf16),
        ],
        name="alpha_slots",
    )(row_counts, alpha_blocks, alpha_types, coeffs_t, split_table(alpha_table))
    tiles = split_table(beta_table)
    own = lax.all_to_all(coeff_slots, "col", split_axis=0, concat_axis=0, tiled=True)
    own, alpha_slots, tiles = lax.optimization_barrier((own, alpha_slots, tiles))
    tiles = in_vmem(tiles)
    route = [(i, i ^ 1) for i in range(8)]
    partner_first = lax.ppermute(own[:, :SPLIT], "cls", route)
    alpha = lax.all_to_all(alpha_slots, "col", split_axis=0, concat_axis=0, tiled=True)
    sizes = [PARTS[0][1], PARTS[1][1]]
    own_first, own_last = pl.pallas_call(
        own_kernel,
        in_specs=[vmem()],
        out_specs=[vmem(), vmem()],
        out_shape=[jax.ShapeDtypeStruct((BLOCKS, size, 256), bf16) for size in sizes],
        name="own_split",
    )(own)
    rest, own_first, own_last = lax.optimization_barrier((own[:, SPLIT:], own_first, own_last))
    partner_last = lax.ppermute(rest, "cls", route)
    blocks, types = beta_blocks.T, beta_types.T
    first = pl.pallas_call(
        first_kernel,
        in_specs=[smem(), smem(), hbm(), hbm(), vmem()],
        out_specs=vmem(),
        out_shape=jax.ShapeDtypeStruct((sizes[0], BLOCKS * BLK), f32),
        scratch_shapes=[
            pltpu.VMEM((2 * BLOCKS, sizes[0], 256), bf16),
            pltpu.VMEM((COLS, SPLIT, 128), f32),
            pltpu.SemaphoreType.DMA((2,)),
        ],
        name="beta_first",
    )(blocks, types, own_first, partner_first, tiles)
    return pl.pallas_call(
        last_kernel,
        in_specs=[smem(), smem(), hbm(), vmem(), vmem(), hbm(), hbm()],
        out_specs=hbm(),
        out_shape=jax.ShapeDtypeStruct((CAP, BLOCKS * BLK), f32),
        scratch_shapes=[
            pltpu.VMEM((2 * BLOCKS, sizes[1], 256), bf16),
            pltpu.VMEM((COLS, PACK, 128), f32),
            pltpu.VMEM((CAP, BLOCKS * BLK), f32),
            pltpu.SemaphoreType.DMA((3,)),
            pltpu.SemaphoreType.DMA((4,)),
        ],
        name="beta_last",
    )(blocks, types, own_last, in_vmem(partner_last), tiles, first, alpha)


def solution(mesh):
    return jax.shard_map(
        on_device,
        mesh=mesh,
        in_specs=(P(("cls", "col"), None), P(), P(), P(), P(), P("cls", None), P("cls", None), P()),
        out_specs=P("col", "cls"),
        check_vma=False,
    )
```

time: 70 us -> 74.1 us (1.059)
  Pallas kernels: 27.3 us -> 31.9 us
  waiting for transfers between devices: 18.7 us -> 14.2 us
  local copies, waits for them, and re-layouts: 4.01 us -> 6.89 us
    ppermute x1 -> x2, waiting for transfers between devices: 2.3 us -> 11.9 us  [the longest x1 11.9 us: on_device(): partner_first = lax.ppermute(own[:, :SPLIT], 'cls', route)]
    all_to_all x1, waiting for transfers between devices: 9.19 us -> 0.01 us  [on_device(): lax.all_to_all(alpha_slots, 'col', split_axis=0, concat_axis=0, tiled=True)]
    all_to_all x1, waiting for transfers between devices: 7.24 us -> 2.28 us  [on_device(): lax.all_to_all(coeff_slots, 'col', split_axis=0, concat_axis=0, tiled=True)]
    pallas_call x2 -> x3, Pallas kernels: 17.1 us -> 21.5 us  [the longest x1 8.32 us: on_device(): pl.pallas_call(first_kernel, in_specs=[smem(), smem(), hbm(), hbm(), vmem...]
    slice x0 -> x2, local copies, waits for them, and re-layouts: none -> 1.71 us  [the longest x1 0.93 us: on_device(): partner_first = lax.ppermute(own[:, :SPLIT], 'cls', route)]
    another operation x2, other arithmetic: 1.15 us -> 2.74 us
    unnamed x2 -> x6, local copies, waits for them, and re-layouts: 0.01 us -> 1.02 us
    concatenate x2, other arithmetic: 3.13 us -> 2.16 us  [split_table(): return jnp.concatenate([hi, tiles - hi], 2).astype(bf16)]
  transfers between devices with their start and end apart: 3 -> 4, of which waited for: 3 -> 2; matrix products, arithmetic and copies ran while one was open for 12% -> 15% of each run, Pallas kernels for 18% -> 28%
where the time goes in v6:
time: 74.1 us; the launch traced here: 73.2 us
  Pallas kernels  31.9 us (43%)
  starting transfers between devices  15.4 us (21%)
  waiting for transfers between devices  14.2 us (19%)
  local copies, waits for them, and re-layouts  6.89 us (9%)
  other arithmetic  4.9 us (7%)
    ppermute x1, waiting for transfers between devices, on_device(): partner_first = lax.ppermute(own[:, :SPLIT], 'cls', route)  11.9 us
    all_to_all x1, starting transfers between devices, on_device(): lax.all_to_all(coeff_slots, 'col', split_axis=0, concat_axis=0, tiled=True)  8.58 us
    pallas_call x1, Pallas kernels, on_device(): pl.pallas_call(first_kernel, in_specs=[smem(), smem(), hbm(), hbm(), vmem...  8.32 us
    pallas_call x1, Pallas kernels, on_device(): pl.pallas_call(last_kernel, in_specs=[smem(), smem(), hbm(), vmem(), vmem...  7.96 us
    pallas_call x1, Pallas kernels, on_device(): pl.pallas_call(alpha_kernel, in_specs=[smem(), smem(), smem(), vmem(), vm...  7.15 us
    pallas_call x1, Pallas kernels, on_device(): pl.pallas_call(own_kernel, in_specs=[vmem()], out_specs=[vmem(), vmem()],...  5.23 us
    all_to_all x1, starting transfers between devices, on_device(): lax.all_to_all(alpha_slots, 'col', split_axis=0, concat_axis=0, tiled=True)  5.13 us
    reshape x2, local copies, waits for them, and re-layouts, split_table(): tiles = table.reshape(table.shape[0], BLK, BLK)  4.16 us
  transfers between devices with their start and end apart: 4, of which 2 were waited for; matrix products, arithmetic and copies ran while one was open for 15% of the time, Pallas kernels for 28%

profile of v6, /device:TPU:1, one launch (start us, length us, event | category | flops | bytes accessed | tf_op | source)
XLA Modules:
  0.0 73.2 jit_solution(13413688349408467792)
XLA Ops:
  0.0 0.0 copy-start.2
  0.0 3.2 %coeff_slots.1 = f32[32,72,128]{2,1,0:T(8,128)} custom-call(s32[32]{0:T(128)} %counts_ref.3, f32[192,1024]{1,0:T(8,128)} %x_ref.3), custom_call_target="tpu_custom_call" | custom-call | tf_op jit(solution)/shard_map/coeff_slots/pallas_call | solution.py:250
  3.2 8.6 %all-to-all-start = ((f32[32,72,128]{2,1,0:T(8,128)}), f32[32,72,128]{2,1,0:T(8,128)S(1)}, u32[]{:S(2)}, u32[]{:S(2)}) async-start(f32[32,72,128]{2,1,0:T(8,128)} %coeff_slots.1), calls=%async_computation | async-start | bytes 2359296 | tf_op jit(solution)/shard_map/all_to_all | solution.py:272
  11.8 0.0 copy-done.2
  11.8 2.2 %reshape.6 = f32[64,64,64]{2,1,0:T(8,128)} reshape(f32[64,4096]{1,0:T(8,128)S(1)} %copy-done.2) | data formatting | bytes 2097152 | tf_op jit(solution)/shard_map/reshape | solution.py:243
  14.0 2.0 %reshape.7 = f32[64,64,64]{2,1,0:T(8,128)S(1)} reshape(f32[64,4096]{1,0:T(8,128)} %param.12) | data formatting | bytes 2097152 | tf_op jit(solution)/shard_map/reshape | solution.py:243
  16.0 2.2 %reduce-precision_convert_fusion.1 = (bf16[64,64,64]{2,1,0:T(8,128)(2,1)S(1)}, bf16[64,64,64]{2,1,0:T(8,128)(2,1)S(1)}) fusion(f32[64,64,64]{2,1,0:T(8,128)} %reshape.6), kind=kLoop, calls=%fused_computation.3 | loop fusion | flops 1048576 | bytes 2097152 | tf_op jit(solution)/shard_map/convert.2
  18.1 1.6 %pad_maximum_fusion.table_ref = bf16[64,64,128]{2,1,0:T(8,128)(2,1)} fusion(bf16[64,64,64]{2,1,0:T(8,128)(2,1)S(1)} %get-tuple-element.24, bf16[64,64,64]{2,1,0:T(8,128)(2,1)S(1)} %get-tuple-element.23), kind=kLoop, calls=%fused_computation.6 | loop fusion | flops 2097152 | bytes 2097152 | tf_op jit(solution)/shard_map/concatenate | solution.py:245
  19.7 7.1 %alpha_slots.1 = f32[32,72,128]{2,1,0:T(8,128)} custom-call(s32[32]{0:T(128)} %counts_ref.3, s32[16,16]{1,0:T(8,128)} %blocks_ref.1, s32[16,16]{1,0:T(8,128)} %types_ref.1, f32[192,1024]{1,0:T(8,128)} %x_ref.3, bf16[64,64,128]{2,1,0:T(8,128)(2,1)} %pad_maximum_fusion.table_ref), custom_call_target="tpu_custom_call" | custom-call | tf_op jit(solution)/shard_map/alpha_slots/pallas_call | solution.py:258
  26.9 0.6 reduce-precision_convert_fusion
  27.4 0.6 pad_maximum_fusion.1.table_ref
  28.0 2.3 %all-to-all-done.own_ref = f32[32,72,128]{2,1,0:T(8,128)S(1)} async-done(((f32[32,72,128]{2,1,0:T(8,128)}), f32[32,72,128]{2,1,0:T(8,128)S(1)}, u32[]{:S(2)}, u32[]{:S(2)}) %all-to-all-start) | async-done | bytes 1179680 | tf_op jit(solution)/shard_map/all_to_all | solution.py:272
  30.3 0.0 copy-start
  30.3 5.1 %all-to-all-start.1 = ((f32[32,72,128]{2,1,0:T(8,128)}), f32[32,72,128]{2,1,0:T(8,128)S(1)}, u32[]{:S(2)}, u32[]{:S(2)}) async-start(f32[32,72,128]{2,1,0:T(8,128)} %alpha_slots.1), calls=%async_computation.1 | async-start | bytes 2359296 | tf_op jit(solution)/shard_map/all_to_all | solution.py:277
  35.5 0.9 %slice.7 = f32[32,48,128]{2,1,0:T(8,128)} slice(f32[32,72,128]{2,1,0:T(8,128)S(1)} %all-to-all-done.own_ref), slice={[0:32], [0:48], [0:128]} | slice | bytes 1572864 | tf_op jit(solution)/shard_map/slice | solution.py:276
  36.4 1.6 %collective-permute-start.1 = (f32[32,48,128]{2,1,0:T(8,128)}, f32[32,48,128]{2,1,0:T(8,128)}, u32[]{:S(2)}, u32[]{:S(2)}) collective-permute-start(f32[32,48,128]{2,1,0:T(8,128)} %slice.7), channel_id=1, source_target_pairs={{0,32},{32,0},{64,96},{96,64},{128,160},{160,128},{192,224},{224,1... | collective-permute-start | bytes 2359304 | tf_op jit(solution)/shard_map/ppermute | solution.py:276
  38.0 0.8 %slice.6 = f32[32,24,128]{2,1,0:T(8,128)} slice(f32[32,72,128]{2,1,0:T(8,128)S(1)} %all-to-all-done.own_ref), slice={[0:32], [48:72], [0:128]} | slice | bytes 786432 | tf_op jit(solution)/shard_map/slice | solution.py:286
  38.8 0.0 copy-done
  38.8 5.2 %own_split.1 = (bf16[96,32,256]{2,1,0:T(8,128)(2,1)}, bf16[96,16,256]{2,1,0:T(8,128)(2,1)}) custom-call(f32[32,72,128]{2,1,0:T(8,128)} %copy-done), custom_call_target="tpu_custom_call" | custom-call | tf_op jit(solution)/shard_map/own_split/pallas_call | solution.py:279
  44.0 0.0 collective-permute-start
  44.0 11.9 %collective-permute-done.1.partner_hbm = f32[32,48,128]{2,1,0:T(8,128)} collective-permute-done((f32[32,48,128]{2,1,0:T(8,128)}, f32[32,48,128]{2,1,0:T(8,128)}, u32[]{:S(2)}, u32[]{:S(2)}) %collective-permute-start.1) | collective-permute-done | bytes 786464 | tf_op jit(solution)/shard_map/ppermute | solution.py:276
  55.9 8.3 %beta_first.1.first_hbm = f32[32,6144]{1,0:T(8,128)} custom-call(s32[12,96]{1,0:T(8,128)} %bitcast.2, s32[12,96]{1,0:T(8,128)} %bitcast.4, bf16[96,32,256]{2,1,0:T(8,128)(2,1)} %get-tuple-element.19.own_hbm, f32[32,48,128]{2,1,0:T(8,128)} %collective-permute-done.1.partner_hbm, bf16[64,64,128]{2,1,0:T(8,128)(2,1)S(1)} %pad_maximum_fusion.1.table_ref), custom_call_target="tpu_custom_call" | custom-call | tf_op jit(solution)/shard_map/beta_first/pallas_call | solution.py:289
  64.2 0.0 collective-permute-done.partner_ref
  64.3 0.0 all-to-all-done.1.alpha_hbm
  64.3 0.0 copy-start.1
  64.3 1.0 %copy-done.1 = f32[32,72,128]{2,1,0:T(8,128)} copy-done((f32[32,72,128]{2,1,0:T(8,128)}, f32[32,72,128]{2,1,0:T(8,128)S(1)}, u32[]{:S(2)}) %copy-start.1) | copy-done | bytes 1179672
  65.3 8.0 %beta_last.1 = f32[48,6144]{1,0:T(8,128)} custom-call(s32[12,96]{1,0:T(8,128)} %bitcast.3, s32[12,96]{1,0:T(8,128)} %bitcast.5, bf16[96,16,256]{2,1,0:T(8,128)(2,1)} %get-tuple-element.16.own_hbm, f32[32,24,128]{2,1,0:T(8,128)S(1)} %collective-permute-done.partner_ref, bf16[64,64,128]{2,1,0:T(8,128)(2,1)S(1)} %pad_maximum_fusion.1.table_ref, ...), custom_call_target="tpu_custom_call" | custom-call | tf_op jit(solution)/shard_map/beta_last/pallas_call | solution.py:301
Async XLA Ops:
  0.0 11.8 %copy-start.2 = (f32[64,4096]{1,0:T(8,128)S(1)}, f32[64,4096]{1,0:T(8,128)}, u32[]{:S(2)}) copy-start(f32[64,4096]{1,0:T(8,128)} %param.9) | copy-start | bytes 3145732
  3.2 27.1 %all-to-all-start = ((f32[32,72,128]{2,1,0:T(8,128)}), f32[32,72,128]{2,1,0:T(8,128)S(1)}, u32[]{:S(2)}, u32[]{:S(2)}) async-start(f32[32,72,128]{2,1,0:T(8,128)} %coeff_slots.1), calls=%async_computation | async-start | bytes 2359296 | tf_op jit(solution)/shard_map/all_to_all | solution.py:272
  30.3 8.5 %copy-start = (f32[32,72,128]{2,1,0:T(8,128)}, f32[32,72,128]{2,1,0:T(8,128)S(1)}, u32[]{:S(2)}) copy-start(f32[32,72,128]{2,1,0:T(8,128)S(1)} %all-to-all-done.own_ref) | copy-start | bytes 3538948
  30.3 33.9 %all-to-all-start.1 = ((f32[32,72,128]{2,1,0:T(8,128)}), f32[32,72,128]{2,1,0:T(8,128)S(1)}, u32[]{:S(2)}, u32[]{:S(2)}) async-start(f32[32,72,128]{2,1,0:T(8,128)} %alpha_slots.1), calls=%async_computation.1 | async-start | bytes 2359296 | tf_op jit(solution)/shard_map/all_to_all | solution.py:277
  36.4 19.5 %collective-permute-start.1 = (f32[32,48,128]{2,1,0:T(8,128)}, f32[32,48,128]{2,1,0:T(8,128)}, u32[]{:S(2)}, u32[]{:S(2)}) collective-permute-start(f32[32,48,128]{2,1,0:T(8,128)} %slice.7), channel_id=1, source_target_pairs={{0,32},{32,0},{64,96},{96,64},{128,160},{160,128},{192,224},{224,1... | collective-permute-start | bytes 2359304 | tf_op jit(solution)/shard_map/ppermute | solution.py:276
  44.0 20.2 %collective-permute-start = (f32[32,24,128]{2,1,0:T(8,128)}, f32[32,24,128]{2,1,0:T(8,128)S(1)}, u32[]{:S(2)}, u32[]{:S(2)}) collective-permute-start(f32[32,24,128]{2,1,0:T(8,128)} %slice.6), channel_id=1, source_target_pairs={{0,32},{32,0},{64,96},{96,64},{128,160},{160,128},{192,224},{224,1... | collective-permute-start | bytes 1179656 | tf_op jit(solution)/shard_map/ppermute | solution.py:287
  64.3 1.0 %copy-start.1 = (f32[32,72,128]{2,1,0:T(8,128)}, f32[32,72,128]{2,1,0:T(8,128)S(1)}, u32[]{:S(2)}) copy-start(f32[32,72,128]{2,1,0:T(8,128)S(1)} %all-to-all-done.1.alpha_hbm) | copy-start | bytes 3538948

commit v7 on v6

--- a/solution.py
+++ b/solution.py
@@ -12,13 +12,15 @@
 BLK = 64
 COLS = 32
 CAP = 48
+LOCAL = 192
 HALF = CAP // 2
 PACK = CAP + HALF
 BLOCKS = 96
 DEPTH = 12
 PARTS = ((0, 32, 0), (32, 16, 48))
+PIECES = 4
 SPLIT = 48
-TRIP = 12
+TRIP = 24
 ROWS = NA + CAP + 8
 
 
@@ -31,15 +33,15 @@
     return lax.broadcasted_iota(jnp.int32, shape, len(shape) - 1) < BLK
 
 
-def load_transposed(x_ref, buf_ref):
-    for c in range(NA // 128):
+def transpose_columns(x_ref, buf_ref, chunks):
+    for c in chunks:
         cols = slice(128 * c, 128 * c + 128)
         last = x_ref[128:192, cols]
         buf_ref[cols, 0:128] = x_ref[0:128, cols].T
         buf_ref[cols, 128:256] = jnp.concatenate([last, last], 0).T
 
 
-def write_slots(counts_ref, buf_ref, out_ref):
+def write_slots(counts_ref, buf_ref, out_ref, done=None):
     buf_ref[NA:ROWS, :] = jnp.zeros((ROWS - NA, 256), f32)
     left = left_half((8, 128))
     sub = lax.broadcasted_iota(jnp.int32, (8, 256), 0)
@@ -64,16 +66,38 @@
             out_ref[j, at + size:at + size + size // 2, :] = jnp.concatenate(low, 0) if half > 1 else low[0]
         return start + count
 
-    lax.fori_loop(0, COLS, one, jnp.int32(0))
-
-
-def coeff_kernel(counts_ref, x_ref, out_ref, buf_ref):
-    load_transposed(x_ref, buf_ref)
-    write_slots(counts_ref, buf_ref, out_ref)
+    start = jnp.int32(0)
+    for piece in range(PIECES):
+        each = COLS // PIECES
+        start = lax.fori_loop(each * piece, each * piece + each, one, start)
+        if done is not None:
+            done(piece)
+
+
+def coeff_kernel(counts_ref, x_hbm, out_hbm, x_ref, out_ref, buf_ref, in_sems, out_sems):
+    width, each = NA // 2, COLS // PIECES
+    loads = []
+    for piece in range(2):
+        cols = slice(width * piece, width * piece + width)
+        loads.append(pltpu.make_async_copy(x_hbm.at[:, cols], x_ref.at[:, cols], in_sems.at[piece]))
+        loads[-1].start()
+    for piece in range(2):
+        loads[piece].wait()
+        transpose_columns(x_ref, buf_ref, range(width // 128 * piece, width // 128 * (piece + 1)))
+    stores = []
+
+    def done(piece):
+        rows = slice(each * piece, each * piece + each)
+        stores.append(pltpu.make_async_copy(out_ref.at[rows], out_hbm.at[rows], out_sems.at[piece]))
+        stores[-1].start()
+
+    write_slots(counts_ref, buf_ref, out_ref, done)
+    for store in stores:
+        store.wait()
 
 
 def alpha_kernel(counts_ref, blocks_ref, types_ref, x_ref, table_ref, out_ref, buf_ref, a_ref, hi_ref, lo_ref):
-    load_transposed(x_ref, buf_ref)
+    transpose_columns(x_ref, buf_ref, range(NA // 128))
     blocks = NA // BLK
     for b in range(blocks):
         hi, lo = split(buf_ref[BLK * b:BLK * b + BLK, :])
@@ -160,13 +184,10 @@
     lax.fori_loop(0, BLOCKS // (2 * TRIP), trip, 0)
 
 
-def first_kernel(blocks_ref, types_ref, own_hbm, partner_hbm, table_ref, out_ref, z_ref, partner_ref, sems):
+def first_kernel(blocks_ref, types_ref, own_hbm, partner_ref, table_ref, out_ref, z_ref, sem):
     size = PARTS[0][1]
-    own_copy = pltpu.make_async_copy(own_hbm, z_ref.at[0:BLOCKS], sems.at[0])
-    partner_copy = pltpu.make_async_copy(partner_hbm, partner_ref, sems.at[1])
-    partner_copy.start()
+    own_copy = pltpu.make_async_copy(own_hbm, z_ref.at[0:BLOCKS], sem)
     own_copy.start()
-    partner_copy.wait()
     unpack(partner_ref, size, 0, z_ref, BLOCKS)
     own_copy.wait()
 
@@ -177,16 +198,14 @@
 
 
 def last_kernel(
-    blocks_ref, types_ref, own_hbm, partner_ref, table_ref, first_hbm, alpha_hbm, out_hbm,
-    z_ref, alpha_ref, out_ref, sems, out_sems,
+    blocks_ref, types_ref, own_hbm, partner_ref, table_ref, first_hbm, alpha_ref, out_hbm,
+    z_ref, out_ref, sems, out_sems,
 ):
     (_, size_a, at_a), (start, size, at_b) = PARTS
     own_copy = pltpu.make_async_copy(own_hbm, z_ref.at[0:BLOCKS], sems.at[0])
     first_copy = pltpu.make_async_copy(first_hbm, out_ref.at[0:start, :], sems.at[1])
-    alpha_copy = pltpu.make_async_copy(alpha_hbm, alpha_ref, sems.at[2])
     own_copy.start()
     first_copy.start()
-    alpha_copy.start()
     unpack(partner_ref, size, 0, z_ref, BLOCKS)
     own_copy.wait()
 
@@ -195,7 +214,6 @@
 
     product(blocks_ref, types_ref, z_ref, table_ref, size, store)
     first_copy.wait()
-    alpha_copy.wait()
 
     def triple(u, carry):
         for rows, length, at in ((0, size_a, at_a), (start, size, at_b)):
@@ -249,10 +267,16 @@
     slots = jax.ShapeDtypeStruct((COLS, PACK, 128), f32)
     coeff_slots = pl.pallas_call(
         coeff_kernel,
-        in_specs=[smem(), vmem()],
-        out_specs=vmem(),
+        in_specs=[smem(), hbm()],
+        out_specs=hbm(),
         out_shape=slots,
-        scratch_shapes=[pltpu.VMEM((ROWS, 256), f32)],
+        scratch_shapes=[
+            pltpu.VMEM((LOCAL, NA), f32),
+            pltpu.VMEM((COLS, PACK, 128), f32),
+            pltpu.VMEM((ROWS, 256), f32),
+            pltpu.SemaphoreType.DMA((2,)),
+            pltpu.SemaphoreType.DMA((PIECES,)),
+        ],
         name="coeff_slots",
     )(row_counts, coeffs_t)
     alpha_slots = pl.pallas_call(
@@ -273,7 +297,7 @@
     own, alpha_slots, tiles = lax.optimization_barrier((own, alpha_slots, tiles))
     tiles = in_vmem(tiles)
     route = [(i, i ^ 1) for i in range(8)]
-    partner_first = lax.ppermute(own[:, :SPLIT], "cls", route)
+    partner_first = lax.ppermute(in_vmem(own[:, :SPLIT]), "cls", route)
     alpha = lax.all_to_all(alpha_slots, "col", split_axis=0, concat_axis=0, tiled=True)
     sizes = [PARTS[0][1], PARTS[1][1]]
     own_first, own_last = pl.pallas_call(
@@ -288,30 +312,28 @@
     blocks, types = beta_blocks.T, beta_types.T
     first = pl.pallas_call(
         first_kernel,
-        in_specs=[smem(), smem(), hbm(), hbm(), vmem()],
+        in_specs=[smem(), smem(), hbm(), vmem(), vmem()],
         out_specs=vmem(),
         out_shape=jax.ShapeDtypeStruct((sizes[0], BLOCKS * BLK), f32),
         scratch_shapes=[
             pltpu.VMEM((2 * BLOCKS, sizes[0], 256), bf16),
-            pltpu.VMEM((COLS, SPLIT, 128), f32),
-            pltpu.SemaphoreType.DMA((2,)),
+            pltpu.SemaphoreType.DMA,
         ],
         name="beta_first",
-    )(blocks, types, own_first, partner_first, tiles)
+    )(blocks, types, own_first, in_vmem(partner_first), tiles)
     return pl.pallas_call(
         last_kernel,
-        in_specs=[smem(), smem(), hbm(), vmem(), vmem(), hbm(), hbm()],
+        in_specs=[smem(), smem(), hbm(), vmem(), vmem(), hbm(), vmem()],
         out_specs=hbm(),
         out_shape=jax.ShapeDtypeStruct((CAP, BLOCKS * BLK), f32),
         scratch_shapes=[
             pltpu.VMEM((2 * BLOCKS, sizes[1], 256), bf16),
-            pltpu.VMEM((COLS, PACK, 128), f32),
             pltpu.VMEM((CAP, BLOCKS * BLK), f32),
-            pltpu.SemaphoreType.DMA((3,)),
+            pltpu.SemaphoreType.DMA((2,)),
             pltpu.SemaphoreType.DMA((4,)),
         ],
         name="beta_last",
-    )(blocks, types, own_last, in_vmem(partner_last), tiles, first, alpha)
+    )(blocks, types, own_last, in_vmem(partner_last), tiles, first, in_vmem(alpha))
 
 
 def solution(mesh):

time: 74.1 us -> 74.4 us (level)
  Pallas kernels: 31.9 us -> 30.3 us
  local copies, waits for them, and re-layouts: 6.89 us -> 8.16 us
    ppermute x1, waiting for transfers between devices: 0.01 us -> 1.74 us  [on_device(): partner_last = lax.ppermute(rest, 'cls', route)]
    pallas_call x2, Pallas kernels: 11.5 us -> 10.3 us  [the longest x1 6.67 us: on_device(): pl.pallas_call(first_kernel, in_specs=[smem(), smem(), hbm(), vmem(), vme...]
    ppermute x1, waiting for transfers between devices: 11.9 us -> 10.7 us  [on_device(): partner_first = lax.ppermute(in_vmem(own[:, :SPLIT]), 'cls', route)]
    slice x1, local copies, waits for them, and re-layouts: 0.78 us -> 1.8 us  [on_device(): own[:, SPLIT:]]
  transfers between devices with their start and end apart: 4 -> 4, of which waited for: 2 -> 3; matrix products, arithmetic and copies ran while one was open for 15% -> 16% of each run, Pallas kernels for 28% -> 26%
where the time goes in v7:
time: 74.4 us; the launch traced here: 73.7 us
  Pallas kernels  30.3 us (41%)
  starting transfers between devices  15.4 us (21%)
  waiting for transfers between devices  14.7 us (20%)
  local copies, waits for them, and re-layouts  8.16 us (11%)
  other arithmetic  4.9 us (7%)
    ppermute x1, waiting for transfers between devices, on_device(): partner_first = lax.ppermute(in_vmem(own[:, :SPLIT]), 'cls', route)  10.7 us
    all_to_all x1, starting transfers between devices, on_device(): lax.all_to_all(coeff_slots, 'col', split_axis=0, concat_axis=0, tiled=True)  8.59 us
    pallas_call x1, Pallas kernels, on_device(): pl.pallas_call(last_kernel, in_specs=[smem(), smem(), hbm(), vmem(), vmem...  7.59 us
    pallas_call x1, Pallas kernels, on_device(): pl.pallas_call(alpha_kernel, in_specs=[smem(), smem(), smem(), vmem(), vm...  7.17 us
    pallas_call x1, Pallas kernels, on_device(): pl.pallas_call(first_kernel, in_specs=[smem(), smem(), hbm(), vmem(), vme...  6.67 us
    pallas_call x1, Pallas kernels, on_device(): pl.pallas_call(own_kernel, in_specs=[vmem()], out_specs=[vmem(), vmem()],...  5.28 us
    all_to_all x1, starting transfers between devices, on_device(): lax.all_to_all(alpha_slots, 'col', split_axis=0, concat_axis=0, tiled=True)  5.17 us
    reshape x2, local copies, waits for them, and re-layouts, split_table(): tiles = table.reshape(table.shape[0], BLK, BLK)  4.17 us
  transfers between devices with their start and end apart: 4, of which 3 were waited for; matrix products, arithmetic and copies ran while one was open for 16% of the time, Pallas kernels for 26%

profile of v7, /device:TPU:1, one launch (start us, length us, event | category | flops | bytes accessed | tf_op | source)
XLA Modules:
  0.0 73.7 jit_solution(3117408157244986150)
XLA Ops:
  0.0 0.0 copy-start.3
  0.0 3.6 %coeff_slots.1 = f32[32,72,128]{2,1,0:T(8,128)} custom-call(s32[32]{0:T(128)} %counts_ref.3, f32[192,1024]{1,0:T(8,128)} %x_ref.1), custom_call_target="tpu_custom_call" | custom-call | tf_op jit(solution)/shard_map/coeff_slots/pallas_call | solution.py:268
  3.6 8.6 %all-to-all-start = ((f32[32,72,128]{2,1,0:T(8,128)}), f32[32,72,128]{2,1,0:T(8,128)S(1)}, u32[]{:S(2)}, u32[]{:S(2)}) async-start(f32[32,72,128]{2,1,0:T(8,128)} %coeff_slots.1), calls=%async_computation | async-start | bytes 2359296 | tf_op jit(solution)/shard_map/all_to_all | solution.py:296
  12.2 0.0 copy-done.3
  12.2 2.2 %reshape.6 = f32[64,64,64]{2,1,0:T(8,128)} reshape(f32[64,4096]{1,0:T(8,128)S(1)} %copy-done.3) | data formatting | bytes 2097152 | tf_op jit(solution)/shard_map/reshape | solution.py:261
  14.4 2.0 %reshape.7 = f32[64,64,64]{2,1,0:T(8,128)S(1)} reshape(f32[64,4096]{1,0:T(8,128)} %param.12) | data formatting | bytes 2097152 | tf_op jit(solution)/shard_map/reshape | solution.py:261
  16.4 2.2 %reduce-precision_convert_fusion.1 = (bf16[64,64,64]{2,1,0:T(8,128)(2,1)S(1)}, bf16[64,64,64]{2,1,0:T(8,128)(2,1)S(1)}) fusion(f32[64,64,64]{2,1,0:T(8,128)} %reshape.6), kind=kLoop, calls=%fused_computation.3 | loop fusion | flops 1048576 | bytes 2097152 | tf_op jit(solution)/shard_map/convert.2
  18.5 1.6 %pad_maximum_fusion.table_ref = bf16[64,64,128]{2,1,0:T(8,128)(2,1)} fusion(bf16[64,64,64]{2,1,0:T(8,128)(2,1)S(1)} %get-tuple-element.24, bf16[64,64,64]{2,1,0:T(8,128)(2,1)S(1)} %get-tuple-element.23), kind=kLoop, calls=%fused_computation.6 | loop fusion | flops 2097152 | bytes 2097152 | tf_op jit(solution)/shard_map/concatenate | solution.py:263
  20.1 7.2 %alpha_slots.1 = f32[32,72,128]{2,1,0:T(8,128)} custom-call(s32[32]{0:T(128)} %counts_ref.3, s32[16,16]{1,0:T(8,128)} %blocks_ref.1, s32[16,16]{1,0:T(8,128)} %types_ref.1, f32[192,1024]{1,0:T(8,128)} %x_ref.1, bf16[64,64,128]{2,1,0:T(8,128)(2,1)} %pad_maximum_fusion.table_ref), custom_call_target="tpu_custom_call" | custom-call | tf_op jit(solution)/shard_map/alpha_slots/pallas_call | solution.py:282
  27.3 0.6 reduce-precision_convert_fusion
  27.9 0.6 pad_maximum_fusion.1.table_ref
  28.5 0.0 copy-start
  28.5 2.2 %all-to-all-done.own_ref = f32[32,72,128]{2,1,0:T(8,128)S(1)} async-done(((f32[32,72,128]{2,1,0:T(8,128)}), f32[32,72,128]{2,1,0:T(8,128)S(1)}, u32[]{:S(2)}, u32[]{:S(2)}) %all-to-all-start) | async-done | bytes 1179680 | tf_op jit(solution)/shard_map/all_to_all | solution.py:296
  30.7 0.0 copy-start.2
  30.7 5.2 %all-to-all-start.1 = ((f32[32,72,128]{2,1,0:T(8,128)}), f32[32,72,128]{2,1,0:T(8,128)S(1)}, u32[]{:S(2)}, u32[]{:S(2)}) async-start(f32[32,72,128]{2,1,0:T(8,128)} %alpha_slots.1), calls=%async_computation.1 | async-start | bytes 2359296 | tf_op jit(solution)/shard_map/all_to_all | solution.py:301
  35.9 0.0 copy-done.2
  35.9 1.0 %slice.7 = f32[32,48,128]{2,1,0:T(8,128)} slice(f32[32,72,128]{2,1,0:T(8,128)S(1)} %all-to-all-done.own_ref), slice={[0:32], [0:48], [0:128]} | slice | bytes 1572864 | tf_op jit(solution)/shard_map/slice | solution.py:300
  36.9 1.6 %collective-permute-start.1 = (f32[32,48,128]{2,1,0:T(8,128)}, f32[32,48,128]{2,1,0:T(8,128)S(1)}, u32[]{:S(2)}, u32[]{:S(2)}) collective-permute-start(f32[32,48,128]{2,1,0:T(8,128)} %slice.7), channel_id=1, source_target_pairs={{0,32},{32,0},{64,96},{96,64},{128,160},{160,128},{192,224},{224,1... | collective-permute-start | bytes 2359304 | tf_op jit(solution)/shard_map/ppermute | solution.py:300
  38.5 1.8 %slice.6 = f32[32,24,128]{2,1,0:T(8,128)} slice(f32[32,72,128]{2,1,0:T(8,128)} %copy-done.2), slice={[0:32], [48:72], [0:128]} | slice | bytes 786432 | tf_op jit(solution)/shard_map/slice | solution.py:310
  40.3 5.3 %own_split.1 = (bf16[96,32,256]{2,1,0:T(8,128)(2,1)}, bf16[96,16,256]{2,1,0:T(8,128)(2,1)}) custom-call(f32[32,72,128]{2,1,0:T(8,128)} %copy-done.2), custom_call_target="tpu_custom_call" | custom-call | tf_op jit(solution)/shard_map/own_split/pallas_call | solution.py:303
  45.6 0.0 collective-permute-start
  45.6 10.7 %collective-permute-done.1.partner_ref = f32[32,48,128]{2,1,0:T(8,128)S(1)} collective-permute-done((f32[32,48,128]{2,1,0:T(8,128)}, f32[32,48,128]{2,1,0:T(8,128)S(1)}, u32[]{:S(2)}, u32[]{:S(2)}) %collective-permute-start.1) | collective-permute-done | bytes 786464 | tf_op jit(solution)/shard_map/ppermute | solution.py:300
  56.3 0.0 copy-done
  56.3 6.7 %beta_first.1.first_hbm = f32[32,6144]{1,0:T(8,128)} custom-call(s32[12,96]{1,0:T(8,128)} %bitcast.2, s32[12,96]{1,0:T(8,128)} %bitcast.4, bf16[96,32,256]{2,1,0:T(8,128)(2,1)} %get-tuple-element.19.own_hbm, f32[32,48,128]{2,1,0:T(8,128)S(1)} %collective-permute-done.1.partner_ref, bf16[64,64,128]{2,1,0:T(8,128)(2,1)S(1)} %pad_maximum_fusion.1.table_ref), custom_call_target="tpu_custom_call" | custom-call | tf_op jit(solution)/shard_map/beta_first/pallas_call | solution.py:313
  63.0 1.7 %collective-permute-done.partner_ref = f32[32,24,128]{2,1,0:T(8,128)S(1)} collective-permute-done((f32[32,24,128]{2,1,0:T(8,128)}, f32[32,24,128]{2,1,0:T(8,128)S(1)}, u32[]{:S(2)}, u32[]{:S(2)}) %collective-permute-start) | collective-permute-done | bytes 393248 | tf_op jit(solution)/shard_map/ppermute | solution.py:311
  64.7 0.0 all-to-all-done.1.alpha_ref
  64.7 0.0 copy-start.1
  64.7 1.2 %copy-done.1 = bf16[64,64,128]{2,1,0:T(8,128)(2,1)S(1)} copy-done((bf16[64,64,128]{2,1,0:T(8,128)(2,1)S(1)}, bf16[64,64,128]{2,1,0:T(8,128)(2,1)}, u32[]{:S(2)}) %copy-start.1) | copy-done | bytes 1048600
  66.0 7.6 %beta_last.1 = f32[48,6144]{1,0:T(8,128)} custom-call(s32[12,96]{1,0:T(8,128)} %bitcast.3, s32[12,96]{1,0:T(8,128)} %bitcast.5, bf16[96,16,256]{2,1,0:T(8,128)(2,1)} %get-tuple-element.16.own_hbm, f32[32,24,128]{2,1,0:T(8,128)S(1)} %collective-permute-done.partner_ref, bf16[64,64,128]{2,1,0:T(8,128)(2,1)S(1)} %copy-done.1, f32[32,6144]{1,0:T(8,128)} %beta_first.1.first_hbm, ...), custom_call_target="tpu_custom_call" | custom-call | tf_op jit(solution)/shard_map/beta_last/pallas_call | solution.py:324
Async XLA Ops:
  0.0 12.2 %copy-start.3 = (f32[64,4096]{1,0:T(8,128)S(1)}, f32[64,4096]{1,0:T(8,128)}, u32[]{:S(2)}) copy-start(f32[64,4096]{1,0:T(8,128)} %param.9) | copy-start | bytes 3145732
  3.6 27.1 %all-to-all-start = ((f32[32,72,128]{2,1,0:T(8,128)}), f32[32,72,128]{2,1,0:T(8,128)S(1)}, u32[]{:S(2)}, u32[]{:S(2)}) async-start(f32[32,72,128]{2,1,0:T(8,128)} %coeff_slots.1), calls=%async_computation | async-start | bytes 2359296 | tf_op jit(solution)/shard_map/all_to_all | solution.py:296
  28.5 27.8 %copy-start = (bf16[64,64,128]{2,1,0:T(8,128)(2,1)}, bf16[64,64,128]{2,1,0:T(8,128)(2,1)S(1)}, u32[]{:S(2)}) copy-start(bf16[64,64,128]{2,1,0:T(8,128)(2,1)S(1)} %pad_maximum_fusion.1.table_ref) | copy-start | bytes 3145732
  30.7 5.2 %copy-start.2 = (f32[32,72,128]{2,1,0:T(8,128)}, f32[32,72,128]{2,1,0:T(8,128)S(1)}, u32[]{:S(2)}) copy-start(f32[32,72,128]{2,1,0:T(8,128)S(1)} %all-to-all-done.own_ref) | copy-start | bytes 3538948
  30.7 34.0 %all-to-all-start.1 = ((f32[32,72,128]{2,1,0:T(8,128)}), f32[32,72,128]{2,1,0:T(8,128)S(1)}, u32[]{:S(2)}, u32[]{:S(2)}) async-start(f32[32,72,128]{2,1,0:T(8,128)} %alpha_slots.1), calls=%async_computation.1 | async-start | bytes 2359296 | tf_op jit(solution)/shard_map/all_to_all | solution.py:301
  36.9 19.4 %collective-permute-start.1 = (f32[32,48,128]{2,1,0:T(8,128)}, f32[32,48,128]{2,1,0:T(8,128)S(1)}, u32[]{:S(2)}, u32[]{:S(2)}) collective-permute-start(f32[32,48,128]{2,1,0:T(8,128)} %slice.7), channel_id=1, source_target_pairs={{0,32},{32,0},{64,96},{96,64},{128,160},{160,128},{192,224},{224,1... | collective-permute-start | bytes 2359304 | tf_op jit(solution)/shard_map/ppermute | solution.py:300
  45.6 19.1 %collective-permute-start = (f32[32,24,128]{2,1,0:T(8,128)}, f32[32,24,128]{2,1,0:T(8,128)S(1)}, u32[]{:S(2)}, u32[]{:S(2)}) collective-permute-start(f32[32,24,128]{2,1,0:T(8,128)} %slice.6), channel_id=1, source_target_pairs={{0,32},{32,0},{64,96},{96,64},{128,160},{160,128},{192,224},{224,1... | collective-permute-start | bytes 1179656 | tf_op jit(solution)/shard_map/ppermute | solution.py:311
  64.7 1.2 %copy-start.1 = (bf16[64,64,128]{2,1,0:T(8,128)(2,1)S(1)}, bf16[64,64,128]{2,1,0:T(8,128)(2,1)}, u32[]{:S(2)}) copy-start(bf16[64,64,128]{2,1,0:T(8,128)(2,1)} %copy-done) | copy-start | bytes 3145732

commit v8 on v7

--- a/solution.py
+++ b/solution.py
@@ -33,12 +33,17 @@
     return lax.broadcasted_iota(jnp.int32, shape, len(shape) - 1) < BLK
 
 
-def transpose_columns(x_ref, buf_ref, chunks):
-    for c in chunks:
+def transpose_pair(x_ref, buf_ref):
+    for c in range(NA // 128):
         cols = slice(128 * c, 128 * c + 128)
-        last = x_ref[128:192, cols]
         buf_ref[cols, 0:128] = x_ref[0:128, cols].T
-        buf_ref[cols, 128:256] = jnp.concatenate([last, last], 0).T
+
+
+def transpose_third(x_ref, buf_ref):
+    for c in range(NA // 128):
+        cols = slice(128 * c, 128 * c + 128)
+        third = x_ref[128:LOCAL, cols]
+        buf_ref[cols, 128:256] = jnp.concatenate([third, third], 0).T
 
 
 def write_slots(counts_ref, buf_ref, out_ref, done=None):
@@ -75,15 +80,15 @@
 
 
 def coeff_kernel(counts_ref, x_hbm, out_hbm, x_ref, out_ref, buf_ref, in_sems, out_sems):
-    width, each = NA // 2, COLS // PIECES
+    each = COLS // PIECES
     loads = []
-    for piece in range(2):
-        cols = slice(width * piece, width * piece + width)
-        loads.append(pltpu.make_async_copy(x_hbm.at[:, cols], x_ref.at[:, cols], in_sems.at[piece]))
+    for piece, rows in enumerate((slice(0, 128), slice(128, LOCAL))):
+        loads.append(pltpu.make_async_copy(x_hbm.at[rows], x_ref.at[rows], in_sems.at[piece]))
         loads[-1].start()
-    for piece in range(2):
-        loads[piece].wait()
-        transpose_columns(x_ref, buf_ref, range(width // 128 * piece, width // 128 * (piece + 1)))
+    loads[0].wait()
+    transpose_pair(x_ref, buf_ref)
+    loads[1].wait()
+    transpose_third(x_ref, buf_ref)
     stores = []
 
     def done(piece):
@@ -97,7 +102,8 @@
 
 
 def alpha_kernel(counts_ref, blocks_ref, types_ref, x_ref, table_ref, out_ref, buf_ref, a_ref, hi_ref, lo_ref):
-    transpose_columns(x_ref, buf_ref, range(NA // 128))
+    transpose_pair(x_ref, buf_ref)
+    transpose_third(x_ref, buf_ref)
     blocks = NA // BLK
     for b in range(blocks):
         hi, lo = split(buf_ref[BLK * b:BLK * b + BLK, :])
@@ -184,12 +190,15 @@
     lax.fori_loop(0, BLOCKS // (2 * TRIP), trip, 0)
 
 
-def first_kernel(blocks_ref, types_ref, own_hbm, partner_ref, table_ref, out_ref, z_ref, sem):
+def first_kernel(blocks_ref, types_ref, own_hbm, partner_ref, table_hbm, out_ref, z_ref, table_ref, sems):
     size = PARTS[0][1]
-    own_copy = pltpu.make_async_copy(own_hbm, z_ref.at[0:BLOCKS], sem)
+    own_copy = pltpu.make_async_copy(own_hbm, z_ref.at[0:BLOCKS], sems.at[0])
+    table_copy = pltpu.make_async_copy(table_hbm, table_ref, sems.at[1])
     own_copy.start()
+    table_copy.start()
     unpack(partner_ref, size, 0, z_ref, BLOCKS)
     own_copy.wait()
+    table_copy.wait()
 
     def store(col, value):
         out_ref[:, col] = value
@@ -198,16 +207,19 @@
 
 
 def last_kernel(
-    blocks_ref, types_ref, own_hbm, partner_ref, table_ref, first_hbm, alpha_ref, out_hbm,
-    z_ref, out_ref, sems, out_sems,
+    blocks_ref, types_ref, own_hbm, partner_ref, table_hbm, first_hbm, alpha_ref, out_hbm,
+    z_ref, table_ref, out_ref, sems, out_sems,
 ):
     (_, size_a, at_a), (start, size, at_b) = PARTS
     own_copy = pltpu.make_async_copy(own_hbm, z_ref.at[0:BLOCKS], sems.at[0])
     first_copy = pltpu.make_async_copy(first_hbm, out_ref.at[0:start, :], sems.at[1])
+    table_copy = pltpu.make_async_copy(table_hbm, table_ref, sems.at[2])
     own_copy.start()
+    table_copy.start()
     first_copy.start()
     unpack(partner_ref, size, 0, z_ref, BLOCKS)
     own_copy.wait()
+    table_copy.wait()
 
     def store(col, value):
         out_ref[start:CAP, col] = value
@@ -295,9 +307,8 @@
     tiles = split_table(beta_table)
     own = lax.all_to_all(coeff_slots, "col", split_axis=0, concat_axis=0, tiled=True)
     own, alpha_slots, tiles = lax.optimization_barrier((own, alpha_slots, tiles))
-    tiles = in_vmem(tiles)
     route = [(i, i ^ 1) for i in range(8)]
-    partner_first = lax.ppermute(in_vmem(own[:, :SPLIT]), "cls", route)
+    partner_first = lax.ppermute(own[:, :SPLIT], "cls", route)
     alpha = lax.all_to_all(alpha_slots, "col", split_axis=0, concat_axis=0, tiled=True)
     sizes = [PARTS[0][1], PARTS[1][1]]
     own_first, own_last = pl.pallas_call(
@@ -306,30 +317,32 @@
         out_specs=[vmem(), vmem()],
         out_shape=[jax.ShapeDtypeStruct((BLOCKS, size, 256), bf16) for size in sizes],
         name="own_split",
-    )(own)
+    )(in_vmem(own))
     rest, own_first, own_last = lax.optimization_barrier((own[:, SPLIT:], own_first, own_last))
     partner_last = lax.ppermute(rest, "cls", route)
     blocks, types = beta_blocks.T, beta_types.T
     first = pl.pallas_call(
         first_kernel,
-        in_specs=[smem(), smem(), hbm(), vmem(), vmem()],
+        in_specs=[smem(), smem(), hbm(), vmem(), hbm()],
         out_specs=vmem(),
         out_shape=jax.ShapeDtypeStruct((sizes[0], BLOCKS * BLK), f32),
         scratch_shapes=[
             pltpu.VMEM((2 * BLOCKS, sizes[0], 256), bf16),
-            pltpu.SemaphoreType.DMA,
+            pltpu.VMEM((64, BLK, 128), bf16),
+            pltpu.SemaphoreType.DMA((2,)),
         ],
         name="beta_first",
     )(blocks, types, own_first, in_vmem(partner_first), tiles)
     return pl.pallas_call(
         last_kernel,
-        in_specs=[smem(), smem(), hbm(), vmem(), vmem(), hbm(), vmem()],
+        in_specs=[smem(), smem(), hbm(), vmem(), hbm(), hbm(), vmem()],
         out_specs=hbm(),
         out_shape=jax.ShapeDtypeStruct((CAP, BLOCKS * BLK), f32),
         scratch_shapes=[
             pltpu.VMEM((2 * BLOCKS, sizes[1], 256), bf16),
+            pltpu.VMEM((64, BLK, 128), bf16),
             pltpu.VMEM((CAP, BLOCKS * BLK), f32),
-            pltpu.SemaphoreType.DMA((2,)),
+            pltpu.SemaphoreType.DMA((3,)),
             pltpu.SemaphoreType.DMA((4,)),
         ],
         name="beta_last",

time: 74.4 us -> 74.3 us (level)
  local copies, waits for them, and re-layouts: 8.16 us -> 5.14 us
  waiting for transfers between devices: 14.7 us -> 16.1 us
  starting transfers between devices: 15.4 us -> 16.4 us
  other arithmetic: 4.9 us -> 5.86 us
    ppermute x1, waiting for transfers between devices: 10.7 us -> 13.7 us  [on_device(): partner_first = lax.ppermute(own[:, :SPLIT], 'cls', route)]
    slice x1, local copies, waits for them, and re-layouts: 1.8 us -> 0.03 us  [on_device(): own[:, SPLIT:]]
    pallas_call x1, Pallas kernels: 5.28 us -> 4.03 us  [on_device(): pl.pallas_call(own_kernel, in_specs=[vmem()], out_specs=[vmem(), vmem()],...]
    unnamed x8 -> x2, local copies, waits for them, and re-layouts: 1.24 us -> 0.01 us
    all_to_all x1, waiting for transfers between devices: 2.24 us -> 1.24 us  [on_device(): lax.all_to_all(coeff_slots, 'col', split_axis=0, concat_axis=0, tiled=True)]
    all_to_all x1, starting transfers between devices: 5.17 us -> 6.15 us  [on_device(): lax.all_to_all(alpha_slots, 'col', split_axis=0, concat_axis=0, tiled=True)]
    concatenate x2, other arithmetic: 2.16 us -> 3.12 us  [split_table(): return jnp.concatenate([hi, tiles - hi], 2).astype(bf16)]
    pallas_call x2, Pallas kernels: 14.3 us -> 15.2 us  [the longest x1 7.88 us: on_device(): pl.pallas_call(last_kernel, in_specs=[smem(), smem(), hbm(), vmem(), hbm(...]
  transfers between devices with their start and end apart: 4 -> 4, of which waited for: 3 -> 3; matrix products, arithmetic and copies ran while one was open for 16% -> 15% of each run, Pallas kernels for 26% -> 25%
where the time goes in v8:
time: 74.3 us; the launch traced here: 73.7 us
  Pallas kernels  30 us (40%)
  starting transfers between devices  16.4 us (22%)
  waiting for transfers between devices  16.1 us (22%)
  other arithmetic  5.86 us (8%)
  local copies, waits for them, and re-layouts  5.14 us (7%)
    ppermute x1, waiting for transfers between devices, on_device(): partner_first = lax.ppermute(own[:, :SPLIT], 'cls', route)  13.7 us
    all_to_all x1, starting transfers between devices, on_device(): lax.all_to_all(coeff_slots, 'col', split_axis=0, concat_axis=0, tiled=True)  8.59 us
    pallas_call x1, Pallas kernels, on_device(): pl.pallas_call(last_kernel, in_specs=[smem(), smem(), hbm(), vmem(), hbm(...  7.88 us
    pallas_call x1, Pallas kernels, on_device(): pl.pallas_call(first_kernel, in_specs=[smem(), smem(), hbm(), vmem(), hbm...  7.27 us
    pallas_call x1, Pallas kernels, on_device(): pl.pallas_call(alpha_kernel, in_specs=[smem(), smem(), smem(), vmem(), vm...  7.22 us
    all_to_all x1, starting transfers between devices, on_device(): lax.all_to_all(alpha_slots, 'col', split_axis=0, concat_axis=0, tiled=True)  6.15 us
    reshape x2, local copies, waits for them, and re-layouts, split_table(): tiles = table.reshape(table.shape[0], BLK, BLK)  4.17 us
    pallas_call x1, Pallas kernels, on_device(): pl.pallas_call(own_kernel, in_specs=[vmem()], out_specs=[vmem(), vmem()],...  4.03 us
  transfers between devices with their start and end apart: 4, of which 3 were waited for; matrix products, arithmetic and copies ran while one was open for 15% of the time, Pallas kernels for 25%

profile of v8, /device:TPU:1, one launch (start us, length us, event | category | flops | bytes accessed | tf_op | source)
XLA Modules:
  0.0 73.7 jit_solution(7432890644716094892)
XLA Ops:
  0.0 0.0 copy-start
  0.0 3.6 %coeff_slots.1 = f32[32,72,128]{2,1,0:T(8,128)} custom-call(s32[32]{0:T(128)} %counts_ref.3, f32[192,1024]{1,0:T(8,128)} %x_ref.1), custom_call_target="tpu_custom_call" | custom-call | tf_op jit(solution)/shard_map/coeff_slots/pallas_call | solution.py:280
  3.6 8.6 %all-to-all-start = ((f32[32,72,128]{2,1,0:T(8,128)}), f32[32,72,128]{2,1,0:T(8,128)S(1)}, u32[]{:S(2)}, u32[]{:S(2)}) async-start(f32[32,72,128]{2,1,0:T(8,128)} %coeff_slots.1), calls=%async_computation | async-start | bytes 2359296 | tf_op jit(solution)/shard_map/all_to_all | solution.py:308
  12.2 0.0 copy-done
  12.2 2.2 %reshape.6 = f32[64,64,64]{2,1,0:T(8,128)} reshape(f32[64,4096]{1,0:T(8,128)S(1)} %copy-done) | data formatting | bytes 2097152 | tf_op jit(solution)/shard_map/reshape | solution.py:273
  14.4 2.0 %reshape.7 = f32[64,64,64]{2,1,0:T(8,128)S(1)} reshape(f32[64,4096]{1,0:T(8,128)} %param.12) | data formatting | bytes 2097152 | tf_op jit(solution)/shard_map/reshape | solution.py:273
  16.4 2.2 %reduce-precision_convert_fusion.1 = (bf16[64,64,64]{2,1,0:T(8,128)(2,1)S(1)}, bf16[64,64,64]{2,1,0:T(8,128)(2,1)S(1)}) fusion(f32[64,64,64]{2,1,0:T(8,128)} %reshape.6), kind=kLoop, calls=%fused_computation.3 | loop fusion | flops 1048576 | bytes 2097152 | tf_op jit(solution)/shard_map/convert.2
  18.6 1.6 %pad_maximum_fusion.table_ref = bf16[64,64,128]{2,1,0:T(8,128)(2,1)} fusion(bf16[64,64,64]{2,1,0:T(8,128)(2,1)S(1)} %get-tuple-element.24, bf16[64,64,64]{2,1,0:T(8,128)(2,1)S(1)} %get-tuple-element.23), kind=kLoop, calls=%fused_computation.6 | loop fusion | flops 2097152 | bytes 2097152 | tf_op jit(solution)/shard_map/concatenate | solution.py:275
  20.2 7.2 %alpha_slots.1 = f32[32,72,128]{2,1,0:T(8,128)} custom-call(s32[32]{0:T(128)} %counts_ref.3, s32[16,16]{1,0:T(8,128)} %blocks_ref.1, s32[16,16]{1,0:T(8,128)} %types_ref.1, f32[192,1024]{1,0:T(8,128)} %x_ref.1, bf16[64,64,128]{2,1,0:T(8,128)(2,1)} %pad_maximum_fusion.table_ref), custom_call_target="tpu_custom_call" | custom-call | tf_op jit(solution)/shard_map/alpha_slots/pallas_call | solution.py:294
  27.4 0.6 reduce-precision_convert_fusion
  28.0 1.6 %pad_maximum_fusion.1.table_hbm = bf16[64,64,128]{2,1,0:T(8,128)(2,1)} fusion(bf16[64,64,64]{2,1,0:T(8,128)(2,1)S(1)} %get-tuple-element.22, bf16[64,64,64]{2,1,0:T(8,128)(2,1)S(1)} %get-tuple-element.21), kind=kLoop, calls=%fused_computation.7 | loop fusion | flops 2097152 | bytes 2097152 | tf_op jit(solution)/shard_map/concatenate | solution.py:275
  29.5 1.2 %all-to-all-done.own_ref = f32[32,72,128]{2,1,0:T(8,128)S(1)} async-done(((f32[32,72,128]{2,1,0:T(8,128)}), f32[32,72,128]{2,1,0:T(8,128)S(1)}, u32[]{:S(2)}, u32[]{:S(2)}) %all-to-all-start) | async-done | bytes 1179680 | tf_op jit(solution)/shard_map/all_to_all | solution.py:308
  30.8 6.1 %all-to-all-start.1 = ((f32[32,72,128]{2,1,0:T(8,128)}), f32[32,72,128]{2,1,0:T(8,128)S(1)}, u32[]{:S(2)}, u32[]{:S(2)}) async-start(f32[32,72,128]{2,1,0:T(8,128)} %alpha_slots.1), calls=%async_computation.1 | async-start | bytes 2359296 | tf_op jit(solution)/shard_map/all_to_all | solution.py:312
  36.9 0.9 %slice.7 = f32[32,48,128]{2,1,0:T(8,128)} slice(f32[32,72,128]{2,1,0:T(8,128)S(1)} %all-to-all-done.own_ref), slice={[0:32], [0:48], [0:128]} | slice | bytes 1572864 | tf_op jit(solution)/shard_map/slice | solution.py:311
  37.8 1.6 %collective-permute-start.1 = (f32[32,48,128]{2,1,0:T(8,128)}, f32[32,48,128]{2,1,0:T(8,128)S(1)}, u32[]{:S(2)}, u32[]{:S(2)}) collective-permute-start(f32[32,48,128]{2,1,0:T(8,128)} %slice.7), channel_id=1, source_target_pairs={{0,32},{32,0},{64,96},{96,64},{128,160},{160,128},{192,224},{224,1... | collective-permute-start | bytes 2359304 | tf_op jit(solution)/shard_map/ppermute | solution.py:311
  39.5 4.0 %own_split.1 = (bf16[96,32,256]{2,1,0:T(8,128)(2,1)}, bf16[96,16,256]{2,1,0:T(8,128)(2,1)}) custom-call(f32[32,72,128]{2,1,0:T(8,128)S(1)} %all-to-all-done.own_ref), custom_call_target="tpu_custom_call" | custom-call | tf_op jit(solution)/shard_map/own_split/pallas_call | solution.py:314
  43.5 0.0 collective-permute-start
  43.5 13.7 %collective-permute-done.1.partner_ref = f32[32,48,128]{2,1,0:T(8,128)S(1)} collective-permute-done((f32[32,48,128]{2,1,0:T(8,128)}, f32[32,48,128]{2,1,0:T(8,128)S(1)}, u32[]{:S(2)}, u32[]{:S(2)}) %collective-permute-start.1) | collective-permute-done | bytes 786464 | tf_op jit(solution)/shard_map/ppermute | solution.py:311
  57.3 7.3 %beta_first.1.first_hbm = f32[32,6144]{1,0:T(8,128)} custom-call(s32[12,96]{1,0:T(8,128)} %bitcast.2, s32[12,96]{1,0:T(8,128)} %bitcast.4, bf16[96,32,256]{2,1,0:T(8,128)(2,1)} %get-tuple-element.19.own_hbm, f32[32,48,128]{2,1,0:T(8,128)S(1)} %collective-permute-done.1.partner_ref, bf16[64,64,128]{2,1,0:T(8,128)(2,1)} %pad_maximum_fusion.1.table_hbm), custom_call_target="tpu_custom_call" | custom-call | tf_op jit(solution)/shard_map/beta_first/pallas_call | solution.py:324
  64.6 1.1 %collective-permute-done.partner_ref = f32[32,24,128]{2,1,0:T(8,128)S(1)} collective-permute-done((f32[32,24,128]{2,1,0:T(8,128)S(1)}, f32[32,24,128]{2,1,0:T(8,128)S(1)}, u32[]{:S(2)}, u32[]{:S(2)}) %collective-permute-start) | collective-permute-done | bytes 393248 | tf_op jit(solution)/shard_map/ppermute | solution.py:322
  65.7 0.0 all-to-all-done.1.alpha_ref
  65.7 7.9 %beta_last.1 = f32[48,6144]{1,0:T(8,128)} custom-call(s32[12,96]{1,0:T(8,128)} %bitcast.3, s32[12,96]{1,0:T(8,128)} %bitcast.5, bf16[96,16,256]{2,1,0:T(8,128)(2,1)} %get-tuple-element.16.own_hbm, f32[32,24,128]{2,1,0:T(8,128)S(1)} %collective-permute-done.partner_ref, bf16[64,64,128]{2,1,0:T(8,128)(2,1)} %pad_maximum_fusion.1.table_hbm, ...), custom_call_target="tpu_custom_call" | custom-call | tf_op jit(solution)/shard_map/beta_last/pallas_call | solution.py:336
  (1 shorter events, 0.0 us)
Async XLA Ops:
  0.0 12.2 %copy-start = (f32[64,4096]{1,0:T(8,128)S(1)}, f32[64,4096]{1,0:T(8,128)}, u32[]{:S(2)}) copy-start(f32[64,4096]{1,0:T(8,128)} %param.9) | copy-start | bytes 3145732
  3.6 27.1 %all-to-all-start = ((f32[32,72,128]{2,1,0:T(8,128)}), f32[32,72,128]{2,1,0:T(8,128)S(1)}, u32[]{:S(2)}, u32[]{:S(2)}) async-start(f32[32,72,128]{2,1,0:T(8,128)} %coeff_slots.1), calls=%async_computation | async-start | bytes 2359296 | tf_op jit(solution)/shard_map/all_to_all | solution.py:308
  30.8 34.9 %all-to-all-start.1 = ((f32[32,72,128]{2,1,0:T(8,128)}), f32[32,72,128]{2,1,0:T(8,128)S(1)}, u32[]{:S(2)}, u32[]{:S(2)}) async-start(f32[32,72,128]{2,1,0:T(8,128)} %alpha_slots.1), calls=%async_computation.1 | async-start | bytes 2359296 | tf_op jit(solution)/shard_map/all_to_all | solution.py:312
  37.8 19.4 %collective-permute-start.1 = (f32[32,48,128]{2,1,0:T(8,128)}, f32[32,48,128]{2,1,0:T(8,128)S(1)}, u32[]{:S(2)}, u32[]{:S(2)}) collective-permute-start(f32[32,48,128]{2,1,0:T(8,128)} %slice.7), channel_id=1, source_target_pairs={{0,32},{32,0},{64,96},{96,64},{128,160},{160,128},{192,224},{224,1... | collective-permute-start | bytes 2359304 | tf_op jit(solution)/shard_map/ppermute | solution.py:311
  43.5 22.2 %collective-permute-start = (f32[32,24,128]{2,1,0:T(8,128)S(1)}, f32[32,24,128]{2,1,0:T(8,128)S(1)}, u32[]{:S(2)}, u32[]{:S(2)}) collective-permute-start(f32[32,24,128]{2,1,0:T(8,128)S(1)} %slice.6), channel_id=1, source_target_pairs={{0,32},{32,0},{64,96},{96,64},{128,160},{160,128},{192,224},{224,1... | collective-permute-start | bytes 1179656 | tf_op jit(solution)/shard_map/ppermute | solution.py:322

commit v9 on v8

--- a/solution.py
+++ b/solution.py
@@ -18,7 +18,6 @@
 BLOCKS = 96
 DEPTH = 12
 PARTS = ((0, 32, 0), (32, 16, 48))
-PIECES = 4
 SPLIT = 48
 TRIP = 24
 ROWS = NA + CAP + 8
@@ -46,7 +45,7 @@
         buf_ref[cols, 128:256] = jnp.concatenate([third, third], 0).T
 
 
-def write_slots(counts_ref, buf_ref, out_ref, done=None):
+def write_slots(counts_ref, buf_ref, out_ref):
     buf_ref[NA:ROWS, :] = jnp.zeros((ROWS - NA, 256), f32)
     left = left_half((8, 128))
     sub = lax.broadcasted_iota(jnp.int32, (8, 256), 0)
@@ -71,34 +70,13 @@
             out_ref[j, at + size:at + size + size // 2, :] = jnp.concatenate(low, 0) if half > 1 else low[0]
         return start + count
 
-    start = jnp.int32(0)
-    for piece in range(PIECES):
-        each = COLS // PIECES
-        start = lax.fori_loop(each * piece, each * piece + each, one, start)
-        if done is not None:
-            done(piece)
-
-
-def coeff_kernel(counts_ref, x_hbm, out_hbm, x_ref, out_ref, buf_ref, in_sems, out_sems):
-    each = COLS // PIECES
-    loads = []
-    for piece, rows in enumerate((slice(0, 128), slice(128, LOCAL))):
-        loads.append(pltpu.make_async_copy(x_hbm.at[rows], x_ref.at[rows], in_sems.at[piece]))
-        loads[-1].start()
-    loads[0].wait()
+    lax.fori_loop(0, COLS, one, jnp.int32(0))
+
+
+def coeff_kernel(counts_ref, x_ref, out_ref, buf_ref):
     transpose_pair(x_ref, buf_ref)
-    loads[1].wait()
     transpose_third(x_ref, buf_ref)
-    stores = []
-
-    def done(piece):
-        rows = slice(each * piece, each * piece + each)
-        stores.append(pltpu.make_async_copy(out_ref.at[rows], out_hbm.at[rows], out_sems.at[piece]))
-        stores[-1].start()
-
-    write_slots(counts_ref, buf_ref, out_ref, done)
-    for store in stores:
-        store.wait()
+    write_slots(counts_ref, buf_ref, out_ref)
 
 
 def alpha_kernel(counts_ref, blocks_ref, types_ref, x_ref, table_ref, out_ref, buf_ref, a_ref, hi_ref, lo_ref):
@@ -253,6 +231,10 @@
         copy.wait()
 
 
+def grant(mib, **kw):
+    return pltpu.CompilerParams(vmem_limit_bytes=mib << 20, **kw)
+
+
 def in_vmem(x):
     return pltpu.with_memory_space_constraint(x, pltpu.VMEM)
 
@@ -279,18 +261,13 @@
     slots = jax.ShapeDtypeStruct((COLS, PACK, 128), f32)
     coeff_slots = pl.pallas_call(
         coeff_kernel,
-        in_specs=[smem(), hbm()],
-        out_specs=hbm(),
+        in_specs=[smem(), vmem()],
+        out_specs=vmem(),
         out_shape=slots,
-        scratch_shapes=[
-            pltpu.VMEM((LOCAL, NA), f32),
-            pltpu.VMEM((COLS, PACK, 128), f32),
-            pltpu.VMEM((ROWS, 256), f32),
-            pltpu.SemaphoreType.DMA((2,)),
-            pltpu.SemaphoreType.DMA((PIECES,)),
-        ],
+        scratch_shapes=[pltpu.VMEM((ROWS, 256), f32)],
         name="coeff_slots",
     )(row_counts, coeffs_t)
+    coeff_slots, alpha_table, beta_table = lax.optimization_barrier((coeff_slots, alpha_table, beta_table))
     alpha_slots = pl.pallas_call(
         alpha_kernel,
         in_specs=[smem(), smem(), smem(), vmem(), vmem()],
@@ -316,6 +293,7 @@
         in_specs=[vmem()],
         out_specs=[vmem(), vmem()],
         out_shape=[jax.ShapeDtypeStruct((BLOCKS, size, 256), bf16) for size in sizes],
+        compiler_params=grant(16),
         name="own_split",
     )(in_vmem(own))
     rest, own_first, own_last = lax.optimization_barrier((own[:, SPLIT:], own_first, own_last))
@@ -331,6 +309,7 @@
             pltpu.VMEM((64, BLK, 128), bf16),
             pltpu.SemaphoreType.DMA((2,)),
         ],
+        compiler_params=grant(24),
         name="beta_first",
     )(blocks, types, own_first, in_vmem(partner_first), tiles)
     return pl.pallas_call(
@@ -345,6 +324,7 @@
             pltpu.SemaphoreType.DMA((3,)),
             pltpu.SemaphoreType.DMA((4,)),
         ],
+        compiler_params=grant(24),
         name="beta_last",
     )(blocks, types, own_last, in_vmem(partner_last), tiles, first, in_vmem(alpha))
 

time: 74.3 us -> 72.6 us (0.977)
  Pallas kernels: 30 us -> 27 us
  waiting for transfers between devices: 16.1 us -> 18.4 us
  local copies, waits for them, and re-layouts: 5.14 us -> 6.26 us
  other arithmetic: 5.86 us -> 4.9 us
  starting transfers between devices: 16.4 us -> 15.5 us
    unnamed x2 -> x10, local copies, waits for them, and re-layouts: 0.01 us -> 2.02 us
    pallas_call x1, Pallas kernels: 4.03 us -> 2.66 us  [on_device(): pl.pallas_call(own_kernel, in_specs=[vmem()], out_specs=[vmem(), vmem()],...]
    pallas_call x1, Pallas kernels: 7.27 us -> 6.23 us  [on_device(): pl.pallas_call(first_kernel, in_specs=[smem(), smem(), hbm(), vmem(), hbm...]
    ppermute x1, waiting for transfers between devices: 1.15 us -> 2.18 us  [on_device(): partner_last = lax.ppermute(rest, 'cls', route)]
    all_to_all x1, waiting for transfers between devices: 1.24 us -> 2.24 us  [on_device(): lax.all_to_all(coeff_slots, 'col', split_axis=0, concat_axis=0, tiled=True)]
    all_to_all x1, starting transfers between devices: 6.15 us -> 5.17 us  [on_device(): lax.all_to_all(alpha_slots, 'col', split_axis=0, concat_axis=0, tiled=True)]
    concatenate x2, other arithmetic: 3.12 us -> 2.16 us  [split_table(): return jnp.concatenate([hi, tiles - hi], 2).astype(bf16)]
    slice x1, local copies, waits for them, and re-layouts: 0.93 us -> 0.05 us  [on_device(): partner_first = lax.ppermute(own[:, :SPLIT], 'cls', route)]
  transfers between devices with their start and end apart: 4 -> 4, of which waited for: 3 -> 3; matrix products, arithmetic and copies ran while one was open for 15% -> 13% of each run, Pallas kernels for 25% -> 22%
where the time goes in v9:
time: 72.6 us; the launch traced here: 72.2 us
  Pallas kernels  27 us (37%)
  waiting for transfers between devices  18.4 us (25%)
  starting transfers between devices  15.5 us (21%)
  local copies, waits for them, and re-layouts  6.26 us (9%)
  other arithmetic  4.9 us (7%)
    ppermute x1, waiting for transfers between devices, on_device(): partner_first = lax.ppermute(own[:, :SPLIT], 'cls', route)  14 us
    all_to_all x1, starting transfers between devices, on_device(): lax.all_to_all(coeff_slots, 'col', split_axis=0, concat_axis=0, tiled=True)  8.58 us
    pallas_call x1, Pallas kernels, on_device(): pl.pallas_call(last_kernel, in_specs=[smem(), smem(), hbm(), vmem(), hbm(...  7.72 us
    pallas_call x1, Pallas kernels, on_device(): pl.pallas_call(alpha_kernel, in_specs=[smem(), smem(), smem(), vmem(), vm...  7.18 us
    pallas_call x1, Pallas kernels, on_device(): pl.pallas_call(first_kernel, in_specs=[smem(), smem(), hbm(), vmem(), hbm...  6.23 us
    all_to_all x1, starting transfers between devices, on_device(): lax.all_to_all(alpha_slots, 'col', split_axis=0, concat_axis=0, tiled=True)  5.17 us
    reshape x2, local copies, waits for them, and re-layouts, split_table(): tiles = table.reshape(table.shape[0], BLK, BLK)  4.16 us
    pallas_call x1, Pallas kernels, on_device(): pl.pallas_call(coeff_kernel, in_specs=[smem(), vmem()], out_specs=vmem(),...  3.19 us
  transfers between devices with their start and end apart: 4, of which 3 were waited for; matrix products, arithmetic and copies ran while one was open for 13% of the time, Pallas kernels for 22%

profile of v9, /device:TPU:1, one launch (start us, length us, event | category | flops | bytes accessed | tf_op | source)
XLA Modules:
  0.0 72.2 jit_solution(4483121561882427272)
XLA Ops:
  0.0 0.0 copy-start.4
  0.0 3.2 %coeff_slots.1 = f32[32,72,128]{2,1,0:T(8,128)} custom-call(s32[32]{0:T(128)} %counts_ref.3, f32[192,1024]{1,0:T(8,128)} %x_ref.3), custom_call_target="tpu_custom_call" | custom-call | tf_op jit(solution)/shard_map/coeff_slots/pallas_call | solution.py:262
  3.2 8.6 %all-to-all-start = ((f32[32,72,128]{2,1,0:T(8,128)}), f32[32,72,128]{2,1,0:T(8,128)S(1)}, u32[]{:S(2)}, u32[]{:S(2)}) async-start(f32[32,72,128]{2,1,0:T(8,128)} %coeff_slots.1), calls=%async_computation | async-start | bytes 2359296 | tf_op jit(solution)/shard_map/all_to_all | solution.py:285
  11.8 0.0 copy-done.4
  11.8 2.2 %reshape.6 = f32[64,64,64]{2,1,0:T(8,128)} reshape(f32[64,4096]{1,0:T(8,128)S(1)} %copy-done.4) | data formatting | bytes 2097152 | tf_op jit(solution)/shard_map/reshape | solution.py:255
  14.0 2.0 %reshape.7 = f32[64,64,64]{2,1,0:T(8,128)S(1)} reshape(f32[64,4096]{1,0:T(8,128)} %param.12) | data formatting | bytes 2097152 | tf_op jit(solution)/shard_map/reshape | solution.py:255
  16.0 2.2 %reduce-precision_convert_fusion.1 = (bf16[64,64,64]{2,1,0:T(8,128)(2,1)S(1)}, bf16[64,64,64]{2,1,0:T(8,128)(2,1)S(1)}) fusion(f32[64,64,64]{2,1,0:T(8,128)} %reshape.6), kind=kLoop, calls=%fused_computation.3 | loop fusion | flops 1048576 | bytes 2097152 | tf_op jit(solution)/shard_map/convert.2
  18.1 1.6 %pad_maximum_fusion.table_ref = bf16[64,64,128]{2,1,0:T(8,128)(2,1)} fusion(bf16[64,64,64]{2,1,0:T(8,128)(2,1)S(1)} %get-tuple-element.30, bf16[64,64,64]{2,1,0:T(8,128)(2,1)S(1)} %get-tuple-element.29), kind=kLoop, calls=%fused_computation.6 | loop fusion | flops 2097152 | bytes 2097152 | tf_op jit(solution)/shard_map/concatenate | solution.py:257
  19.7 7.2 %alpha_slots.1 = f32[32,72,128]{2,1,0:T(8,128)} custom-call(s32[32]{0:T(128)} %counts_ref.3, s32[16,16]{1,0:T(8,128)} %blocks_ref.1, s32[16,16]{1,0:T(8,128)} %types_ref.1, f32[192,1024]{1,0:T(8,128)} %x_ref.3, bf16[64,64,128]{2,1,0:T(8,128)(2,1)} %pad_maximum_fusion.table_ref), custom_call_target="tpu_custom_call" | custom-call | tf_op jit(solution)/shard_map/alpha_slots/pallas_call | solution.py:271
  26.9 0.6 reduce-precision_convert_fusion
  27.5 0.6 pad_maximum_fusion.1.table_hbm
  28.1 2.2 %all-to-all-done.own_ref = f32[32,72,128]{2,1,0:T(8,128)S(1)} async-done(((f32[32,72,128]{2,1,0:T(8,128)}), f32[32,72,128]{2,1,0:T(8,128)S(1)}, u32[]{:S(2)}, u32[]{:S(2)}) %all-to-all-start) | async-done | bytes 1179680 | tf_op jit(solution)/shard_map/all_to_all | solution.py:285
  30.3 5.2 %all-to-all-start.1 = ((f32[32,72,128]{2,1,0:T(8,128)}), f32[32,72,128]{2,1,0:T(8,128)S(1)}, u32[]{:S(2)}, u32[]{:S(2)}) async-start(f32[32,72,128]{2,1,0:T(8,128)} %alpha_slots.1), calls=%async_computation.1 | async-start | bytes 2359296 | tf_op jit(solution)/shard_map/all_to_all | solution.py:289
  35.5 0.0 copy-start.2
  35.5 0.0 copy-start.3
  35.5 0.1 slice.7
  35.6 1.7 %collective-permute-start.1 = (f32[32,48,128]{2,1,0:T(8,128)S(1)}, f32[32,48,128]{2,1,0:T(8,128)S(1)}, u32[]{:S(2)}, u32[]{:S(2)}) collective-permute-start(f32[32,48,128]{2,1,0:T(8,128)S(1)} %slice.7), channel_id=1, source_target_pairs={{0,32},{32,0},{64,96},{96,64},{128,160},{160,128},{192,224},{224,1... | collective-permute-start | bytes 2359304 | tf_op jit(solution)/shard_map/ppermute | solution.py:288
  37.3 2.7 %own_split.1 = (bf16[96,32,256]{2,1,0:T(8,128)(2,1)S(1)}, bf16[96,16,256]{2,1,0:T(8,128)(2,1)S(1)}) custom-call(f32[32,72,128]{2,1,0:T(8,128)S(1)} %all-to-all-done.own_ref), custom_call_target="tpu_custom_call" | custom-call | tf_op jit(solution)/shard_map/own_split/pallas_call | solution.py:291
  40.0 0.0 copy-start
  40.0 0.9 %copy-done = bf16[96,16,256]{2,1,0:T(8,128)(2,1)} copy-done((bf16[96,16,256]{2,1,0:T(8,128)(2,1)}, bf16[96,16,256]{2,1,0:T(8,128)(2,1)S(1)}, u32[]{:S(2)}) %copy-start) | copy-done | bytes 786456
  40.9 0.0 collective-permute-start
  40.9 14.0 %collective-permute-done.1.partner_ref = f32[32,48,128]{2,1,0:T(8,128)S(1)} collective-permute-done((f32[32,48,128]{2,1,0:T(8,128)S(1)}, f32[32,48,128]{2,1,0:T(8,128)S(1)}, u32[]{:S(2)}, u32[]{:S(2)}) %collective-permute-start.1) | collective-permute-done | bytes 786464 | tf_op jit(solution)/shard_map/ppermute | solution.py:288
  54.9 0.0 copy-done.2
  54.9 0.0 copy-done.3
  54.9 6.2 %beta_first.1.first_hbm = f32[32,6144]{1,0:T(8,128)S(1)} custom-call(s32[12,96]{1,0:T(8,128)S(1)} %bitcast.2, s32[12,96]{1,0:T(8,128)S(1)} %bitcast.4, bf16[96,32,256]{2,1,0:T(8,128)(2,1)S(1)} %get-tuple-element.25.own_hbm, f32[32,48,128]{2,1,0:T(8,128)S(1)} %collective-permute-done.1.partner_ref, bf16[64,64,128]{2,1,0:T(8,128)(2,1)S(1)} %pad_maximum_fusion.1.table_hbm), custom_call_target="tpu_custom_call" | custom-call | tf_op jit(solution)/shard_map/beta_first/pallas_call | solution.py:302
  61.1 2.2 %collective-permute-done.partner_ref = f32[32,24,128]{2,1,0:T(8,128)S(1)} collective-permute-done((f32[32,24,128]{2,1,0:T(8,128)S(1)}, f32[32,24,128]{2,1,0:T(8,128)S(1)}, u32[]{:S(2)}, u32[]{:S(2)}) %collective-permute-start) | collective-permute-done | bytes 393248 | tf_op jit(solution)/shard_map/ppermute | solution.py:300
  63.3 0.0 all-to-all-done.1.alpha_ref
  63.3 0.0 copy-start.1
  63.3 1.1 %copy-done.1 = bf16[96,16,256]{2,1,0:T(8,128)(2,1)S(1)} copy-done((bf16[96,16,256]{2,1,0:T(8,128)(2,1)S(1)}, bf16[96,16,256]{2,1,0:T(8,128)(2,1)}, u32[]{:S(2)}) %copy-start.1) | copy-done | bytes 786456
  64.4 7.7 %beta_last.1 = f32[48,6144]{1,0:T(8,128)} custom-call(s32[12,96]{1,0:T(8,128)S(1)} %bitcast.3, s32[12,96]{1,0:T(8,128)S(1)} %bitcast.5, bf16[96,16,256]{2,1,0:T(8,128)(2,1)S(1)} %copy-done.1, f32[32,24,128]{2,1,0:T(8,128)S(1)} %collective-permute-done.partner_ref, bf16[64,64,128]{2,1,0:T(8,128)(2,1)S(1)} %pad_maximum_fusion.1.table_hbm, ...), custom_call_target="tpu_custom_call" | custom-call | tf_op jit(solution)/shard_map/beta_last/pallas_call | solution.py:315
  (1 shorter events, 0.0 us)
Async XLA Ops:
  0.0 11.8 %copy-start.4 = (f32[64,4096]{1,0:T(8,128)S(1)}, f32[64,4096]{1,0:T(8,128)}, u32[]{:S(2)}) copy-start(f32[64,4096]{1,0:T(8,128)} %param.9) | copy-start | bytes 3145732
  3.2 27.1 %all-to-all-start = ((f32[32,72,128]{2,1,0:T(8,128)}), f32[32,72,128]{2,1,0:T(8,128)S(1)}, u32[]{:S(2)}, u32[]{:S(2)}) async-start(f32[32,72,128]{2,1,0:T(8,128)} %coeff_slots.1), calls=%async_computation | async-start | bytes 2359296 | tf_op jit(solution)/shard_map/all_to_all | solution.py:285
  30.3 33.0 %all-to-all-start.1 = ((f32[32,72,128]{2,1,0:T(8,128)}), f32[32,72,128]{2,1,0:T(8,128)S(1)}, u32[]{:S(2)}, u32[]{:S(2)}) async-start(f32[32,72,128]{2,1,0:T(8,128)} %alpha_slots.1), calls=%async_computation.1 | async-start | bytes 2359296 | tf_op jit(solution)/shard_map/all_to_all | solution.py:289
  35.5 19.4 %copy-start.2 = (s32[96,12]{0,1:T(8,128)S(1)}, s32[96,12]{0,1:T(8,128)}, u32[]{:S(2)}) copy-start(s32[96,12]{0,1:T(8,128)} %param.13) | copy-start | bytes 13828
  35.5 19.4 %copy-start.3 = (s32[96,12]{0,1:T(8,128)S(1)}, s32[96,12]{0,1:T(8,128)}, u32[]{:S(2)}) copy-start(s32[96,12]{0,1:T(8,128)} %param.14) | copy-start | bytes 13828
  35.6 19.3 %collective-permute-start.1 = (f32[32,48,128]{2,1,0:T(8,128)S(1)}, f32[32,48,128]{2,1,0:T(8,128)S(1)}, u32[]{:S(2)}, u32[]{:S(2)}) collective-permute-start(f32[32,48,128]{2,1,0:T(8,128)S(1)} %slice.7), channel_id=1, source_target_pairs={{0,32},{32,0},{64,96},{96,64},{128,160},{160,128},{192,224},{224,1... | collective-permute-start | bytes 2359304 | tf_op jit(solution)/shard_map/ppermute | solution.py:288
  40.0 0.9 %copy-start = (bf16[96,16,256]{2,1,0:T(8,128)(2,1)}, bf16[96,16,256]{2,1,0:T(8,128)(2,1)S(1)}, u32[]{:S(2)}) copy-start(bf16[96,16,256]{2,1,0:T(8,128)(2,1)S(1)} %get-tuple-element.22.own_hbm) | copy-start | bytes 2359300
  40.9 22.4 %collective-permute-start = (f32[32,24,128]{2,1,0:T(8,128)S(1)}, f32[32,24,128]{2,1,0:T(8,128)S(1)}, u32[]{:S(2)}, u32[]{:S(2)}) collective-permute-start(f32[32,24,128]{2,1,0:T(8,128)S(1)} %slice.6), channel_id=1, source_target_pairs={{0,32},{32,0},{64,96},{96,64},{128,160},{160,128},{192,224},{224,1... | collective-permute-start | bytes 1179656 | tf_op jit(solution)/shard_map/ppermute | solution.py:300
  63.3 1.1 %copy-start.1 = (bf16[96,16,256]{2,1,0:T(8,128)(2,1)S(1)}, bf16[96,16,256]{2,1,0:T(8,128)(2,1)}, u32[]{:S(2)}) copy-start(bf16[96,16,256]{2,1,0:T(8,128)(2,1)} %copy-done) | copy-start | bytes 2359300

commit v10 on v9

--- a/solution.py
+++ b/solution.py
@@ -19,7 +19,7 @@
 DEPTH = 12
 PARTS = ((0, 32, 0), (32, 16, 48))
 SPLIT = 48
-TRIP = 24
+TRIP = 12
 ROWS = NA + CAP + 8
 
 
@@ -136,12 +136,18 @@
     lax.fori_loop(0, COLS, one, 0, unroll=2)
 
 
-def own_kernel(own_ref, za_ref, zb_ref):
-    for (first, size, at), z_ref in zip(PARTS, (za_ref, zb_ref)):
+def own_kernel(own_ref, za_hbm, zb_hbm, za_ref, zb_ref, sems):
+    copies = []
+    for n, (z_ref, z_hbm) in enumerate(((za_ref, za_hbm), (zb_ref, zb_hbm))):
+        _, size, at = PARTS[n]
         unpack(own_ref, size, at, z_ref, 0)
-
-
-def product(blocks_ref, types_ref, z_ref, table_ref, size, store):
+        copies.append(pltpu.make_async_copy(z_ref, z_hbm, sems.at[n]))
+        copies[n].start()
+    for copy in copies:
+        copy.wait()
+
+
+def product(blocks_ref, types_ref, z_ref, table_ref, size, trip_pairs, store, before=None, after=None):
     pick = left_half((size, 256)) | (lax.broadcasted_iota(jnp.int32, (size, 256), 1) // BLK == 2)
     left = left_half((size, 128))
 
@@ -159,80 +165,86 @@
         return both + swap(both)
 
     def trip(n, carry):
-        for i in range(TRIP):
-            p = n * TRIP + i
+        for i in range(trip_pairs):
+            p = n * trip_pairs + i
             col = pl.ds(pl.multiple_of(p * 128, 128), 128)
-            store(col, jnp.where(left, block(2 * p), block(2 * p + 1)))
+            store(p, i % 3, col, jnp.where(left, block(2 * p), block(2 * p + 1)))
         return carry
 
-    lax.fori_loop(0, BLOCKS // (2 * TRIP), trip, 0)
-
-
-def first_kernel(blocks_ref, types_ref, own_hbm, partner_ref, table_hbm, out_ref, z_ref, table_ref, sems):
+    if before is None:
+        lax.fori_loop(0, BLOCKS // (2 * trip_pairs), trip, 0)
+        return
+    for n in range(BLOCKS // (2 * trip_pairs)):
+        before(n)
+        trip(n, 0)
+        after(n)
+
+
+def first_kernel(blocks_ref, types_ref, own_hbm, partner_ref, table_ref, out_ref, z_ref, sem):
     size = PARTS[0][1]
-    own_copy = pltpu.make_async_copy(own_hbm, z_ref.at[0:BLOCKS], sems.at[0])
-    table_copy = pltpu.make_async_copy(table_hbm, table_ref, sems.at[1])
+    own_copy = pltpu.make_async_copy(own_hbm, z_ref.at[0:BLOCKS], sem)
     own_copy.start()
-    table_copy.start()
     unpack(partner_ref, size, 0, z_ref, BLOCKS)
     own_copy.wait()
-    table_copy.wait()
-
-    def store(col, value):
+
+    def store(p, kind, col, value):
         out_ref[:, col] = value
 
-    product(blocks_ref, types_ref, z_ref, table_ref, size, store)
+    product(blocks_ref, types_ref, z_ref, table_ref, size, 2 * TRIP, store)
+
+
+def alpha_tile(alpha_ref, u, kind, length, at):
+    left = left_half((length, 128))
+    if kind == 0:
+        return alpha_ref[2 * u, at:at + length, :]
+    main = swap(alpha_ref[2 * u + 1, at:at + length, :])
+    low_rows = slice(at + length, at + length + length // 2)
+    if kind == 1:
+        low = alpha_ref[2 * u, low_rows, :]
+        return jnp.where(left, jnp.concatenate([low, swap(low)], 0), main)
+    low = alpha_ref[2 * u + 1, low_rows, :]
+    return jnp.where(left, main, jnp.concatenate([swap(low), low], 0))
 
 
 def last_kernel(
-    blocks_ref, types_ref, own_hbm, partner_ref, table_hbm, first_hbm, alpha_ref, out_hbm,
-    z_ref, table_ref, out_ref, sems, out_sems,
+    blocks_ref, types_ref, own_hbm, partner_ref, table_hbm, first_hbm, alpha_hbm, out_hbm,
+    z_ref, table_ref, alpha_ref, out_ref, sems, in_sems, alpha_sems, out_sems,
 ):
     (_, size_a, at_a), (start, size, at_b) = PARTS
-    own_copy = pltpu.make_async_copy(own_hbm, z_ref.at[0:BLOCKS], sems.at[0])
-    first_copy = pltpu.make_async_copy(first_hbm, out_ref.at[0:start, :], sems.at[1])
-    table_copy = pltpu.make_async_copy(table_hbm, table_ref, sems.at[2])
+    table_copy = pltpu.make_async_copy(table_hbm, table_ref, sems.at[0])
+    own_copy = pltpu.make_async_copy(own_hbm, z_ref.at[0:BLOCKS], sems.at[1])
+    table_copy.start()
     own_copy.start()
-    table_copy.start()
-    first_copy.start()
+    pieces = [slice(TRIP * 128 * n, TRIP * 128 * (n + 1)) for n in range(BLOCKS // (2 * TRIP))]
+    loads, alphas, stores = [], [], []
+    each = COLS // len(pieces)
+    for n, cols in enumerate(pieces):
+        senders = slice(each * n, each * (n + 1))
+        alphas.append(pltpu.make_async_copy(alpha_hbm.at[senders], alpha_ref.at[senders], alpha_sems.at[n]))
+        alphas[n].start()
+        loads.append(pltpu.make_async_copy(first_hbm.at[:, cols], out_ref.at[0:start, cols], in_sems.at[n]))
+        loads[n].start()
     unpack(partner_ref, size, 0, z_ref, BLOCKS)
+    table_copy.wait()
     own_copy.wait()
-    table_copy.wait()
-
-    def store(col, value):
-        out_ref[start:CAP, col] = value
-
-    product(blocks_ref, types_ref, z_ref, table_ref, size, store)
-    first_copy.wait()
-
-    def triple(u, carry):
-        for rows, length, at in ((0, size_a, at_a), (start, size, at_b)):
-            left = left_half((length, 128))
-            a_main, _, a_low, a_low_r = fields(alpha_ref, 2 * u, length, at)
-            _, b_main_r, b_low, b_low_r = fields(alpha_ref, 2 * u + 1, length, at)
-            alphas = (
-                a_main,
-                jnp.where(left, jnp.concatenate([a_low, a_low_r], 0), b_main_r),
-                jnp.where(left, b_main_r, jnp.concatenate([b_low_r, b_low], 0)),
-            )
-            for n in range(3):
-                col = pl.ds(pl.multiple_of(u * 384 + 128 * n, 128), 128)
-                out_ref[rows:rows + length, col] = alphas[n] + out_ref[rows:rows + length, col]
-        return carry
-
-    copies = []
-    for part in range(4):
-        lax.fori_loop(4 * part, 4 * part + 4, triple, 0, unroll=2)
-        cols = slice(1536 * part, 1536 * part + 1536)
-        copy = pltpu.make_async_copy(out_ref.at[:, cols], out_hbm.at[:, cols], out_sems.at[part])
-        copy.start()
-        copies.append(copy)
-    for copy in copies:
+
+    def store(p, kind, col, value):
+        u = p // 3
+        out_ref[0:start, col] = alpha_tile(alpha_ref, u, kind, size_a, at_a) + out_ref[0:start, col]
+        out_ref[start:CAP, col] = alpha_tile(alpha_ref, u, kind, size, at_b) + value
+
+    def before(n):
+        for i in {0: (0,), 1: range(1, len(pieces))}.get(n, ()):
+            loads[i].wait()
+            alphas[i].wait()
+
+    def after(n):
+        stores.append(pltpu.make_async_copy(out_ref.at[:, pieces[n]], out_hbm.at[:, pieces[n]], out_sems.at[n]))
+        stores[n].start()
+
+    product(blocks_ref, types_ref, z_ref, table_ref, size, TRIP, store, before, after)
+    for copy in stores:
         copy.wait()
-
-
-def grant(mib, **kw):
-    return pltpu.CompilerParams(vmem_limit_bytes=mib << 20, **kw)
 
 
 def in_vmem(x):
@@ -291,9 +303,10 @@
     own_first, own_last = pl.pallas_call(
         own_kernel,
         in_specs=[vmem()],
-        out_specs=[vmem(), vmem()],
+        out_specs=[hbm(), hbm()],
         out_shape=[jax.ShapeDtypeStruct((BLOCKS, size, 256), bf16) for size in sizes],
-        compiler_params=grant(16),
+        scratch_shapes=[pltpu.VMEM((BLOCKS, size, 256), bf16) for size in sizes]
+        + [pltpu.SemaphoreType.DMA((2,))],
         name="own_split",
     )(in_vmem(own))
     rest, own_first, own_last = lax.optimization_barrier((own[:, SPLIT:], own_first, own_last))
@@ -301,32 +314,32 @@
     blocks, types = beta_blocks.T, beta_types.T
     first = pl.pallas_call(
         first_kernel,
-        in_specs=[smem(), smem(), hbm(), vmem(), hbm()],
+        in_specs=[smem(), smem(), hbm(), vmem(), vmem()],
         out_specs=vmem(),
         out_shape=jax.ShapeDtypeStruct((sizes[0], BLOCKS * BLK), f32),
         scratch_shapes=[
             pltpu.VMEM((2 * BLOCKS, sizes[0], 256), bf16),
-            pltpu.VMEM((64, BLK, 128), bf16),
-            pltpu.SemaphoreType.DMA((2,)),
+            pltpu.SemaphoreType.DMA,
         ],
-        compiler_params=grant(24),
         name="beta_first",
-    )(blocks, types, own_first, in_vmem(partner_first), tiles)
+    )(blocks, types, own_first, in_vmem(partner_first), in_vmem(tiles))
     return pl.pallas_call(
         last_kernel,
-        in_specs=[smem(), smem(), hbm(), vmem(), hbm(), hbm(), vmem()],
+        in_specs=[smem(), smem(), hbm(), vmem(), hbm(), hbm(), hbm()],
         out_specs=hbm(),
         out_shape=jax.ShapeDtypeStruct((CAP, BLOCKS * BLK), f32),
         scratch_shapes=[
             pltpu.VMEM((2 * BLOCKS, sizes[1], 256), bf16),
             pltpu.VMEM((64, BLK, 128), bf16),
+            pltpu.VMEM((COLS, PACK, 128), f32),
             pltpu.VMEM((CAP, BLOCKS * BLK), f32),
-            pltpu.SemaphoreType.DMA((3,)),
-            pltpu.SemaphoreType.DMA((4,)),
+            pltpu.SemaphoreType.DMA((2,)),
+            pltpu.SemaphoreType.DMA((BLOCKS // (2 * TRIP),)),
+            pltpu.SemaphoreType.DMA((BLOCKS // (2 * TRIP),)),
+            pltpu.SemaphoreType.DMA((BLOCKS // (2 * TRIP),)),
         ],
-        compiler_params=grant(24),
         name="beta_last",
-    )(blocks, types, own_last, in_vmem(partner_last), tiles, first, in_vmem(alpha))
+    )(blocks, types, own_last, in_vmem(partner_last), tiles, first, alpha)
 
 
 def solution(mesh):

time: 72.6 us -> 73.2 us (level)
  Pallas kernels: 27 us -> 28.9 us
  local copies, waits for them, and re-layouts: 6.26 us -> 5.14 us
    unnamed x10 -> x4, local copies, waits for them, and re-layouts: 2.02 us -> 0.01 us
    pallas_call x2, Pallas kernels: 8.89 us -> 10.3 us  [the longest x1 6.69 us: on_device(): pl.pallas_call(first_kernel, in_specs=[smem(), smem(), hbm(), vmem(), vme...]
    slice x1, local copies, waits for them, and re-layouts: 0.05 us -> 0.93 us  [on_device(): partner_first = lax.ppermute(own[:, :SPLIT], 'cls', route)]
  transfers between devices with their start and end apart: 4 -> 4, of which waited for: 3 -> 3; matrix products, arithmetic and copies ran while one was open for 13% -> 14% of each run, Pallas kernels for 22% -> 24%
where the time goes in v10:
time: 73.2 us; the launch traced here: 72.7 us
  Pallas kernels  28.9 us (39%)
  waiting for transfers between devices  17.7 us (24%)
  starting transfers between devices  15.7 us (21%)
  local copies, waits for them, and re-layouts  5.14 us (7%)
  other arithmetic  4.9 us (7%)
    ppermute x1, waiting for transfers between devices, on_device(): partner_first = lax.ppermute(own[:, :SPLIT], 'cls', route)  13.8 us
    all_to_all x1, starting transfers between devices, on_device(): lax.all_to_all(coeff_slots, 'col', split_axis=0, concat_axis=0, tiled=True)  8.58 us
    pallas_call x1, Pallas kernels, on_device(): pl.pallas_call(last_kernel, in_specs=[smem(), smem(), hbm(), vmem(), hbm(...  8.22 us
    pallas_call x1, Pallas kernels, on_device(): pl.pallas_call(alpha_kernel, in_specs=[smem(), smem(), smem(), vmem(), vm...  7.19 us
    pallas_call x1, Pallas kernels, on_device(): pl.pallas_call(first_kernel, in_specs=[smem(), smem(), hbm(), vmem(), vme...  6.69 us
    all_to_all x1, starting transfers between devices, on_device(): lax.all_to_all(alpha_slots, 'col', split_axis=0, concat_axis=0, tiled=True)  5.24 us
    reshape x2, local copies, waits for them, and re-layouts, split_table(): tiles = table.reshape(table.shape[0], BLK, BLK)  4.17 us
    pallas_call x1, Pallas kernels, on_device(): pl.pallas_call(own_kernel, in_specs=[vmem()], out_specs=[hbm(), hbm()], o...  3.6 us
  transfers between devices with their start and end apart: 4, of which 3 were waited for; matrix products, arithmetic and copies ran while one was open for 14% of the time, Pallas kernels for 24%

profile of v10, /device:TPU:1, one launch (start us, length us, event | category | flops | bytes accessed | tf_op | source)
XLA Modules:
  0.0 72.7 jit_solution(142599155096221344)
XLA Ops:
  0.0 0.0 copy-start.1
  0.0 3.2 %coeff_slots.1 = f32[32,72,128]{2,1,0:T(8,128)} custom-call(s32[32]{0:T(128)} %counts_ref.3, f32[192,1024]{1,0:T(8,128)} %x_ref.3), custom_call_target="tpu_custom_call" | custom-call | tf_op jit(solution)/shard_map/coeff_slots/pallas_call | solution.py:274
  3.2 8.6 %all-to-all-start = ((f32[32,72,128]{2,1,0:T(8,128)}), f32[32,72,128]{2,1,0:T(8,128)S(1)}, u32[]{:S(2)}, u32[]{:S(2)}) async-start(f32[32,72,128]{2,1,0:T(8,128)} %coeff_slots.1), calls=%async_computation | async-start | bytes 2359296 | tf_op jit(solution)/shard_map/all_to_all | solution.py:297
  11.8 0.0 copy-done.1
  11.8 2.2 %reshape.6 = f32[64,64,64]{2,1,0:T(8,128)} reshape(f32[64,4096]{1,0:T(8,128)S(1)} %copy-done.1) | data formatting | bytes 2097152 | tf_op jit(solution)/shard_map/reshape | solution.py:267
  14.0 2.0 %reshape.7 = f32[64,64,64]{2,1,0:T(8,128)S(1)} reshape(f32[64,4096]{1,0:T(8,128)} %param.12) | data formatting | bytes 2097152 | tf_op jit(solution)/shard_map/reshape | solution.py:267
  16.0 2.2 %reduce-precision_convert_fusion.1 = (bf16[64,64,64]{2,1,0:T(8,128)(2,1)S(1)}, bf16[64,64,64]{2,1,0:T(8,128)(2,1)S(1)}) fusion(f32[64,64,64]{2,1,0:T(8,128)} %reshape.6), kind=kLoop, calls=%fused_computation.3 | loop fusion | flops 1048576 | bytes 2097152 | tf_op jit(solution)/shard_map/convert.2
  18.1 1.6 %pad_maximum_fusion.table_ref = bf16[64,64,128]{2,1,0:T(8,128)(2,1)} fusion(bf16[64,64,64]{2,1,0:T(8,128)(2,1)S(1)} %get-tuple-element.30, bf16[64,64,64]{2,1,0:T(8,128)(2,1)S(1)} %get-tuple-element.29), kind=kLoop, calls=%fused_computation.6 | loop fusion | flops 2097152 | bytes 2097152 | tf_op jit(solution)/shard_map/concatenate | solution.py:269
  19.7 7.2 %alpha_slots.1 = f32[32,72,128]{2,1,0:T(8,128)} custom-call(s32[32]{0:T(128)} %counts_ref.3, s32[16,16]{1,0:T(8,128)} %blocks_ref.1, s32[16,16]{1,0:T(8,128)} %types_ref.1, f32[192,1024]{1,0:T(8,128)} %x_ref.3, bf16[64,64,128]{2,1,0:T(8,128)(2,1)} %pad_maximum_fusion.table_ref), custom_call_target="tpu_custom_call" | custom-call | tf_op jit(solution)/shard_map/alpha_slots/pallas_call | solution.py:283
  26.9 0.6 reduce-precision_convert_fusion
  27.5 0.6 pad_maximum_fusion.1.table_ref.table_hbm
  28.1 0.0 copy-start
  28.1 2.2 %all-to-all-done.own_ref = f32[32,72,128]{2,1,0:T(8,128)S(1)} async-done(((f32[32,72,128]{2,1,0:T(8,128)}), f32[32,72,128]{2,1,0:T(8,128)S(1)}, u32[]{:S(2)}, u32[]{:S(2)}) %all-to-all-start) | async-done | bytes 1179680 | tf_op jit(solution)/shard_map/all_to_all | solution.py:297
  30.3 5.2 %all-to-all-start.1 = ((f32[32,72,128]{2,1,0:T(8,128)}), f32[32,72,128]{2,1,0:T(8,128)}, u32[]{:S(2)}, u32[]{:S(2)}) async-start(f32[32,72,128]{2,1,0:T(8,128)} %alpha_slots.1), calls=%async_computation.1 | async-start | bytes 2359296 | tf_op jit(solution)/shard_map/all_to_all | solution.py:301
  35.6 0.9 %slice.7 = f32[32,48,128]{2,1,0:T(8,128)} slice(f32[32,72,128]{2,1,0:T(8,128)S(1)} %all-to-all-done.own_ref), slice={[0:32], [0:48], [0:128]} | slice | bytes 1572864 | tf_op jit(solution)/shard_map/slice | solution.py:300
  36.5 1.6 %collective-permute-start.1 = (f32[32,48,128]{2,1,0:T(8,128)}, f32[32,48,128]{2,1,0:T(8,128)S(1)}, u32[]{:S(2)}, u32[]{:S(2)}) collective-permute-start(f32[32,48,128]{2,1,0:T(8,128)} %slice.7), channel_id=1, source_target_pairs={{0,32},{32,0},{64,96},{96,64},{128,160},{160,128},{192,224},{224,1... | collective-permute-start | bytes 2359304 | tf_op jit(solution)/shard_map/ppermute | solution.py:300
  38.2 3.6 %own_split.1 = (bf16[96,32,256]{2,1,0:T(8,128)(2,1)}, bf16[96,16,256]{2,1,0:T(8,128)(2,1)}) custom-call(f32[32,72,128]{2,1,0:T(8,128)S(1)} %all-to-all-done.own_ref), custom_call_target="tpu_custom_call" | custom-call | tf_op jit(solution)/shard_map/own_split/pallas_call | solution.py:303
  41.8 0.3 collective-permute-start
  42.0 13.8 %collective-permute-done.1.partner_ref = f32[32,48,128]{2,1,0:T(8,128)S(1)} collective-permute-done((f32[32,48,128]{2,1,0:T(8,128)}, f32[32,48,128]{2,1,0:T(8,128)S(1)}, u32[]{:S(2)}, u32[]{:S(2)}) %collective-permute-start.1) | collective-permute-done | bytes 786464 | tf_op jit(solution)/shard_map/ppermute | solution.py:300
  55.8 0.0 copy-done
  55.8 6.7 %beta_first.1.first_hbm = f32[32,6144]{1,0:T(8,128)} custom-call(s32[12,96]{1,0:T(8,128)} %bitcast.2, s32[12,96]{1,0:T(8,128)} %bitcast.4, bf16[96,32,256]{2,1,0:T(8,128)(2,1)} %get-tuple-element.25.own_hbm, f32[32,48,128]{2,1,0:T(8,128)S(1)} %collective-permute-done.1.partner_ref, bf16[64,64,128]{2,1,0:T(8,128)(2,1)S(1)} %pad_maximum_fusion.1.table_ref.table_hbm), custom_call_target="tpu_custom_call" | custom-call | tf_op jit(solution)/shard_map/beta_first/pallas_call | solution.py:315
  62.5 1.7 %collective-permute-done.partner_ref = f32[32,24,128]{2,1,0:T(8,128)S(1)} collective-permute-done((f32[32,24,128]{2,1,0:T(8,128)S(1)}, f32[32,24,128]{2,1,0:T(8,128)S(1)}, u32[]{:S(2)}, u32[]{:S(2)}) %collective-permute-start) | collective-permute-done | bytes 393248 | tf_op jit(solution)/shard_map/ppermute | solution.py:313
  64.3 0.0 all-to-all-done.1.alpha_hbm
  64.3 8.2 %beta_last.1 = f32[48,6144]{1,0:T(8,128)} custom-call(s32[12,96]{1,0:T(8,128)} %bitcast.3, s32[12,96]{1,0:T(8,128)} %bitcast.5, bf16[96,16,256]{2,1,0:T(8,128)(2,1)} %get-tuple-element.22.own_hbm, f32[32,24,128]{2,1,0:T(8,128)S(1)} %collective-permute-done.partner_ref, bf16[64,64,128]{2,1,0:T(8,128)(2,1)} %copy-done, f32[32,6144]{1,0:T(8,128)} %beta_first.1.first_hbm, ...), custom_call_target="tpu_custom_call" | custom-call | tf_op jit(solution)/shard_map/beta_last/pallas_call | solution.py:326
  (1 shorter events, 0.0 us)
Async XLA Ops:
  0.0 11.8 %copy-start.1 = (f32[64,4096]{1,0:T(8,128)S(1)}, f32[64,4096]{1,0:T(8,128)}, u32[]{:S(2)}) copy-start(f32[64,4096]{1,0:T(8,128)} %param.9) | copy-start | bytes 3145732
  3.2 27.1 %all-to-all-start = ((f32[32,72,128]{2,1,0:T(8,128)}), f32[32,72,128]{2,1,0:T(8,128)S(1)}, u32[]{:S(2)}, u32[]{:S(2)}) async-start(f32[32,72,128]{2,1,0:T(8,128)} %coeff_slots.1), calls=%async_computation | async-start | bytes 2359296 | tf_op jit(solution)/shard_map/all_to_all | solution.py:297
  28.1 27.8 %copy-start = (bf16[64,64,128]{2,1,0:T(8,128)(2,1)}, bf16[64,64,128]{2,1,0:T(8,128)(2,1)S(1)}, u32[]{:S(2)}) copy-start(bf16[64,64,128]{2,1,0:T(8,128)(2,1)S(1)} %pad_maximum_fusion.1.table_ref.table_hbm) | copy-start | bytes 3145732
  30.3 34.0 %all-to-all-start.1 = ((f32[32,72,128]{2,1,0:T(8,128)}), f32[32,72,128]{2,1,0:T(8,128)}, u32[]{:S(2)}, u32[]{:S(2)}) async-start(f32[32,72,128]{2,1,0:T(8,128)} %alpha_slots.1), calls=%async_computation.1 | async-start | bytes 2359296 | tf_op jit(solution)/shard_map/all_to_all | solution.py:301
  36.5 19.4 %collective-permute-start.1 = (f32[32,48,128]{2,1,0:T(8,128)}, f32[32,48,128]{2,1,0:T(8,128)S(1)}, u32[]{:S(2)}, u32[]{:S(2)}) collective-permute-start(f32[32,48,128]{2,1,0:T(8,128)} %slice.7), channel_id=1, source_target_pairs={{0,32},{32,0},{64,96},{96,64},{128,160},{160,128},{192,224},{224,1... | collective-permute-start | bytes 2359304 | tf_op jit(solution)/shard_map/ppermute | solution.py:300
  41.8 22.5 %collective-permute-start = (f32[32,24,128]{2,1,0:T(8,128)S(1)}, f32[32,24,128]{2,1,0:T(8,128)S(1)}, u32[]{:S(2)}, u32[]{:S(2)}) collective-permute-start(f32[32,24,128]{2,1,0:T(8,128)S(1)} %slice.6), channel_id=1, source_target_pairs={{0,32},{32,0},{64,96},{96,64},{128,160},{160,128},{192,224},{224,1... | collective-permute-start | bytes 1179656 | tf_op jit(solution)/shard_map/ppermute | solution.py:313

commit v11 on v10

--- a/solution.py
+++ b/solution.py
@@ -180,12 +180,18 @@
         after(n)
 
 
-def first_kernel(blocks_ref, types_ref, own_hbm, partner_ref, table_ref, out_ref, z_ref, sem):
+def first_kernel(blocks_ref, types_ref, own_hbm, partner_hbm, table_hbm, out_ref, z_ref, partner_ref, table_ref, sems):
     size = PARTS[0][1]
-    own_copy = pltpu.make_async_copy(own_hbm, z_ref.at[0:BLOCKS], sem)
+    partner_copy = pltpu.make_async_copy(partner_hbm, partner_ref, sems.at[0])
+    own_copy = pltpu.make_async_copy(own_hbm, z_ref.at[0:BLOCKS], sems.at[1])
+    table_copy = pltpu.make_async_copy(table_hbm, table_ref, sems.at[2])
+    partner_copy.start()
     own_copy.start()
+    table_copy.start()
+    partner_copy.wait()
     unpack(partner_ref, size, 0, z_ref, BLOCKS)
     own_copy.wait()
+    table_copy.wait()
 
     def store(p, kind, col, value):
         out_ref[:, col] = value
@@ -293,9 +299,8 @@
         ],
         name="alpha_slots",
     )(row_counts, alpha_blocks, alpha_types, coeffs_t, split_table(alpha_table))
-    tiles = split_table(beta_table)
     own = lax.all_to_all(coeff_slots, "col", split_axis=0, concat_axis=0, tiled=True)
-    own, alpha_slots, tiles = lax.optimization_barrier((own, alpha_slots, tiles))
+    own, alpha_slots = lax.optimization_barrier((own, alpha_slots))
     route = [(i, i ^ 1) for i in range(8)]
     partner_first = lax.ppermute(own[:, :SPLIT], "cls", route)
     alpha = lax.all_to_all(alpha_slots, "col", split_axis=0, concat_axis=0, tiled=True)
@@ -309,20 +314,25 @@
         + [pltpu.SemaphoreType.DMA((2,))],
         name="own_split",
     )(in_vmem(own))
-    rest, own_first, own_last = lax.optimization_barrier((own[:, SPLIT:], own_first, own_last))
+    rest, own_first, own_last, beta_table = lax.optimization_barrier(
+        (own[:, SPLIT:], own_first, own_last, beta_table)
+    )
+    tiles = split_table(beta_table)
     partner_last = lax.ppermute(rest, "cls", route)
     blocks, types = beta_blocks.T, beta_types.T
     first = pl.pallas_call(
         first_kernel,
-        in_specs=[smem(), smem(), hbm(), vmem(), vmem()],
+        in_specs=[smem(), smem(), hbm(), hbm(), hbm()],
         out_specs=vmem(),
         out_shape=jax.ShapeDtypeStruct((sizes[0], BLOCKS * BLK), f32),
         scratch_shapes=[
             pltpu.VMEM((2 * BLOCKS, sizes[0], 256), bf16),
-            pltpu.SemaphoreType.DMA,
+            pltpu.VMEM((COLS, SPLIT, 128), f32),
+            pltpu.VMEM((64, BLK, 128), bf16),
+            pltpu.SemaphoreType.DMA((3,)),
         ],
         name="beta_first",
-    )(blocks, types, own_first, in_vmem(partner_first), in_vmem(tiles))
+    )(blocks, types, own_first, partner_first, tiles)
     return pl.pallas_call(
         last_kernel,
         in_specs=[smem(), smem(), hbm(), vmem(), hbm(), hbm(), hbm()],

time: 73.2 us -> 72.6 us (level)
  Pallas kernels: 28.9 us -> 30.2 us
    all_to_all x1, waiting for transfers between devices: 2.21 us -> 7.18 us  [on_device(): lax.all_to_all(coeff_slots, 'col', split_axis=0, concat_axis=0, tiled=True)]
    ppermute x1, waiting for transfers between devices: 13.8 us -> 10.1 us  [on_device(): partner_first = lax.ppermute(own[:, :SPLIT], 'cls', route)]
    another operation x2, other arithmetic: 2.74 us -> 1.15 us
    ppermute x1, waiting for transfers between devices: 1.73 us -> 0.2 us  [on_device(): partner_last = lax.ppermute(rest, 'cls', route)]
    pallas_call x1, Pallas kernels: 6.69 us -> 8.12 us  [on_device(): pl.pallas_call(first_kernel, in_specs=[smem(), smem(), hbm(), hbm(), hbm(...]
    reshape x2, local copies, waits for them, and re-layouts: 4.17 us -> 2.84 us  [split_table(): tiles = table.reshape(table.shape[0], BLK, BLK)]
    concatenate x2, other arithmetic: 2.16 us -> 3.12 us  [split_table(): return jnp.concatenate([hi, tiles - hi], 2).astype(bf16)]
    slice x1, local copies, waits for them, and re-layouts: 0.03 us -> 0.76 us  [on_device(): own[:, SPLIT:]]
  transfers between devices with their start and end apart: 4 -> 4, of which waited for: 3 -> 3; matrix products, arithmetic and copies ran while one was open for 14% -> 12% of each run, Pallas kernels for 24% -> 26%
where the time goes in v11:
time: 72.6 us; the launch traced here: 71.9 us
  Pallas kernels  30.2 us (42%)
  waiting for transfers between devices  17.5 us (24%)
  starting transfers between devices  15.1 us (21%)
  local copies, waits for them, and re-layouts  4.54 us (6%)
  other arithmetic  4.27 us (6%)
    ppermute x1, waiting for transfers between devices, on_device(): partner_first = lax.ppermute(own[:, :SPLIT], 'cls', route)  10.1 us
    all_to_all x1, starting transfers between devices, on_device(): lax.all_to_all(coeff_slots, 'col', split_axis=0, concat_axis=0, tiled=True)  8.58 us
    pallas_call x1, Pallas kernels, on_device(): pl.pallas_call(last_kernel, in_specs=[smem(), smem(), hbm(), vmem(), hbm(...  8.24 us
    pallas_call x1, Pallas kernels, on_device(): pl.pallas_call(first_kernel, in_specs=[smem(), smem(), hbm(), hbm(), hbm(...  8.12 us
    pallas_call x1, Pallas kernels, on_device(): pl.pallas_call(alpha_kernel, in_specs=[smem(), smem(), smem(), vmem(), vm...  7.2 us
    all_to_all x1, waiting for transfers between devices, on_device(): lax.all_to_all(coeff_slots, 'col', split_axis=0, concat_axis=0, tiled=True)  7.18 us
    all_to_all x1, starting transfers between devices, on_device(): lax.all_to_all(alpha_slots, 'col', split_axis=0, concat_axis=0, tiled=True)  4.64 us
    pallas_call x1, Pallas kernels, on_device(): pl.pallas_call(own_kernel, in_specs=[vmem()], out_specs=[hbm(), hbm()], o...  3.58 us
  transfers between devices with their start and end apart: 4, of which 3 were waited for; matrix products, arithmetic and copies ran while one was open for 12% of the time, Pallas kernels for 26%

profile of v11, /device:TPU:1, one launch (start us, length us, event | category | flops | bytes accessed | tf_op | source)
XLA Modules:
  0.0 71.9 jit_solution(15850296422592653516)
XLA Ops:
  0.0 3.1 %coeff_slots.1 = f32[32,72,128]{2,1,0:T(8,128)} custom-call(s32[32]{0:T(128)} %counts_ref.3, f32[192,1024]{1,0:T(8,128)} %x_ref.3), custom_call_target="tpu_custom_call" | custom-call | tf_op jit(solution)/shard_map/coeff_slots/pallas_call | solution.py:280
  3.1 8.6 %all-to-all-start = ((f32[32,72,128]{2,1,0:T(8,128)}), f32[32,72,128]{2,1,0:T(8,128)S(1)}, u32[]{:S(2)}, u32[]{:S(2)}) async-start(f32[32,72,128]{2,1,0:T(8,128)} %coeff_slots.1), calls=%async_computation | async-start | bytes 2359296 | tf_op jit(solution)/shard_map/all_to_all | solution.py:302
  11.7 2.0 %reshape.6 = f32[64,64,64]{2,1,0:T(8,128)S(1)} reshape(f32[64,4096]{1,0:T(8,128)} %param.9) | data formatting | bytes 2097152 | tf_op jit(solution)/shard_map/reshape | solution.py:273
  13.7 0.6 reduce-precision_convert_fusion.1
  14.3 1.6 %pad_maximum_fusion.table_ref = bf16[64,64,128]{2,1,0:T(8,128)(2,1)} fusion(bf16[64,64,64]{2,1,0:T(8,128)(2,1)S(1)} %get-tuple-element.30, bf16[64,64,64]{2,1,0:T(8,128)(2,1)S(1)} %get-tuple-element.29), kind=kLoop, calls=%fused_computation.6 | loop fusion | flops 2097152 | bytes 2097152 | tf_op jit(solution)/shard_map/concatenate | solution.py:275
  15.8 7.2 %alpha_slots.1 = f32[32,72,128]{2,1,0:T(8,128)} custom-call(s32[32]{0:T(128)} %counts_ref.3, s32[16,16]{1,0:T(8,128)} %blocks_ref.1, s32[16,16]{1,0:T(8,128)} %types_ref.1, f32[192,1024]{1,0:T(8,128)} %x_ref.3, bf16[64,64,128]{2,1,0:T(8,128)(2,1)} %pad_maximum_fusion.table_ref), custom_call_target="tpu_custom_call" | custom-call | tf_op jit(solution)/shard_map/alpha_slots/pallas_call | solution.py:289
  23.0 7.2 %all-to-all-done.own_ref = f32[32,72,128]{2,1,0:T(8,128)S(1)} async-done(((f32[32,72,128]{2,1,0:T(8,128)}), f32[32,72,128]{2,1,0:T(8,128)S(1)}, u32[]{:S(2)}, u32[]{:S(2)}) %all-to-all-start) | async-done | bytes 1179680 | tf_op jit(solution)/shard_map/all_to_all | solution.py:302
  30.2 4.6 %all-to-all-start.1 = ((f32[32,72,128]{2,1,0:T(8,128)}), f32[32,72,128]{2,1,0:T(8,128)}, u32[]{:S(2)}, u32[]{:S(2)}) async-start(f32[32,72,128]{2,1,0:T(8,128)} %alpha_slots.1), calls=%async_computation.1 | async-start | bytes 2359296 | tf_op jit(solution)/shard_map/all_to_all | solution.py:306
  34.9 0.0 copy-start
  34.9 0.9 %slice.7 = f32[32,48,128]{2,1,0:T(8,128)} slice(f32[32,72,128]{2,1,0:T(8,128)S(1)} %all-to-all-done.own_ref), slice={[0:32], [0:48], [0:128]} | slice | bytes 1572864 | tf_op jit(solution)/shard_map/slice | solution.py:305
  35.8 1.6 %collective-permute-start.1 = (f32[32,48,128]{2,1,0:T(8,128)}, f32[32,48,128]{2,1,0:T(8,128)}, u32[]{:S(2)}, u32[]{:S(2)}) collective-permute-start(f32[32,48,128]{2,1,0:T(8,128)} %slice.7), channel_id=1, source_target_pairs={{0,32},{32,0},{64,96},{96,64},{128,160},{160,128},{192,224},{224,1... | collective-permute-start | bytes 2359304 | tf_op jit(solution)/shard_map/ppermute | solution.py:305
  37.5 0.8 %slice.6 = f32[32,24,128]{2,1,0:T(8,128)} slice(f32[32,72,128]{2,1,0:T(8,128)S(1)} %all-to-all-done.own_ref), slice={[0:32], [48:72], [0:128]} | slice | bytes 786432 | tf_op jit(solution)/shard_map/slice | solution.py:318
  38.2 3.6 %own_split.1 = (bf16[96,32,256]{2,1,0:T(8,128)(2,1)}, bf16[96,16,256]{2,1,0:T(8,128)(2,1)}) custom-call(f32[32,72,128]{2,1,0:T(8,128)S(1)} %all-to-all-done.own_ref), custom_call_target="tpu_custom_call" | custom-call | tf_op jit(solution)/shard_map/own_split/pallas_call | solution.py:308
  41.8 0.3 collective-permute-start
  42.1 0.0 copy-done
  42.1 0.8 %reshape.7 = f32[64,64,64]{2,1,0:T(8,128)S(1)} reshape(f32[64,4096]{1,0:T(8,128)S(1)} %copy-done) | data formatting | bytes 2097152 | tf_op jit(solution)/shard_map/reshape | solution.py:273
  42.9 0.6 reduce-precision_convert_fusion
  43.5 1.6 %pad_maximum_fusion.1.table_hbm = bf16[64,64,128]{2,1,0:T(8,128)(2,1)} fusion(bf16[64,64,64]{2,1,0:T(8,128)(2,1)S(1)} %get-tuple-element.28, bf16[64,64,64]{2,1,0:T(8,128)(2,1)S(1)} %get-tuple-element.27), kind=kLoop, calls=%fused_computation.7 | loop fusion | flops 2097152 | bytes 2097152 | tf_op jit(solution)/shard_map/concatenate | solution.py:275
  45.1 10.1 %collective-permute-done.1.partner_hbm = f32[32,48,128]{2,1,0:T(8,128)} collective-permute-done((f32[32,48,128]{2,1,0:T(8,128)}, f32[32,48,128]{2,1,0:T(8,128)}, u32[]{:S(2)}, u32[]{:S(2)}) %collective-permute-start.1) | collective-permute-done | bytes 786464 | tf_op jit(solution)/shard_map/ppermute | solution.py:305
  55.2 8.1 %beta_first.1.first_hbm = f32[32,6144]{1,0:T(8,128)} custom-call(s32[12,96]{1,0:T(8,128)} %bitcast.2, s32[12,96]{1,0:T(8,128)} %bitcast.4, bf16[96,32,256]{2,1,0:T(8,128)(2,1)} %get-tuple-element.25.own_hbm, f32[32,48,128]{2,1,0:T(8,128)} %collective-permute-done.1.partner_hbm, bf16[64,64,128]{2,1,0:T(8,128)(2,1)} %pad_maximum_fusion.1.table_hbm), custom_call_target="tpu_custom_call" | custom-call | tf_op jit(solution)/shard_map/beta_first/pallas_call | solution.py:323
  63.3 0.2 collective-permute-done.partner_ref
  63.5 0.0 all-to-all-done.1.alpha_hbm
  63.5 8.2 %beta_last.1 = f32[48,6144]{1,0:T(8,128)} custom-call(s32[12,96]{1,0:T(8,128)} %bitcast.3, s32[12,96]{1,0:T(8,128)} %bitcast.5, bf16[96,16,256]{2,1,0:T(8,128)(2,1)} %get-tuple-element.22.own_hbm, f32[32,24,128]{2,1,0:T(8,128)S(1)} %collective-permute-done.partner_ref, bf16[64,64,128]{2,1,0:T(8,128)(2,1)} %pad_maximum_fusion.1.table_hbm, ...), custom_call_target="tpu_custom_call" | custom-call | tf_op jit(solution)/shard_map/beta_last/pallas_call | solution.py:336
Async XLA Ops:
  3.1 27.1 %all-to-all-start = ((f32[32,72,128]{2,1,0:T(8,128)}), f32[32,72,128]{2,1,0:T(8,128)S(1)}, u32[]{:S(2)}, u32[]{:S(2)}) async-start(f32[32,72,128]{2,1,0:T(8,128)} %coeff_slots.1), calls=%async_computation | async-start | bytes 2359296 | tf_op jit(solution)/shard_map/all_to_all | solution.py:302
  30.2 33.3 %all-to-all-start.1 = ((f32[32,72,128]{2,1,0:T(8,128)}), f32[32,72,128]{2,1,0:T(8,128)}, u32[]{:S(2)}, u32[]{:S(2)}) async-start(f32[32,72,128]{2,1,0:T(8,128)} %alpha_slots.1), calls=%async_computation.1 | async-start | bytes 2359296 | tf_op jit(solution)/shard_map/all_to_all | solution.py:306
  34.9 7.2 %copy-start = (f32[64,4096]{1,0:T(8,128)S(1)}, f32[64,4096]{1,0:T(8,128)}, u32[]{:S(2)}) copy-start(f32[64,4096]{1,0:T(8,128)} %param.12) | copy-start | bytes 3145732
  35.8 19.3 %collective-permute-start.1 = (f32[32,48,128]{2,1,0:T(8,128)}, f32[32,48,128]{2,1,0:T(8,128)}, u32[]{:S(2)}, u32[]{:S(2)}) collective-permute-start(f32[32,48,128]{2,1,0:T(8,128)} %slice.7), channel_id=1, source_target_pairs={{0,32},{32,0},{64,96},{96,64},{128,160},{160,128},{192,224},{224,1... | collective-permute-start | bytes 2359304 | tf_op jit(solution)/shard_map/ppermute | solution.py:305
  41.8 21.7 %collective-permute-start = (f32[32,24,128]{2,1,0:T(8,128)}, f32[32,24,128]{2,1,0:T(8,128)S(1)}, u32[]{:S(2)}, u32[]{:S(2)}) collective-permute-start(f32[32,24,128]{2,1,0:T(8,128)} %slice.6), channel_id=1, source_target_pairs={{0,32},{32,0},{64,96},{96,64},{128,160},{160,128},{192,224},{224,1... | collective-permute-start | bytes 1179656 | tf_op jit(solution)/shard_map/ppermute | solution.py:321

commit v12 on v10

--- a/solution.py
+++ b/solution.py
@@ -207,13 +207,11 @@
 
 
 def last_kernel(
-    blocks_ref, types_ref, own_hbm, partner_ref, table_hbm, first_hbm, alpha_hbm, out_hbm,
-    z_ref, table_ref, alpha_ref, out_ref, sems, in_sems, alpha_sems, out_sems,
+    blocks_ref, types_ref, own_ref, partner_ref, table_ref, first_hbm, alpha_hbm, out_hbm,
+    z_ref, alpha_ref, out_ref, sem, in_sems, alpha_sems, out_sems,
 ):
     (_, size_a, at_a), (start, size, at_b) = PARTS
-    table_copy = pltpu.make_async_copy(table_hbm, table_ref, sems.at[0])
-    own_copy = pltpu.make_async_copy(own_hbm, z_ref.at[0:BLOCKS], sems.at[1])
-    table_copy.start()
+    own_copy = pltpu.make_async_copy(own_ref, z_ref.at[0:BLOCKS], sem)
     own_copy.start()
     pieces = [slice(TRIP * 128 * n, TRIP * 128 * (n + 1)) for n in range(BLOCKS // (2 * TRIP))]
     loads, alphas, stores = [], [], []
@@ -225,7 +223,6 @@
         loads.append(pltpu.make_async_copy(first_hbm.at[:, cols], out_ref.at[0:start, cols], in_sems.at[n]))
         loads[n].start()
     unpack(partner_ref, size, 0, z_ref, BLOCKS)
-    table_copy.wait()
     own_copy.wait()
 
     def store(p, kind, col, value):
@@ -245,6 +242,10 @@
     product(blocks_ref, types_ref, z_ref, table_ref, size, TRIP, store, before, after)
     for copy in stores:
         copy.wait()
+
+
+def grant(mib, **kw):
+    return pltpu.CompilerParams(vmem_limit_bytes=mib << 20, **kw)
 
 
 def in_vmem(x):
@@ -293,9 +294,8 @@
         ],
         name="alpha_slots",
     )(row_counts, alpha_blocks, alpha_types, coeffs_t, split_table(alpha_table))
-    tiles = split_table(beta_table)
     own = lax.all_to_all(coeff_slots, "col", split_axis=0, concat_axis=0, tiled=True)
-    own, alpha_slots, tiles = lax.optimization_barrier((own, alpha_slots, tiles))
+    own, alpha_slots = lax.optimization_barrier((own, alpha_slots))
     route = [(i, i ^ 1) for i in range(8)]
     partner_first = lax.ppermute(own[:, :SPLIT], "cls", route)
     alpha = lax.all_to_all(alpha_slots, "col", split_axis=0, concat_axis=0, tiled=True)
@@ -309,7 +309,10 @@
         + [pltpu.SemaphoreType.DMA((2,))],
         name="own_split",
     )(in_vmem(own))
-    rest, own_first, own_last = lax.optimization_barrier((own[:, SPLIT:], own_first, own_last))
+    rest, own_first, own_last, beta_table = lax.optimization_barrier(
+        (own[:, SPLIT:], own_first, own_last, beta_table)
+    )
+    tiles = split_table(beta_table)
     partner_last = lax.ppermute(rest, "cls", route)
     blocks, types = beta_blocks.T, beta_types.T
     first = pl.pallas_call(
@@ -321,25 +324,25 @@
             pltpu.VMEM((2 * BLOCKS, sizes[0], 256), bf16),
             pltpu.SemaphoreType.DMA,
         ],
+        compiler_params=grant(24),
         name="beta_first",
     )(blocks, types, own_first, in_vmem(partner_first), in_vmem(tiles))
     return pl.pallas_call(
         last_kernel,
-        in_specs=[smem(), smem(), hbm(), vmem(), hbm(), hbm(), hbm()],
+        in_specs=[smem(), smem(), vmem(), vmem(), vmem(), hbm(), hbm()],
         out_specs=hbm(),
         out_shape=jax.ShapeDtypeStruct((CAP, BLOCKS * BLK), f32),
         scratch_shapes=[
             pltpu.VMEM((2 * BLOCKS, sizes[1], 256), bf16),
-            pltpu.VMEM((64, BLK, 128), bf16),
             pltpu.VMEM((COLS, PACK, 128), f32),
             pltpu.VMEM((CAP, BLOCKS * BLK), f32),
-            pltpu.SemaphoreType.DMA((2,)),
+            pltpu.SemaphoreType.DMA,
             pltpu.SemaphoreType.DMA((BLOCKS // (2 * TRIP),)),
             pltpu.SemaphoreType.DMA((BLOCKS // (2 * TRIP),)),
             pltpu.SemaphoreType.DMA((BLOCKS // (2 * TRIP),)),
         ],
         name="beta_last",
-    )(blocks, types, own_last, in_vmem(partner_last), tiles, first, alpha)
+    )(blocks, types, in_vmem(own_last), in_vmem(partner_last), in_vmem(tiles), first, alpha)
 
 
 def solution(mesh):

time: 73.2 us -> 71.6 us (0.978)
  waiting for transfers between devices: 17.7 us -> 15.1 us
  local copies, waits for them, and re-layouts: 5.14 us -> 7 us
  Pallas kernels: 28.9 us -> 27.2 us
  other arithmetic: 4.9 us -> 6.5 us
    ppermute x1, waiting for transfers between devices: 13.8 us -> 7.99 us  [on_device(): partner_first = lax.ppermute(own[:, :SPLIT], 'cls', route)]
    all_to_all x1, waiting for transfers between devices: 2.21 us -> 5.4 us  [on_device(): lax.all_to_all(coeff_slots, 'col', split_axis=0, concat_axis=0, tiled=True)]
    another operation x2, other arithmetic: 2.74 us -> 4.33 us
    pallas_call x1, Pallas kernels: 6.69 us -> 5.76 us  [on_device(): pl.pallas_call(first_kernel, in_specs=[smem(), smem(), hbm(), vmem(), vme...]
    unnamed x4 -> x14, local copies, waits for them, and re-layouts: 0.01 us -> 0.93 us
    pallas_call x1, Pallas kernels: 8.22 us -> 7.45 us  [on_device(): pl.pallas_call(last_kernel, in_specs=[smem(), smem(), vmem(), vmem(), vme...]
    slice x1, local copies, waits for them, and re-layouts: 0.03 us -> 0.78 us  [on_device(): own[:, SPLIT:]]
  transfers between devices with their start and end apart: 4 -> 4, of which waited for: 3 -> 3; matrix products, arithmetic and copies ran while one was open for 14% -> 18% of each run, Pallas kernels for 24% -> 23%
where the time goes in v12:
time: 71.6 us; the launch traced here: 71.2 us
  Pallas kernels  27.2 us (38%)
  starting transfers between devices  15.1 us (21%)
  waiting for transfers between devices  15.1 us (21%)
  local copies, waits for them, and re-layouts  7 us (10%)
  other arithmetic  6.5 us (9%)
    all_to_all x1, starting transfers between devices, on_device(): lax.all_to_all(coeff_slots, 'col', split_axis=0, concat_axis=0, tiled=True)  8.58 us
    ppermute x1, waiting for transfers between devices, on_device(): partner_first = lax.ppermute(own[:, :SPLIT], 'cls', route)  7.99 us
    pallas_call x1, Pallas kernels, on_device(): pl.pallas_call(last_kernel, in_specs=[smem(), smem(), vmem(), vmem(), vme...  7.45 us
    pallas_call x1, Pallas kernels, on_device(): pl.pallas_call(alpha_kernel, in_specs=[smem(), smem(), smem(), vmem(), vm...  7.2 us
    pallas_call x1, Pallas kernels, on_device(): pl.pallas_call(first_kernel, in_specs=[smem(), smem(), hbm(), vmem(), vme...  5.76 us
    all_to_all x1, waiting for transfers between devices, on_device(): lax.all_to_all(coeff_slots, 'col', split_axis=0, concat_axis=0, tiled=True)  5.4 us
    all_to_all x1, starting transfers between devices, on_device(): lax.all_to_all(alpha_slots, 'col', split_axis=0, concat_axis=0, tiled=True)  4.64 us
    reshape x2, local copies, waits for them, and re-layouts, split_table(): tiles = table.reshape(table.shape[0], BLK, BLK)  4.34 us
  transfers between devices with their start and end apart: 4, of which 3 were waited for; matrix products, arithmetic and copies ran while one was open for 18% of the time, Pallas kernels for 23%

profile of v12, /device:TPU:1, one launch (start us, length us, event | category | flops | bytes accessed | tf_op | source)
XLA Modules:
  0.0 71.2 jit_solution(53291933421994414)
XLA Ops:
  0.0 0.0 copy-start.5
  0.0 3.2 %coeff_slots.1 = f32[32,72,128]{2,1,0:T(8,128)} custom-call(s32[32]{0:T(128)} %counts_ref.3, f32[192,1024]{1,0:T(8,128)} %x_ref.3), custom_call_target="tpu_custom_call" | custom-call | tf_op jit(solution)/shard_map/coeff_slots/pallas_call | solution.py:275
  3.2 8.6 %all-to-all-start = ((f32[32,72,128]{2,1,0:T(8,128)}), f32[32,72,128]{2,1,0:T(8,128)S(1)}, u32[]{:S(2)}, u32[]{:S(2)}) async-start(f32[32,72,128]{2,1,0:T(8,128)} %coeff_slots.1), calls=%async_computation | async-start | bytes 2359296 | tf_op jit(solution)/shard_map/all_to_all | solution.py:297
  11.8 0.0 copy-done.5
  11.8 2.2 %reshape.6 = f32[64,64,64]{2,1,0:T(8,128)} reshape(f32[64,4096]{1,0:T(8,128)S(1)} %copy-done.5) | data formatting | bytes 2097152 | tf_op jit(solution)/shard_map/reshape | solution.py:268
  14.0 2.2 %reduce-precision_convert_fusion.1 = (bf16[64,64,64]{2,1,0:T(8,128)(2,1)S(1)}, bf16[64,64,64]{2,1,0:T(8,128)(2,1)S(1)}) fusion(f32[64,64,64]{2,1,0:T(8,128)} %reshape.6), kind=kLoop, calls=%fused_computation.3 | loop fusion | flops 1048576 | bytes 2097152 | tf_op jit(solution)/shard_map/convert.2
  16.1 1.6 %pad_maximum_fusion.table_ref = bf16[64,64,128]{2,1,0:T(8,128)(2,1)} fusion(bf16[64,64,64]{2,1,0:T(8,128)(2,1)S(1)} %get-tuple-element.30, bf16[64,64,64]{2,1,0:T(8,128)(2,1)S(1)} %get-tuple-element.29), kind=kLoop, calls=%fused_computation.6 | loop fusion | flops 2097152 | bytes 2097152 | tf_op jit(solution)/shard_map/concatenate | solution.py:270
  17.7 7.2 %alpha_slots.1 = f32[32,72,128]{2,1,0:T(8,128)} custom-call(s32[32]{0:T(128)} %counts_ref.3, s32[16,16]{1,0:T(8,128)} %blocks_ref.1, s32[16,16]{1,0:T(8,128)} %types_ref.1, f32[192,1024]{1,0:T(8,128)} %x_ref.3, bf16[64,64,128]{2,1,0:T(8,128)(2,1)} %pad_maximum_fusion.table_ref), custom_call_target="tpu_custom_call" | custom-call | tf_op jit(solution)/shard_map/alpha_slots/pallas_call | solution.py:284
  24.9 5.4 %all-to-all-done.own_ref = f32[32,72,128]{2,1,0:T(8,128)S(1)} async-done(((f32[32,72,128]{2,1,0:T(8,128)}), f32[32,72,128]{2,1,0:T(8,128)S(1)}, u32[]{:S(2)}, u32[]{:S(2)}) %all-to-all-start) | async-done | bytes 1179680 | tf_op jit(solution)/shard_map/all_to_all | solution.py:297
  30.3 4.6 %all-to-all-start.1 = ((f32[32,72,128]{2,1,0:T(8,128)}), f32[32,72,128]{2,1,0:T(8,128)}, u32[]{:S(2)}, u32[]{:S(2)}) async-start(f32[32,72,128]{2,1,0:T(8,128)} %alpha_slots.1), calls=%async_computation.1 | async-start | bytes 2359296 | tf_op jit(solution)/shard_map/all_to_all | solution.py:301
  35.0 0.0 copy-start.6
  35.0 0.9 %slice.7 = f32[32,48,128]{2,1,0:T(8,128)} slice(f32[32,72,128]{2,1,0:T(8,128)S(1)} %all-to-all-done.own_ref), slice={[0:32], [0:48], [0:128]} | slice | bytes 1572864 | tf_op jit(solution)/shard_map/slice | solution.py:300
  35.9 1.6 %collective-permute-start.1 = (f32[32,48,128]{2,1,0:T(8,128)}, f32[32,48,128]{2,1,0:T(8,128)S(1)}, u32[]{:S(2)}, u32[]{:S(2)}) collective-permute-start(f32[32,48,128]{2,1,0:T(8,128)} %slice.7), channel_id=1, source_target_pairs={{0,32},{32,0},{64,96},{96,64},{128,160},{160,128},{192,224},{224,1... | collective-permute-start | bytes 2359304 | tf_op jit(solution)/shard_map/ppermute | solution.py:300
  37.6 0.8 %slice.6 = f32[32,24,128]{2,1,0:T(8,128)} slice(f32[32,72,128]{2,1,0:T(8,128)S(1)} %all-to-all-done.own_ref), slice={[0:32], [48:72], [0:128]} | slice | bytes 786432 | tf_op jit(solution)/shard_map/slice | solution.py:313
  38.3 3.6 %own_split.1 = (bf16[96,32,256]{2,1,0:T(8,128)(2,1)}, bf16[96,16,256]{2,1,0:T(8,128)(2,1)}) custom-call(f32[32,72,128]{2,1,0:T(8,128)S(1)} %all-to-all-done.own_ref), custom_call_target="tpu_custom_call" | custom-call | tf_op jit(solution)/shard_map/own_split/pallas_call | solution.py:303
  41.9 0.3 collective-permute-start
  42.2 0.0 copy-done.6
  42.2 2.2 %reshape.7 = f32[64,64,64]{2,1,0:T(8,128)} reshape(f32[64,4096]{1,0:T(8,128)S(1)} %copy-done.6) | data formatting | bytes 2097152 | tf_op jit(solution)/shard_map/reshape | solution.py:268
  44.4 2.2 %reduce-precision_convert_fusion = (bf16[64,64,64]{2,1,0:T(8,128)(2,1)S(1)}, bf16[64,64,64]{2,1,0:T(8,128)(2,1)S(1)}) fusion(f32[64,64,64]{2,1,0:T(8,128)} %reshape.7), kind=kLoop, calls=%fused_computation.1 | loop fusion | flops 1048576 | bytes 2097152 | tf_op jit(solution)/shard_map/convert
  46.5 0.0 copy-start.1
  46.5 0.0 copy-start.3
  46.6 0.0 copy-start.4
  46.6 0.6 pad_maximum_fusion.1.table_ref
  47.2 8.0 %collective-permute-done.1.partner_ref = f32[32,48,128]{2,1,0:T(8,128)S(1)} collective-permute-done((f32[32,48,128]{2,1,0:T(8,128)}, f32[32,48,128]{2,1,0:T(8,128)S(1)}, u32[]{:S(2)}, u32[]{:S(2)}) %collective-permute-start.1) | collective-permute-done | bytes 786464 | tf_op jit(solution)/shard_map/ppermute | solution.py:300
  55.2 0.0 copy-done.1
  55.2 0.0 copy-done.3
  55.2 0.0 copy-done.4
  55.2 0.0 copy-start.2
  55.2 5.8 %beta_first.1.first_hbm = f32[32,6144]{1,0:T(8,128)S(1)} custom-call(s32[12,96]{1,0:T(8,128)S(1)} %bitcast.3, s32[12,96]{1,0:T(8,128)S(1)} %bitcast.5, bf16[96,32,256]{2,1,0:T(8,128)(2,1)S(1)} %copy-done.1, f32[32,48,128]{2,1,0:T(8,128)S(1)} %collective-permute-done.1.partner_ref, bf16[64,64,128]{2,1,0:T(8,128)(2,1)S(1)} %pad_maximum_fusion.1.table_ref), custom_call_target="tpu_custom_call" | custom-call | tf_op jit(solution)/shard_map/beta_first/pallas_call | solution.py:318
  60.9 0.0 copy-start
  61.0 0.9 %copy-done = f32[32,6144]{1,0:T(8,128)} copy-done((f32[32,6144]{1,0:T(8,128)}, f32[32,6144]{1,0:T(8,128)S(1)}, u32[]{:S(2)}) %copy-start) | copy-done | bytes 786456
  61.9 1.7 %collective-permute-done.partner_ref = f32[32,24,128]{2,1,0:T(8,128)S(1)} collective-permute-done((f32[32,24,128]{2,1,0:T(8,128)}, f32[32,24,128]{2,1,0:T(8,128)S(1)}, u32[]{:S(2)}, u32[]{:S(2)}) %collective-permute-start) | collective-permute-done | bytes 393248 | tf_op jit(solution)/shard_map/ppermute | solution.py:316
  63.6 0.0 all-to-all-done.1.alpha_hbm
  63.6 0.0 copy-done.2
  63.6 7.4 %beta_last.1 = f32[48,6144]{1,0:T(8,128)} custom-call(s32[12,96]{1,0:T(8,128)} %bitcast.2, s32[12,96]{1,0:T(8,128)} %bitcast.4, bf16[96,16,256]{2,1,0:T(8,128)(2,1)S(1)} %copy-done.2, f32[32,24,128]{2,1,0:T(8,128)S(1)} %collective-permute-done.partner_ref, bf16[64,64,128]{2,1,0:T(8,128)(2,1)S(1)} %pad_maximum_fusion.1.table_ref, f32[32,6144]{1,0:T(8,128)} %copy-done, ...), custom_call_target="tpu_custom_call" | custom-call | tf_op jit(solution)/shard_map/beta_last/pallas_call | solution.py:330
Async XLA Ops:
  0.0 11.8 %copy-start.5 = (f32[64,4096]{1,0:T(8,128)S(1)}, f32[64,4096]{1,0:T(8,128)}, u32[]{:S(2)}) copy-start(f32[64,4096]{1,0:T(8,128)} %param.9) | copy-start | bytes 3145732
  3.2 27.1 %all-to-all-start = ((f32[32,72,128]{2,1,0:T(8,128)}), f32[32,72,128]{2,1,0:T(8,128)S(1)}, u32[]{:S(2)}, u32[]{:S(2)}) async-start(f32[32,72,128]{2,1,0:T(8,128)} %coeff_slots.1), calls=%async_computation | async-start | bytes 2359296 | tf_op jit(solution)/shard_map/all_to_all | solution.py:297
  30.3 33.3 %all-to-all-start.1 = ((f32[32,72,128]{2,1,0:T(8,128)}), f32[32,72,128]{2,1,0:T(8,128)}, u32[]{:S(2)}, u32[]{:S(2)}) async-start(f32[32,72,128]{2,1,0:T(8,128)} %alpha_slots.1), calls=%async_computation.1 | async-start | bytes 2359296 | tf_op jit(solution)/shard_map/all_to_all | solution.py:301
  35.0 7.2 %copy-start.6 = (f32[64,4096]{1,0:T(8,128)S(1)}, f32[64,4096]{1,0:T(8,128)}, u32[]{:S(2)}) copy-start(f32[64,4096]{1,0:T(8,128)} %param.12) | copy-start | bytes 3145732
  35.9 19.2 %collective-permute-start.1 = (f32[32,48,128]{2,1,0:T(8,128)}, f32[32,48,128]{2,1,0:T(8,128)S(1)}, u32[]{:S(2)}, u32[]{:S(2)}) collective-permute-start(f32[32,48,128]{2,1,0:T(8,128)} %slice.7), channel_id=1, source_target_pairs={{0,32},{32,0},{64,96},{96,64},{128,160},{160,128},{192,224},{224,1... | collective-permute-start | bytes 2359304 | tf_op jit(solution)/shard_map/ppermute | solution.py:300
  41.9 21.7 %collective-permute-start = (f32[32,24,128]{2,1,0:T(8,128)}, f32[32,24,128]{2,1,0:T(8,128)S(1)}, u32[]{:S(2)}, u32[]{:S(2)}) collective-permute-start(f32[32,24,128]{2,1,0:T(8,128)} %slice.6), channel_id=1, source_target_pairs={{0,32},{32,0},{64,96},{96,64},{128,160},{160,128},{192,224},{224,1... | collective-permute-start | bytes 1179656 | tf_op jit(solution)/shard_map/ppermute | solution.py:316
  46.5 8.6 %copy-start.1 = (bf16[96,32,256]{2,1,0:T(8,128)(2,1)S(1)}, bf16[96,32,256]{2,1,0:T(8,128)(2,1)}, u32[]{:S(2)}) copy-start(bf16[96,32,256]{2,1,0:T(8,128)(2,1)} %get-tuple-element.25.own_hbm) | copy-start | bytes 4718596
  46.5 8.6 %copy-start.3 = (s32[96,12]{0,1:T(8,128)S(1)}, s32[96,12]{0,1:T(8,128)}, u32[]{:S(2)}) copy-start(s32[96,12]{0,1:T(8,128)} %param.13) | copy-start | bytes 13828
  46.6 8.6 %copy-start.4 = (s32[96,12]{0,1:T(8,128)S(1)}, s32[96,12]{0,1:T(8,128)}, u32[]{:S(2)}) copy-start(s32[96,12]{0,1:T(8,128)} %param.14) | copy-start | bytes 13828
  55.2 8.4 %copy-start.2 = (bf16[96,16,256]{2,1,0:T(8,128)(2,1)S(1)}, bf16[96,16,256]{2,1,0:T(8,128)(2,1)}, u32[]{:S(2)}) copy-start(bf16[96,16,256]{2,1,0:T(8,128)(2,1)} %get-tuple-element.22.own_ref) | copy-start | bytes 2359300
  60.9 0.9 %copy-start = (f32[32,6144]{1,0:T(8,128)}, f32[32,6144]{1,0:T(8,128)S(1)}, u32[]{:S(2)}) copy-start(f32[32,6144]{1,0:T(8,128)S(1)} %beta_first.1.first_hbm) | copy-start | bytes 2359300
